TPU v7x, 32 devices: a whole 2x2x4 slice. The times are simulated.
32 devices in a mesh: section: 2 (over core), seq: 4 (over y, x), head: 4 (over z).
Axes of the slice: x: 2, y: 2, z: 4, core: 2. Of those that a mesh axis runs over, the one named last changes fastest.
Arguments:
- incoming: bfloat16 [2, 4, 512, 1536], P('section', None, 'seq'), may hold values from -6 to 6
- segment_ids: int32 [4, 512], replicated, may hold values from 0 to 5, as said below
- positions: int32 [4, 512], P(None, 'seq'), may hold values from 0 to 6142, as said below
- conv_gains: float32 [2, 1536], replicated, may hold values from 0.5 to 1.5
- conv_in: bfloat16 [1536, 3, 1536], P(None, None, 'head'), may hold values from -0.15625 to 0.15625
- conv_kernel: float32 [3, 1536], P(None, 'head'), may hold values from -3 to 3
- conv_out: bfloat16 [1536, 1536], P('head'), may hold values from -0.15625 to 0.15625
- conv_gate_up: bfloat16 [1536, 2, 6912], P(None, None, 'head'), may hold values from -0.15625 to 0.15625
- conv_down: bfloat16 [6912, 1536], P('head'), may hold values from -0.078125 to 0.078125
- attn_gains: float32 [2, 1536], replicated, may hold values from 0.5 to 1.5
- w_query: bfloat16 [1536, 1536], P(None, 'head'), may hold values from -0.15625 to 0.15625
- w_keyval: bfloat16 [1536, 2, 512], P(None, None, 'head'), may hold values from -0.15625 to 0.15625
- qk_gains: float32 [2, 64], replicated, may hold values from 0.5 to 1.5
- attn_out: bfloat16 [1536, 1536], P('head'), may hold values from -1.25 to 1.25
- attn_gate_up: bfloat16 [1536, 2, 6912], P(None, None, 'head'), may hold values from -0.15625 to 0.15625
- attn_down: bfloat16 [6912, 1536], P('head'), may hold values from -0.078125 to 0.078125
Outputs:
- section_edges: bfloat16 [2, 4, 512, 1536], P('section', None, 'seq')
- grad_conv_gains: float32 [2, 1536], P(None, ('section', 'seq'))
- grad_conv_in: float32 [1536, 3, 1536], P(('section', 'seq'), None, 'head')
- grad_conv_kernel: float32 [3, 1536], P(None, 'head')
- grad_conv_out: float32 [1536, 1536], P('head', ('section', 'seq'))
- grad_conv_gate_up: float32 [1536, 2, 6912], P(('section', 'seq'), None, 'head')
- grad_conv_down: float32 [6912, 1536], P('head', ('section', 'seq'))
- grad_attn_gains: float32 [2, 1536], P(None, ('section', 'seq'))
- grad_query: float32 [1536, 1536], P(('section', 'seq'), 'head')
- grad_keyval: float32 [1536, 2, 512], P(('section', 'seq'), None, 'head')
- grad_qk_gains: float32 [2, 64], replicated
- grad_attn_out: float32 [1536, 1536], P('head', ('section', 'seq'))
- grad_attn_gate_up: float32 [1536, 2, 6912], P(('section', 'seq'), None, 'head')
- grad_attn_down: float32 [6912, 1536], P('head', ('section', 'seq'))
Inputs may be any that keep to these rules, and one draw needn't show every extreme that they name: `segment_ids`: 0 at the first token; along the sequence (micro-batches in order) each token's number equals the previous one or exceeds it by one; six documents. Within a document the positions rise by one from token to token; a document's first position is below 6144.
All inputs are finite; a program needn't handle non-finite values.
Results may differ from a plain program's by a relative error of at most 0.04.
Values may be sent and summed in bfloat16 or wider, within the bound.
A program may use at most 320 MiB of HBM per device.

v0:
```python
import jax
import jax.numpy as jnp
from jax import lax
from jax.sharding import PartitionSpec as P

EPS = 1e-05
THETA = 1000000.0
FLOAT = jnp.float32
HALF = jnp.bfloat16


def passed_along(block, axis, distance):
    devices = range(lax.axis_size(axis))
    route = [((i - distance) % len(devices), i) for i in devices]
    return lax.ppermute(block, axis, route)


def shifted(array, axis, by):
    count = lax.axis_size(axis)
    pairs = [(i, i + by) for i in range(count) if 0 <= i + by < count]
    return lax.ppermute(array, axis, pairs)


def product(former, latter):
    return jnp.dot(former, latter, preferred_element_type=FLOAT)


def outer_sum(former, latter):
    return lax.dot_general(former, latter, (((0,), (0,)), ((), ())), preferred_element_type=FLOAT)


def back_product(former, latter):
    return lax.dot_general(former, latter, (((1,), (1,)), ((), ())), preferred_element_type=FLOAT)


def norm_apply(values, gain):
    return values * lax.rsqrt(jnp.mean(values * values, -1, keepdims=True) + EPS) * gain


def rotate(values, cosine, sine_table):
    half_width = values.shape[-1] // 2
    turned = jnp.concatenate([-values[..., half_width:], values[..., :half_width]], -1)
    return values * cosine + turned * sine_table


def swiglu(joined):
    half_width = joined.shape[1] // 2
    return jax.nn.silu(joined[:, :half_width]) * joined[:, half_width:]


def head_total(partial_value):
    return lax.psum(partial_value.astype(jnp.bfloat16), "head").astype(jnp.float32)


def input_total(partial_value):
    return lax.psum(partial_value.astype(jnp.bfloat16), "head").astype(jnp.float32)


def ffn_forward(hidden, gain, gate_up, down_proj):
    normed = norm_apply(hidden, gain).astype(HALF)
    joined = product(normed, gate_up.reshape(gate_up.shape[0], -1))
    active = swiglu(joined).astype(HALF)
    return (hidden + head_total(product(active, down_proj)), (normed, joined, active))


def ffn_backward(grad_result, hidden, gain, gate_up, down_proj, kept_values):
    normed, joined, active = kept_values
    grad_low = grad_result.astype(HALF)
    grad_down = outer_sum(active, grad_low)
    grad_active = back_product(grad_low, down_proj)
    grad_joined = jax.vjp(swiglu, joined)[1](grad_active)[0].astype(HALF)
    flat_gate_up = gate_up.reshape(gate_up.shape[0], -1)
    grad_gate_up = outer_sum(normed, grad_joined).reshape(gate_up.shape)
    grad_normed = input_total(back_product(grad_joined, flat_gate_up))
    grad_hidden, grad_gain = jax.vjp(norm_apply, hidden, gain)[1](grad_normed)
    return (grad_result + grad_hidden, grad_gain, grad_gate_up, grad_down)


def query_key(query_raw, key_raw, gain_pair, cosine, sine_table):
    count_rows = key_raw.shape[0]
    queries = query_raw.reshape(count_rows, key_raw.shape[1], -1, key_raw.shape[2])
    queries = rotate(
        norm_apply(queries, gain_pair[0]), cosine[:, None, None], sine_table[:, None, None]
    )
    key_rows = rotate(norm_apply(key_raw, gain_pair[1]), cosine[:, None], sine_table[:, None])
    return (queries, key_rows)


def per_device(
    incoming,
    segment_ids,
    positions,
    conv_gains,
    conv_in,
    conv_kernel,
    conv_out,
    conv_gate_up,
    conv_down,
    attn_gains,
    w_query,
    w_keyval,
    qk_gains,
    attn_out,
    attn_gate_up,
    attn_down,
):
    section_index = lax.axis_index("section")
    seq_index = lax.axis_index("seq")
    first_section = section_index == 0
    second_section = section_index == 1
    micro_count, row_count, model_width = (incoming.shape[1], incoming.shape[2], incoming.shape[3])
    tokens = micro_count * row_count
    length = segment_ids.shape[0] * segment_ids.shape[1]
    block_tok = length // micro_count
    head_width = qk_gains.shape[1]
    kv_local = w_keyval.shape[2] // head_width
    group_size = w_query.shape[1] // (kv_local * head_width)
    score_scale = head_width ** (-0.5)
    block_len = min(256, tokens)
    local_order = (
        jnp.arange(micro_count, dtype=jnp.int32)[:, None] * block_tok
        + seq_index * row_count
        + jnp.arange(row_count, dtype=jnp.int32)[None, :]
    ).reshape(tokens)
    segments = segment_ids.reshape(length)
    local_segments = segments[local_order]
    padded = jnp.concatenate([jnp.full((2,), -1, jnp.int32), segments])
    same_one = local_segments == padded[local_order + 1]
    same_two = local_segments == padded[local_order]
    key_order = jnp.arange(length, dtype=jnp.int32)
    angle_rates = THETA ** (-jnp.arange(0, head_width, 2).astype(FLOAT) / head_width)
    angles = positions.reshape(tokens).astype(FLOAT)[:, None] * angle_rates[None, :]
    angles = jnp.concatenate([angles, angles], -1)
    cosine = jnp.cos(angles)
    sine_table = jnp.sin(angles)
    own_feed = incoming[0].reshape(tokens, model_width).astype(FLOAT)

    def conv_local(gated, gate_c, earlier, kernel):
        channels = gated.shape[1]
        extended = jnp.concatenate([earlier, gated.reshape(micro_count, row_count, channels)], 1)
        back_one = extended[:, 1 : row_count + 1].reshape(tokens, channels)
        back_two = extended[:, :row_count].reshape(tokens, channels)
        mixed = (
            kernel[2] * gated
            + kernel[1] * jnp.where(same_one[:, None], back_one, 0.0)
            + kernel[0] * jnp.where(same_two[:, None], back_two, 0.0)
        )
        return gate_c * mixed

    def block_mask(segment_block, order_block):
        segment_rows = jnp.repeat(segment_block, group_size)
        order_rows = jnp.repeat(order_block, group_size)
        return (segment_rows[:, None] == segments[None, :]) & (
            key_order[None, :] <= order_rows[:, None]
        )

    def scores_of(query_rows, key_rows, allowed):
        return jnp.where(allowed, back_product(query_rows, key_rows) * score_scale, -1e30)

    def attend(block_in, all_pairs):
        query_block, segment_block, order_block = block_in
        allowed = block_mask(segment_block, order_block)
        outputs, summits, totals = ([], [], [])
        for kv_head in range(kv_local):
            scores = scores_of(
                query_block[:, kv_head].reshape(-1, head_width), all_pairs[:, 0, kv_head], allowed
            )
            summit = jnp.max(scores, -1, keepdims=True)
            raised = jnp.exp(scores - summit)
            row_total = jnp.sum(raised, -1, keepdims=True)
            weights = (raised / row_total).astype(HALF)
            outputs.append(
                product(weights, all_pairs[:, 1, kv_head]).reshape(-1, group_size, head_width)
            )
            summits.append(summit)
            totals.append(row_total)
        return (jnp.stack(outputs, 1), jnp.stack(summits), jnp.stack(totals))

    def attention_backward(entry_rows, grad_result, kept_values):
        (
            normed,
            query_raw,
            pair_raw,
            query_low,
            all_pairs,
            summits,
            totals,
            attended,
            hidden,
            ffn_kept,
        ) = kept_values
        grad_hidden, grad_gain_ffn, grad_gate_up, grad_down = ffn_backward(
            grad_result, hidden, attn_gains[1], attn_gate_up, attn_down, ffn_kept
        )
        grad_low = grad_hidden.astype(HALF)
        grad_out_w = outer_sum(attended, grad_low)
        grad_attended = back_product(grad_low, attn_out).astype(HALF)

        def attend_back(running, block_in):
            query_block, segment_block, order_block, summit_block, total_block, grad_block = (
                block_in
            )
            allowed = block_mask(segment_block, order_block)
            grad_queries = []
            updates = []
            for kv_head in range(kv_local):
                query_rows = query_block[:, kv_head].reshape(-1, head_width)
                grad_rows = grad_block[:, kv_head].reshape(-1, head_width)
                scores = scores_of(query_rows, all_pairs[:, 0, kv_head], allowed)
                probability = jnp.exp(scores - summit_block[kv_head]) / total_block[kv_head]
                grad_probs = back_product(grad_rows, all_pairs[:, 1, kv_head])
                inner_sum = jnp.sum(grad_probs * probability, -1, keepdims=True)
                grad_scores = (probability * (grad_probs - inner_sum)).astype(HALF)
                grad_queries.append(
                    (product(grad_scores, all_pairs[:, 0, kv_head]) * score_scale).reshape(
                        -1, group_size, head_width
                    )
                )
                updates.append(
                    jnp.stack(
                        [
                            outer_sum(grad_scores, query_rows) * score_scale,
                            outer_sum(probability.astype(HALF), grad_rows),
                        ],
                        1,
                    )
                )
            return (running + jnp.stack(updates, 2), jnp.stack(grad_queries, 1))

        blocks_in = (
            query_low.reshape(-1, block_len, kv_local, group_size, head_width),
            local_segments.reshape(-1, block_len),
            local_order.reshape(-1, block_len),
            summits,
            totals,
            grad_attended.reshape(-1, block_len, kv_local, group_size, head_width),
        )
        grad_pairs_all, grad_queries = lax.scan(
            attend_back, jnp.zeros((length, 2, kv_local, head_width), FLOAT), blocks_in
        )
        grad_mine = (
            lax.psum_scatter(
                grad_pairs_all.reshape(micro_count, block_tok, -1).astype(jnp.bfloat16),
                "seq",
                scatter_dimension=1,
                tiled=True,
            )
            .astype(jnp.float32)
            .reshape(tokens, 2, kv_local, head_width)
        )

        def rotary_part(query_part, key_part, gain_pair):
            return query_key(query_part, key_part, gain_pair, cosine, sine_table)

        pull_back = jax.vjp(rotary_part, query_raw, pair_raw[:, 0], qk_gains)[1]
        grad_query_raw, grad_key_raw, grad_qk = pull_back(
            (grad_queries.reshape(tokens, kv_local, group_size, head_width), grad_mine[:, 0])
        )
        grad_query_low = grad_query_raw.astype(HALF)
        grad_pair_low = (
            jnp.stack([grad_key_raw, grad_mine[:, 1]], 1).astype(HALF).reshape(tokens, -1)
        )
        grad_query_w = outer_sum(normed, grad_query_low)
        grad_keyval_w = outer_sum(normed, grad_pair_low).reshape(w_keyval.shape)
        partial_value = back_product(grad_query_low, w_query) + back_product(
            grad_pair_low, w_keyval.reshape(model_width, -1)
        )
        grad_normed, grad_qk = (
            lax.psum(partial_value.astype(jnp.bfloat16), "head").astype(jnp.float32),
            lax.psum(grad_qk.astype(jnp.bfloat16), "head").astype(jnp.float32),
        )
        grad_entry, grad_gain_mix = jax.vjp(norm_apply, entry_rows, attn_gains[0])[1](grad_normed)
        gain_grads = jnp.stack([grad_gain_mix, grad_gain_ffn])
        return (
            grad_hidden + grad_entry,
            (gain_grads, grad_query_w, grad_keyval_w, grad_out_w, grad_gate_up, grad_down),
            grad_qk,
        )

    def settle_attn(grads):
        return tuple((jnp.where(second_section, member, 0.0) for member in grads))

    normed = norm_apply(own_feed, conv_gains[0]).astype(HALF)
    projected = product(normed, conv_in.reshape(model_width, -1)).reshape(tokens, 3, -1)
    gated = projected[:, 0] * projected[:, 2]
    tail_rows = gated.reshape(micro_count, row_count, -1)[:, row_count - 2 :]
    arrived = passed_along(tail_rows, "seq", 1)
    earlier = jnp.where(
        seq_index == 0, jnp.concatenate([jnp.zeros_like(arrived[:1]), arrived[:-1]], 0), arrived
    )
    mixed = conv_local(gated, projected[:, 1], earlier, conv_kernel).astype(HALF)
    hidden = own_feed + head_total(product(mixed, conv_out))
    result, ffn_kept = ffn_forward(hidden, conv_gains[1], conv_gate_up, conv_down)
    handed = jnp.where(first_section, result, 0.0).astype(HALF)
    arrived = shifted(handed, "section", 1).astype(FLOAT)
    attention_normed = norm_apply(arrived, attn_gains[0]).astype(HALF)
    query_raw = product(attention_normed, w_query)
    pair_raw = product(attention_normed, w_keyval.reshape(model_width, -1)).reshape(
        tokens, 2, kv_local, head_width
    )
    queries, key_rows = query_key(query_raw, pair_raw[:, 0], qk_gains, cosine, sine_table)
    query_low = queries.astype(HALF)
    mine = jnp.stack([key_rows, pair_raw[:, 1]], 1).astype(HALF).reshape(micro_count, row_count, -1)
    all_pairs = lax.all_gather(mine, "seq", axis=1, tiled=True).reshape(
        length, 2, kv_local, head_width
    )
    blocks_in = (
        query_low.reshape(-1, block_len, kv_local, group_size, head_width),
        local_segments.reshape(-1, block_len),
        local_order.reshape(-1, block_len),
    )
    outputs, summits, totals = lax.map(lambda block_in: attend(block_in, all_pairs), blocks_in)
    attended = outputs.reshape(tokens, -1).astype(HALF)
    attention_hidden = arrived + head_total(product(attended, attn_out))
    result, attention_ffn_kept = ffn_forward(
        attention_hidden, attn_gains[1], attn_gate_up, attn_down
    )
    attn_kept = (
        attention_normed,
        query_raw,
        pair_raw,
        query_low,
        all_pairs,
        summits,
        totals,
        attended,
        attention_hidden,
        attention_ffn_kept,
    )
    grad_entry, attn_raw, grad_qk = attention_backward(arrived, own_feed, attn_kept)
    produced = result.astype(HALF)
    attn_grads = settle_attn(attn_raw)
    grad_qk = jnp.where(second_section, grad_qk, 0.0)
    grad_arrived = jnp.where(second_section, grad_entry, 0.0).astype(HALF)
    grad_handed = shifted(grad_arrived, "section", -1).astype(FLOAT)
    normed, projected, gated, earlier, mixed, hidden, ffn_kept = (
        normed,
        projected,
        gated,
        earlier,
        mixed,
        hidden,
        ffn_kept,
    )
    grad_hidden, grad_gain_ffn, grad_gate_up, grad_down = ffn_backward(
        grad_handed, hidden, conv_gains[1], conv_gate_up, conv_down, ffn_kept
    )
    grad_low = grad_hidden.astype(HALF)
    grad_mix_w = outer_sum(mixed, grad_low)
    grad_mixed = back_product(grad_low, conv_out)
    pull_back = jax.vjp(conv_local, gated, projected[:, 1], earlier, conv_kernel)[1]
    grad_gated, grad_gate_c, grad_earlier, grad_kernel = pull_back(grad_mixed)
    outgoing = jnp.where(
        seq_index == 0,
        jnp.concatenate([grad_earlier[1:], jnp.zeros_like(grad_earlier[:1])], 0),
        grad_earlier,
    )
    returned = passed_along(outgoing, "seq", -1)
    grad_gated = grad_gated + jnp.pad(returned, ((0, 0), (row_count - 2, 0), (0, 0))).reshape(
        tokens, -1
    )
    grad_projected = (
        jnp.stack([grad_gated * projected[:, 2], grad_gate_c, grad_gated * projected[:, 0]], 1)
        .astype(HALF)
        .reshape(tokens, -1)
    )
    grad_in = outer_sum(normed, grad_projected).reshape(conv_in.shape)
    grad_normed = input_total(back_product(grad_projected, conv_in.reshape(model_width, -1)))
    grad_start, grad_gain_mix = jax.vjp(norm_apply, own_feed, conv_gains[0])[1](grad_normed)
    gain_grads = jnp.stack([grad_gain_mix, grad_gain_ffn])
    grad_start, conv_raw, grad_kernel = (
        grad_hidden + grad_start,
        (gain_grads, grad_in, grad_mix_w, grad_gate_up, grad_down),
        grad_kernel,
    )
    grad_input = grad_start.astype(HALF)
    conv_grads = tuple((jnp.where(first_section, member, 0.0) for member in conv_raw))
    grad_kernel = jnp.where(first_section, grad_kernel, 0.0)
    section_edges = jnp.where(first_section, grad_input, produced).reshape(
        1, micro_count, row_count, model_width
    )
    grad_kernel, grad_qk = lax.psum((grad_kernel, grad_qk), ("section", "seq"))
    reduced = (
        lax.psum_scatter(
            conv_grads[0].astype(jnp.bfloat16), ("section", "seq"), scatter_dimension=1, tiled=True
        ).astype(jnp.float32),
        lax.psum_scatter(
            conv_grads[1].astype(jnp.bfloat16), ("section", "seq"), scatter_dimension=0, tiled=True
        ).astype(jnp.float32),
        lax.psum_scatter(
            conv_grads[2].astype(jnp.bfloat16), ("section", "seq"), scatter_dimension=1, tiled=True
        ).astype(jnp.float32),
        lax.psum_scatter(
            conv_grads[3].astype(jnp.bfloat16), ("section", "seq"), scatter_dimension=0, tiled=True
        ).astype(jnp.float32),
        lax.psum_scatter(
            conv_grads[4].astype(jnp.bfloat16), ("section", "seq"), scatter_dimension=1, tiled=True
        ).astype(jnp.float32),
        lax.psum_scatter(
            attn_grads[0].astype(jnp.bfloat16), ("section", "seq"), scatter_dimension=1, tiled=True
        ).astype(jnp.float32),
        lax.psum_scatter(
            attn_grads[1].astype(jnp.bfloat16), ("section", "seq"), scatter_dimension=0, tiled=True
        ).astype(jnp.float32),
        lax.psum_scatter(
            attn_grads[2].astype(jnp.bfloat16), ("section", "seq"), scatter_dimension=0, tiled=True
        ).astype(jnp.float32),
        lax.psum_scatter(
            attn_grads[3].astype(jnp.bfloat16), ("section", "seq"), scatter_dimension=1, tiled=True
        ).astype(jnp.float32),
        lax.psum_scatter(
            attn_grads[4].astype(jnp.bfloat16), ("section", "seq"), scatter_dimension=0, tiled=True
        ).astype(jnp.float32),
        lax.psum_scatter(
            attn_grads[5].astype(jnp.bfloat16), ("section", "seq"), scatter_dimension=1, tiled=True
        ).astype(jnp.float32),
    )
    conv_final = tuple(reduced[:5])
    attn_final = tuple(reduced[5:])
    return (
        section_edges,
        conv_final[0],
        conv_final[1],
        grad_kernel,
        conv_final[2],
        conv_final[3],
        conv_final[4],
        attn_final[0],
        attn_final[1],
        attn_final[2],
        grad_qk,
        attn_final[3],
        attn_final[4],
        attn_final[5],
    )


def solution(mesh):
    return jax.shard_map(
        per_device,
        mesh=mesh,
        in_specs=(
            P("section", None, "seq", None),
            P(),
            P(None, "seq"),
            P(),
            P(None, None, "head"),
            P(None, "head"),
            P("head", None),
            P(None, None, "head"),
            P("head", None),
            P(),
            P(None, "head"),
            P(None, None, "head"),
            P(),
            P("head", None),
            P(None, None, "head"),
            P("head", None),
        ),
        out_specs=(
            P("section", None, "seq", None),
            P(None, ("section", "seq")),
            P(("section", "seq"), None, "head"),
            P(None, "head"),
            P("head", ("section", "seq")),
            P(("section", "seq"), None, "head"),
            P("head", ("section", "seq")),
            P(None, ("section", "seq")),
            P(("section", "seq"), "head"),
            P(("section", "seq"), None, "head"),
            P(),
            P("head", ("section", "seq")),
            P(("section", "seq"), None, "head"),
            P("head", ("section", "seq")),
        ),
        check_vma=False,
    )
```

profile of v0, /device:TPU:0, one launch (start us, length us, event | category | flops | bytes accessed | tf_op | source)
XLA Modules:
  0.0 1773.5 jit_solution(11176044667307961510)
XLA Ops:
  40.6 70.5 %all-reduce.33.cloned.1.call-done = bf16[512,1536]{1,0:T(8,128)(2,1)} async-done(((bf16[512,1536]{1,0:T(8,128)(2,1)}), bf16[512,1536]{1,0:T(8,128)(2,1)}) %all-reduce.33.cloned.1.call-update) | async-done | bytes 1572880 | tf_op jit(solution)/shard_map/psum | solution.py:52
  134.6 15.8 all-gather.2.cloned.1.call-start
  155.7 47.2 %all-reduce.35.cloned.1.call-done = bf16[512,1536]{1,0:T(8,128)(2,1)} async-done(((bf16[512,1536]{1,0:T(8,128)(2,1)}), bf16[512,1536]{1,0:T(8,128)(2,1)}) %all-reduce.35.cloned.1.call-update) | async-done | bytes 1572880 | tf_op jit(solution)/shard_map/psum | solution.py:52
  223.3 24.3 %all-gather.2.cloned.1.call-done = bf16[4,512,256]{1,0,2:T(4,128)(2,1)} async-done(((bf16[4,128,256]{1,0,2:T(4,128)(2,1)}), bf16[4,512,256]{1,0,2:T(4,128)(2,1)}) %all-gather.2.cloned.1.call-update) | async-done | bytes 1048592 | tf_op jit(solution)/shard_map/all_gather | solution.py:304
  250.2 92.4 %while.28 = (s32[]{:T(128)}, bf16[2,256,2,3,64]{1,4,3,2,0:T(8,128)(2,1)}, f32[2,2,768,1]{2,3,1,0:T(1,128)S(1)}, f32[2,2,768,1]{2,3,1,0:T(1,128)S(1)}, s32[2,256]...) while((s32[]{:T(128)}, ...), condition=%wide.region_12.13_spmd.clone, body=%wide.region_7.12_spmd.clone.sunk | while | flops 840302592 | bytes 71321784 | solution.py:312
  348.3 69.2 %all-reduce.37.cloned.1.call-done = bf16[512,1536]{1,0:T(8,128)(2,1)} async-done(((bf16[512,1536]{1,0:T(8,128)(2,1)}), bf16[512,1536]{1,0:T(8,128)(2,1)}) %all-reduce.37.cloned.1.call-update) | async-done | bytes 1572880 | tf_op jit(solution)/shard_map/psum | solution.py:52
  453.4 68.3 %all-reduce.39.cloned.1.call-done = bf16[512,1536]{1,0:T(8,128)(2,1)} async-done(((bf16[512,1536]{1,0:T(8,128)(2,1)}), bf16[512,1536]{1,0:T(8,128)(2,1)}) %all-reduce.39.cloned.1.call-update) | async-done | bytes 1572880 | tf_op jit(solution)/shard_map/psum | solution.py:56
  531.1 83.4 %while.29 = (s32[]{:T(128)}, f32[2048,2,2,64]{0,3,1,2:T(8,128)}, f32[2,256,2,3,64]{1,0,4,3,2:T(2,128)}, s32[2,256]{1,0:T(2,128)S(1)}, s32[4,512]{1,0:T(4,128)S(1...) while((s32[]{:T(128)}, f32[2048,2,2,64]{0,3,1,2:T(8,128)}, ...), condition=%wide.region_20.21_spmd.clone, body=%wide.region_17.20_spmd.clone.sunk | while | flops 2056714752 | bytes 161730944 | solution.py:238
  617.2 24.9 %copy.146 = bf16[4,512,256]{0,2,1:T(8,128)(2,1)} copy(bf16[4,512,256]{1,0,2:T(4,128)(2,1)S(1)} %convert_element_type.319) | data formatting | bytes 2097152
  642.1 65.2 %reshape.696 = bf16[512,1024]{1,0:T(8,128)(2,1)} reshape(bf16[512,256,4]{2,1,0:T(8,128)(2,1)} %bitcast.456) | data formatting | bytes 2097152
  714.2 20.1 %reduce-scatter.31.cloned.1.call-done = bf16[128,1024]{1,0:T(8,128)(2,1)} async-done(((bf16[512,1024]{1,0:T(8,128)(2,1)}), bf16[128,1024]{1,0:T(8,128)(2,1)}) %reduce-scatter.31.cloned.1.call-update) | async-done | bytes 262160
  734.3 19.8 %reshape.697 = bf16[128,256,4]{2,1,0:T(8,128)(2,1)} reshape(bf16[128,1024]{1,0:T(8,128)(2,1)} %reduce-scatter.31.cloned.1.call-done) | data formatting | bytes 524288
  766.9 69.2 %all-reduce.41.cloned.1.call-done = bf16[512,1536]{1,0:T(8,128)(2,1)} async-done(((bf16[512,1536]{1,0:T(8,128)(2,1)}), bf16[512,1536]{1,0:T(8,128)(2,1)}) %all-reduce.41.cloned.1.call-update) | async-done | bytes 1572880 | tf_op jit(solution)/shard_map/psum | solution.py:269
  873.7 60.9 %all-reduce.43.cloned.1.call-done = bf16[512,1536]{1,0:T(8,128)(2,1)} async-done(((bf16[512,1536]{1,0:T(8,128)(2,1)}), bf16[512,1536]{1,0:T(8,128)(2,1)}) %all-reduce.43.cloned.1.call-update) | async-done | bytes 1572880 | tf_op jit(solution)/shard_map/psum | solution.py:56
  981.5 91.7 %all-reduce.47.cloned.1.call-done = (bf16[512,1536]{1,0:T(8,128)(2,1)}, bf16[512,1536]{1,0:T(8,128)(2,1)}) async-done(((bf16[512,1536]{1,0:T(8,128)(2,1)}, bf16[512,1536]{1,0:T(8,128)(2,1)}), (bf16[512,1536]{1,0:T(8,128)(2,1)}, bf16[512,1536]{1,0:T(8,128)(2,1)})) %all-reduce.47.cloned.1.call-update) | async-done | bytes 3145744 | tf_op jit(solution)/shard_map/psum | solution.py:52
  1118.4 27.7 %copy.135 = bf16[1536,2,1728]{2,1,0:T(2,128)(2,1)} copy(bf16[1536,2,1728]{0,2,1:T(8,128)(2,1)} %bitcast.458) | data formatting | bytes 21233664 | tf_op jit(solution)/shard_map/convert_element_type | solution.py:412
  1172.8 27.7 %copy.132 = bf16[1536,2,1728]{2,1,0:T(2,128)(2,1)} copy(bf16[1536,2,1728]{0,2,1:T(8,128)(2,1)} %bitcast.459) | data formatting | bytes 21233664 | tf_op jit(solution)/shard_map/convert_element_type | solution.py:394
  1230.1 60.1 %reduce-scatter.29.cloned.1.call-done = bf16[1728,192]{0,1:T(8,128)(2,1)} async-done(((bf16[1728,1536]{0,1:T(8,128)(2,1)}), bf16[1728,192]{0,1:T(8,128)(2,1)}) %reduce-scatter.29.cloned.1.call-update) | async-done | bytes 663568 | tf_op jit(solution)/shard_map/reduce_scatter | solution.py:414
  1292.5 15.3 all-reduce.21
  1307.8 22.2 %reduce-scatter.19.cloned.1.call-done = bf16[384,192]{0,1:T(8,128)(2,1)} async-done(((bf16[384,1536]{0,1:T(8,128)(2,1)}), bf16[384,192]{0,1:T(8,128)(2,1)}) %reduce-scatter.19.cloned.1.call-update) | async-done | bytes 147472 | tf_op jit(solution)/shard_map/reduce_scatter | solution.py:390
  1338.4 29.3 %reduce-scatter.33.cloned.1.call-done = bf16[192,2]{1,0:T(8,128)(2,1)} async-done(((bf16[1536,2]{1,0:T(8,128)(2,1)}), bf16[192,2]{1,0:T(8,128)(2,1)}) %reduce-scatter.33.cloned.1.call-update) | async-done | bytes 784
  1369.2 50.4 %reduce-scatter.17.cloned.1.call-done = bf16[192,3,384]{2,0,1:T(8,128)(2,1)} async-done(((bf16[1536,3,384]{2,0,1:T(8,128)(2,1)}), bf16[192,3,384]{2,0,1:T(8,128)(2,1)}) %reduce-scatter.17.cloned.1.call-update) | async-done | bytes 442384 | tf_op jit(solution)/shard_map/reduce_scatter | solution.py:387
  1421.5 59.6 %reduce-scatter.21.cloned.1.call-done = bf16[1728,192]{0,1:T(8,128)(2,1)} async-done(((bf16[1728,1536]{0,1:T(8,128)(2,1)}), bf16[1728,192]{0,1:T(8,128)(2,1)}) %reduce-scatter.21.cloned.1.call-update) | async-done | bytes 663568 | tf_op jit(solution)/shard_map/reduce_scatter | solution.py:396
  1483.4 275.7 %all-reduce.45.cloned.1.call-done = (bf16[1536,2,1728]{2,1,0:T(2,128)(2,1)}, bf16[1536,2,1728]{2,1,0:T(2,128)(2,1)}) async-done(((bf16[1536,2,1728]{2,1,0:T(2,128)(2,1)}, bf16[1536,2,1728]{2,1,0:T(2,128)(2,1)}), (bf16[1536,2,1728]{2,1,0:T(2,128)(2,1)}, bf16[1536,2,1728]{2,1,0:T(2,128)(2,1)})) %all-reduce.45.cloned.1.call-update) | async-done | bytes 21233680
  (654 shorter events, 539.8 us)
Async XLA Ops:
  7.2 103.9 %all-reduce.33.cloned.1.call-start = ((), (), s32[]{:S(2)}) async-start(), calls=%async_computation.10 | async-start | bytes 3145728 | tf_op jit(solution)/shard_map/psum | solution.py:52
  21.5 12.8 collective-permute-start
  40.6 162.3 %all-reduce.35.cloned.1.call-start = ((), (), s32[]{:S(2)}) async-start(), calls=%async_computation.11 | async-start | bytes 3145728 | tf_op jit(solution)/shard_map/psum | solution.py:52
  134.6 113.0 %all-gather.2.cloned.1.call-start = ((), (), s32[]{:S(2)}) async-start(), calls=%async_computation.12 | async-start | bytes 1310720 | tf_op jit(solution)/shard_map/all_gather | solution.py:304
  205.6 4.4 collective-permute-start.1
  207.0 319.1 %copy-start.82 = (f32[1536]{0:T(1024)}, f32[1536]{0:T(1024)S(1)}, u32[]{:S(2)}) copy-start(f32[1536]{0:T(1024)S(1)} %get-tuple-element.338) | copy-start | bytes 18436
  212.9 204.6 %all-reduce.37.cloned.1.call-start = ((), (), s32[]{:S(2)}) async-start(), calls=%async_computation.13 | async-start | bytes 3145728 | tf_op jit(solution)/shard_map/psum | solution.py:52
  348.3 173.4 %all-reduce.39.cloned.1.call-start = ((), (), s32[]{:S(2)}) async-start(), calls=%async_computation.14 | async-start | bytes 3145728 | tf_op jit(solution)/shard_map/psum | solution.py:56
  453.4 280.9 %reduce-scatter.31.cloned.1.call-start = ((), (), s32[]{:S(2)}) async-start(), calls=%async_computation.24 | async-start | bytes 1310720
  707.4 128.8 %all-reduce.41.cloned.1.call-start = ((), (), s32[]{:S(2)}) async-start(), calls=%async_computation.15 | async-start | bytes 3145728 | tf_op jit(solution)/shard_map/psum | solution.py:269
  766.9 167.7 %all-reduce.43.cloned.1.call-start = ((), (), s32[]{:S(2)}) async-start(), calls=%async_computation.16 | async-start | bytes 3145728 | tf_op jit(solution)/shard_map/psum | solution.py:56
  842.2 5.6 collective-permute-start.2
  866.3 206.9 %all-reduce.47.cloned.1.call-start = ((), (), s32[]{:S(2)}) async-start(), calls=%async_computation.28 | async-start | bytes 6291456 | tf_op jit(solution)/shard_map/psum | solution.py:52
  942.2 3.8 collective-permute-start.3
  951.8 250.6 %reduce-scatter.23.cloned.1.call-start = ((), (), s32[]{:S(2)}) async-start(), calls=%async_computation.20 | async-start | bytes 1327104 | tf_op jit(solution)/shard_map/reduce_scatter | solution.py:402
  956.4 247.6 %reduce-scatter.27.cloned.1.call-start = ((), (), s32[]{:S(2)}) async-start(), calls=%async_computation.22 | async-start | bytes 1327104 | tf_op jit(solution)/shard_map/reduce_scatter | solution.py:408
  961.0 253.9 %reduce-scatter.25.cloned.1.call-start = ((), (), s32[]{:S(2)}) async-start(), calls=%async_computation.21 | async-start | bytes 884736 | tf_op jit(solution)/shard_map/reduce_scatter | solution.py:405
  964.2 264.4 %reduce-scatter.35.cloned.1.call-start = ((), (), s32[]{:S(2)}) async-start(), calls=%async_computation.26 | async-start | bytes 442368
  965.3 324.9 %reduce-scatter.29.cloned.1.call-start = ((), (), s32[]{:S(2)}) async-start(), calls=%async_computation.23 | async-start | bytes 6193152 | tf_op jit(solution)/shard_map/reduce_scatter | solution.py:414
  971.8 358.2 %reduce-scatter.19.cloned.1.call-start = ((), (), s32[]{:S(2)}) async-start(), calls=%async_computation.18 | async-start | bytes 1327104 | tf_op jit(solution)/shard_map/reduce_scatter | solution.py:390
  976.7 391.0 %reduce-scatter.33.cloned.1.call-start = ((), (), s32[]{:S(2)}) async-start(), calls=%async_computation.25 | async-start | bytes 442368
  1076.9 342.6 %reduce-scatter.17.cloned.1.call-start = ((), (), s32[]{:S(2)}) async-start(), calls=%async_computation.17 | async-start | bytes 3981312 | tf_op jit(solution)/shard_map/reduce_scatter | solution.py:387
  1082.8 398.4 %reduce-scatter.21.cloned.1.call-start = ((), (), s32[]{:S(2)}) async-start(), calls=%async_computation.19 | async-start | bytes 6193152 | tf_op jit(solution)/shard_map/reduce_scatter | solution.py:396
  1090.7 668.4 %all-reduce.45.cloned.1.call-start = ((), (), s32[]{:S(2)}) async-start(), calls=%async_computation.27 | async-start | bytes 44040192
  (146 other events, 1876.7 us)
Sparse Core Ops, SparseCore 0:
  40.7 70.3 all-reduce.32
  134.7 68.1 all-reduce.34
  213.0 34.4 all-gather.1
  348.4 69.1 all-reduce.36
  453.5 68.1 all-reduce.38
  707.5 26.7 reduce-scatter.30
  767.0 69.1 all-reduce.40
  866.4 68.1 all-reduce.42
  951.9 121.2 all-reduce.46
  1076.7 35.7 reduce-scatter.22
  1115.7 36.7 reduce-scatter.26
  1156.4 34.9 reduce-scatter.24
  1194.8 33.7 reduce-scatter.34
  1232.3 57.8 reduce-scatter.28
  1293.3 36.7 reduce-scatter.18
  1333.9 33.7 reduce-scatter.32
  1371.4 48.0 reduce-scatter.16
  1423.2 57.8 reduce-scatter.20
  1485.1 273.9 all-reduce.44
where the time goes:
time: 1790 us; the launch traced here: 1770 us
  waiting for transfers between devices  1040 us (58%)
  local copies, waits for them, and re-layouts  340 us (19%)
  matrix products  225 us (13%)
  other arithmetic  103 us (6%)
  starting transfers between devices  25.5 us (1%)
  blocking collectives  24.5 us (1%)
    unnamed x23, waiting for transfers between devices  337 us
    psum x4, waiting for transfers between devices, head_total(): lax.psum(partial_value.astype(jnp.bfloat16), 'head').astype(jnp.float32)  279 us
    unnamed x278, local copies, waits for them, and re-layouts  156 us
    psum x2, waiting for transfers between devices, input_total(): lax.psum(partial_value.astype(jnp.bfloat16), 'head').astype(jnp.float32)  129 us
    dot_general x17, matrix products, product(): return jnp.dot(former, latter, preferred_element_type=FLOAT)  81.6 us
    dot_general x21, matrix products, back_product(): lax.dot_general(former, latter, (((1,), (1,)), ((), ())), preferred_eleme...  76.3 us
    psum x1, waiting for transfers between devices, attention_backward(): lax.psum(partial_value.astype(jnp.bfloat16), 'head').astype(jnp.float32)  69.2 us
    dot_general x17, matrix products, outer_sum(): lax.dot_general(former, latter, (((0,), (0,)), ((), ())), preferred_eleme...  67.5 us
  transfers between devices with their start and end apart: 23, of which 18 were waited for; matrix products, arithmetic and copies ran while one was open for 12% of the time, Pallas kernels for 0%

commit v1 on v0

v1 whole, which is shorter than its diff:
```python
import functools

import jax
import jax.numpy as jnp
from jax import lax
from jax.experimental import pallas as pl
from jax.experimental.pallas import tpu as pltpu
from jax.sharding import PartitionSpec as P

EPS = 1e-05
THETA = 1000000.0
FLOAT = jnp.float32
HALF = jnp.bfloat16
MESH = pl.DeviceIdType.MESH
VMEM = pl.BlockSpec(memory_space=pltpu.VMEM)


def product(former, latter):
    return jnp.dot(former, latter, preferred_element_type=FLOAT)


def outer_sum(former, latter):
    return lax.dot_general(former, latter, (((0,), (0,)), ((), ())), preferred_element_type=FLOAT)


def back_product(former, latter):
    return lax.dot_general(former, latter, (((1,), (1,)), ((), ())), preferred_element_type=FLOAT)


def swiglu(joined):
    half_width = joined.shape[1] // 2
    return jax.nn.silu(joined[:, :half_width]) * joined[:, half_width:]


def norm_apply(values, gain):
    return values * lax.rsqrt(jnp.mean(values * values, -1, keepdims=True) + EPS) * gain


def norm_back(values, gain, grad):
    scale = lax.rsqrt(jnp.mean(values * values, -1, keepdims=True) + EPS)
    weighted = grad * gain
    inner = jnp.mean(weighted * values, -1, keepdims=True)
    grad_values = scale * weighted - values * (scale * scale * scale * inner)
    return grad_values, jnp.sum(grad * values * scale, 0, keepdims=True)


def place():
    return lax.axis_index("section"), lax.axis_index("seq"), lax.axis_index("head")


def greet(peers):
    barrier = pltpu.get_barrier_semaphore()
    for peer in peers:
        pl.semaphore_signal(barrier, inc=1, device_id=peer, device_id_type=MESH)
    pl.semaphore_wait(barrier, len(peers))


def head_peers(where, size):
    section, seq, head = where
    return [(section, seq, lax.rem(head + k, size)) for k in range(1, size)]


def remote(source, target, send, recv, peer):
    return pltpu.make_async_remote_copy(
        src_ref=source,
        dst_ref=target,
        send_sem=send,
        recv_sem=recv,
        device_id=peer,
        device_id_type=MESH,
    )


def rows_of(index, count):
    return pl.ds(pl.multiple_of(index * count, count), count)


def scatter_start(part, slots, send, recv, where, size, count):
    copies = []
    for k, peer in enumerate(head_peers(where, size)):
        copy = remote(part.at[rows_of(peer[2], count)], slots.at[k], send.at[k], recv.at[k], peer)
        copy.start()
        copies.append(copy)
    return copies


def scatter_sum(copies, part, slots, where, count):
    total = part[rows_of(where[2], count), :].astype(FLOAT)
    for copy in copies:
        copy.wait()
    for k in range(len(copies)):
        total = total + slots[k].astype(FLOAT)
    return total


def gather_start(full, send, recv, where, size, count):
    mine = full.at[rows_of(where[2], count)]
    copies = []
    for k, peer in enumerate(head_peers(where, size)):
        copy = remote(mine, mine, send.at[k], recv.at[k], peer)
        copy.start()
        copies.append(copy)
    return copies


def wait_all(copies):
    for copy in copies:
        copy.wait()


def turned(values):
    width = values.shape[-1]
    if width == 128:
        lane = lax.broadcasted_iota(jnp.int32, values.shape, 1)
        low = lax.rem(lane, 64) < 32
        return jnp.where(low, -pltpu.roll(values, 96, 1), pltpu.roll(values, 32, 1))
    parts = []
    for start in range(0, width, 64):
        parts += [-values[:, start + 32 : start + 64], values[:, start : start + 32]]
    return jnp.concatenate(parts, -1)


def head_mean(values):
    width = values.shape[-1]
    if width == 64:
        return jnp.mean(values, -1, keepdims=True)
    lane = lax.broadcasted_iota(jnp.int32, values.shape, 1)
    first = jnp.sum(jnp.where(lane < 64, values, 0.0), -1, keepdims=True)
    second = jnp.sum(jnp.where(lane < 64, 0.0, values), -1, keepdims=True)
    return jnp.where(lane < 64, first, second) * (1.0 / 64.0)


def chunks_of(width):
    return [(start, min(128, width - start)) for start in range(0, width, 128)]


def rotary(raw, gain, cosine, sine):
    width = raw.shape[-1]
    normed = raw * lax.rsqrt(head_mean(raw * raw) + EPS) * gain[:, :width]
    return normed * cosine[:, :width] + turned(normed) * sine[:, :width]


def rotary_back(raw, gain, cosine, sine, grad):
    width = raw.shape[-1]
    back = grad * cosine[:, :width] - turned(grad) * sine[:, :width]
    scale = lax.rsqrt(head_mean(raw * raw) + EPS)
    weighted = back * gain[:, :width]
    grad_raw = scale * weighted - raw * (scale * scale * scale * head_mean(weighted * raw))
    return grad_raw, jnp.sum(back * raw * scale, 0, keepdims=True)


def call(body, name, collective, outs, scratch, args, flops=0, moved=0):
    params = dict(vmem_limit_bytes=56 << 20)
    if collective is not None:
        params.update(collective_id=collective, has_side_effects=True)
    return pl.pallas_call(
        body,
        name=name,
        out_shape=[jax.ShapeDtypeStruct(shape, kind) for shape, kind in outs],
        in_specs=[VMEM] * len(args),
        out_specs=[VMEM] * len(outs),
        scratch_shapes=scratch,
        compiler_params=pltpu.CompilerParams(**params),
        cost_estimate=pl.CostEstimate(flops=flops, bytes_accessed=moved, transcendentals=0),
    )(*args)


def dma(count):
    return pltpu.SemaphoreType.DMA((count,))


def per_device(
    incoming,
    segment_ids,
    positions,
    conv_gains,
    conv_in,
    conv_kernel,
    conv_out,
    conv_gate_up,
    conv_down,
    attn_gains,
    w_query,
    w_keyval,
    qk_gains,
    attn_out,
    attn_gate_up,
    attn_down,
):
    sections = lax.axis_size("section")
    seqs = lax.axis_size("seq")
    heads = lax.axis_size("head")
    section, seq, head = place()
    micro, local_rows, width = incoming.shape[1:]
    rows = local_rows // sections
    tokens = micro * rows
    own = tokens // heads
    block_tok = segment_ids.shape[1]
    length = micro * block_tok
    slots = sections * seqs
    channels = conv_in.shape[2]
    hidden_units = conv_down.shape[0]
    head_width = qk_gains.shape[1]
    query_width = w_query.shape[1]
    pair_width = 2 * w_keyval.shape[2]
    kv_local = w_keyval.shape[2] // head_width
    group = query_width // (kv_local * head_width)
    score_scale = head_width ** (-0.5)
    half_model = width // sections

    local_order = (
        jnp.arange(micro, dtype=jnp.int32)[:, None] * block_tok
        + seq * local_rows
        + section * rows
        + jnp.arange(rows, dtype=jnp.int32)[None, :]
    ).reshape(tokens)
    segments = segment_ids.reshape(length)
    padded = jnp.concatenate([jnp.full((2,), -1, jnp.int32), segments])
    local_segments = segments[local_order]
    same = jnp.stack(
        [
            (local_segments == padded[local_order + 1]).astype(FLOAT),
            (local_segments == padded[local_order]).astype(FLOAT),
        ],
        1,
    )
    local_segments = local_segments[:, None]
    angle_rates = THETA ** (-jnp.arange(0, head_width, 2).astype(FLOAT) / head_width)
    local_positions = lax.dynamic_slice_in_dim(positions, section * rows, rows, 1).reshape(tokens)
    angles = local_positions.astype(FLOAT)[:, None] * angle_rates[None, :]
    cosine = jnp.tile(jnp.cos(angles), (1, 4))
    sine = jnp.tile(jnp.sin(angles), (1, 4))
    query_gain = jnp.tile(qk_gains[0:1], (1, 2))
    key_gain = jnp.tile(qk_gains[1:2], (1, 2))
    w_in = conv_in.transpose(1, 0, 2)
    w_pair = w_keyval.reshape(width, pair_width)
    first_up = conv_gate_up.transpose(1, 2, 0).reshape(2 * hidden_units, width)
    second_up = attn_gate_up.transpose(1, 2, 0).reshape(2 * hidden_units, width)

    def shifted_rows(ext, micro_at, back):
        return ext[micro_at, 8 - back : 8 - back + rows, :]

    def conv_forward(
        in_ref, same_ref, gain_ref, win_ref, kernel_ref, wout_ref,
        x_ref, g_ref, n1_ref, pc_ref, edge_ref, y_ref, h1_ref, n2_ref,
        other, edges, normed_edges, ext, part, zslots,
        swap_send, swap_recv, edge_send, edge_recv, zs, zr, gs, gr,
    ):
        where = place()
        s, q, h = where
        partner = (1 - s, q, h)
        following = (s, lax.rem(q + 1, seqs), h)
        preceding = (s, lax.rem(q + seqs - 1, seqs), h)
        greet([partner, following, preceding] + head_peers(where, heads))
        give = pl.multiple_of((1 - s) * rows, rows)
        swap = remote(in_ref.at[0, :, pl.ds(give, rows)], other, swap_send.at[0], swap_recv.at[0], partner)
        swap.start()
        near = remote(in_ref.at[0, :, rows - 16 : rows], edges.at[0], edge_send.at[0], edge_recv.at[0], partner)
        near.start()
        far = remote(
            in_ref.at[0, :, local_rows - 16 : local_rows], edges.at[1], edge_send.at[1], edge_recv.at[1], following
        )
        far.start()
        keep = pl.multiple_of(s * rows, rows)
        swap.wait()
        mine = in_ref[0, :, pl.ds(keep, rows), :].reshape(tokens, width)
        theirs = other[...].reshape(tokens, width)
        first = s == 0
        x = jnp.where(first, mine, theirs)
        x_ref[...] = x
        g_ref[...] = jnp.where(first, theirs, mine)
        n1_ref[...] = norm_apply(x.astype(FLOAT), gain_ref[0:1, :]).astype(HALF)
        near.wait()
        far.wait()
        for m in range(micro):
            before = edges[1, max(m - 1, 0)]
            far_edge = jnp.where(q == 0, before, edges[1, m])
            edge = jnp.where(first, far_edge, edges[0, m]).astype(FLOAT)
            normed_edges[m * 16 : (m + 1) * 16, :] = norm_apply(edge, gain_ref[0:1, :]).astype(HALF)
        for k in range(3):
            pc_ref[k] = product(n1_ref[...], win_ref[k])
        edge_b = product(normed_edges[...], win_ref[0])
        edge_u = product(normed_edges[...], win_ref[2])
        edge_gated = edge_b * edge_u
        gated = pc_ref[0] * pc_ref[2]
        for m in range(micro):
            ext[m, 0:8, :] = edge_gated[m * 16 + 8 : m * 16 + 16, :]
            edge_ref[m] = edge_gated[m * 16 + 8 : m * 16 + 16, :]
            ext[m, 8 : 8 + rows, :] = gated[m * rows : (m + 1) * rows, :]
        for m in range(micro):
            span = slice(m * rows, (m + 1) * rows)
            mixed = (
                kernel_ref[2:3, :] * gated[span]
                + kernel_ref[1:2, :] * jnp.where(same_ref[span, 0:1] > 0, shifted_rows(ext, m, 1), 0.0)
                + kernel_ref[0:1, :] * jnp.where(same_ref[span, 1:2] > 0, shifted_rows(ext, m, 2), 0.0)
            )
            y_ref[span, :] = (pc_ref[1, span, :] * mixed).astype(HALF)
        part[...] = product(y_ref[...], wout_ref[...]).astype(HALF)
        copies = scatter_start(part, zslots, zs, zr, where, heads, own)
        start = x_ref[rows_of(h, own), :].astype(FLOAT)
        hidden = start + scatter_sum(copies, part, zslots, where, own)
        h1_ref[...] = hidden
        n2_ref[rows_of(h, own), :] = norm_apply(hidden, gain_ref[1:2, :]).astype(HALF)
        wait_all(gather_start(n2_ref, gs, gr, where, heads, own))

    zscratch = [pltpu.VMEM((heads - 1, own, width), HALF)]
    zsems = [dma(heads - 1)] * 4
    x, g, n1, projected, edge_gated, mixed, h1, n2 = call(
        conv_forward,
        "conv_forward",
        0,
        [
            ((tokens, width), HALF),
            ((tokens, width), HALF),
            ((tokens, width), HALF),
            ((3, tokens, channels), FLOAT),
            ((micro, 8, channels), FLOAT),
            ((tokens, channels), HALF),
            ((own, width), FLOAT),
            ((tokens, width), HALF),
        ],
        [
            pltpu.VMEM((micro, rows, width), HALF),
            pltpu.VMEM((2, micro, 16, width), HALF),
            pltpu.VMEM((micro * 16, width), HALF),
            pltpu.VMEM((micro, 8 + rows, channels), FLOAT),
            pltpu.VMEM((tokens, width), HALF),
        ]
        + zscratch
        + [dma(1), dma(1), dma(2), dma(2)]
        + zsems,
        [incoming, same, conv_gains, w_in, conv_kernel, conv_out],
        flops=10**9,
        moved=80 << 20,
    )

    def ffn_forward(normed, up, down):
        joined = back_product(normed, up)
        active = swiglu(joined).astype(HALF)
        return joined, active, product(active, down).astype(HALF)

    def ffn_backward(grad_low, joined, up, down):
        grad_active = back_product(grad_low, down)
        grad_joined = jax.vjp(swiglu, joined)[1](grad_active)[0].astype(HALF)
        return grad_joined, product(grad_joined, up).astype(HALF)

    f1, a1, part = ffn_forward(n2, first_up, conv_down)

    def enter_attention(part_ref, h1_ref, gain_ref, m_ref, n3_ref, zslots, zs, zr, gs, gr):
        where = place()
        greet(head_peers(where, heads))
        copies = scatter_start(part_ref, zslots, zs, zr, where, heads, own)
        middle = (h1_ref[...] + scatter_sum(copies, part_ref, zslots, where, own)).astype(HALF).astype(FLOAT)
        m_ref[...] = middle
        n3_ref[rows_of(where[2], own), :] = norm_apply(middle, gain_ref[0:1, :]).astype(HALF)
        wait_all(gather_start(n3_ref, gs, gr, where, heads, own))

    middle, n3 = call(
        enter_attention,
        "enter_attention",
        1,
        [((own, width), FLOAT), ((tokens, width), HALF)],
        zscratch + zsems,
        [part, h1, attn_gains],
        moved=60 << 20,
    )

    def slot_peer(me, j, h):
        other = lax.rem(me + j, slots)
        return (lax.rem(other, sections), lax.div(other, sections), h)

    def query_key(n3_ref, wq_ref, wp_ref, cos_ref, sin_ref, qg_ref, kg_ref, qr_ref, r_ref, q_ref, all_ref, send, recv):
        s, q, h = place()
        me = q * sections + s
        peers = [slot_peer(me, j, h) for j in range(1, slots)]
        greet(peers)
        cos, sin = cos_ref[...], sin_ref[...]
        r_ref[...] = product(n3_ref[...], wp_ref[...])
        half_pair = pair_width // 2
        for start, size in chunks_of(half_pair):
            span = slice(start, start + size)
            all_ref[me, :, span] = rotary(r_ref[:, span], kg_ref[...], cos, sin).astype(HALF)
        all_ref[me, :, half_pair:] = r_ref[:, half_pair:].astype(HALF)
        copies = []
        for j, peer in enumerate(peers):
            copy = remote(all_ref.at[me], all_ref.at[me], send.at[j], recv.at[j], peer)
            copy.start()
            copies.append(copy)
        qr_ref[...] = product(n3_ref[...], wq_ref[...])
        for start, size in chunks_of(query_width):
            span = slice(start, start + size)
            q_ref[:, span] = rotary(qr_ref[:, span], qg_ref[...], cos, sin).astype(HALF)
        wait_all(copies)

    query_raw, pair_raw, queries, all_pairs = call(
        query_key,
        "query_key",
        2,
        [
            ((tokens, query_width), FLOAT),
            ((tokens, pair_width), FLOAT),
            ((tokens, query_width), HALF),
            ((slots, tokens, pair_width), HALF),
        ],
        [dma(slots - 1), dma(slots - 1)],
        [n3, w_query, w_pair, cosine, sine, query_gain, key_gain],
        flops=5 * 10**8,
        moved=40 << 20,
    )

    def query_rows(ref, m, c):
        block = ref[m * rows : (m + 1) * rows, :]
        base = c * group * head_width
        return jnp.concatenate(
            [block[:, base + r * head_width : base + (r + 1) * head_width] for r in range(group)], 0
        )

    def keys_of(all_ref, at, c, kind):
        block = all_ref[:, at * rows : (at + 1) * rows, :].reshape(block_tok, pair_width)
        base = kind * kv_local * head_width + c * head_width
        return block[:, base : base + head_width]

    def allowed_pairs(segq_ref, seg_ref, m, at, s, q):
        own_segments = segq_ref[m * rows : (m + 1) * rows, :]
        allowed = own_segments == seg_ref[at : at + 1, :]
        if at == m:
            base = q * local_rows + s * rows
            order = base + lax.broadcasted_iota(jnp.int32, (rows, block_tok), 0)
            allowed = allowed & (lax.broadcasted_iota(jnp.int32, (rows, block_tok), 1) <= order)
        bias = jnp.where(allowed, 0.0, -1e30)
        return jnp.concatenate([bias] * group, 0)

    def probabilities(rows_in, keys, biases):
        scores = [
            jnp.where(bias < 0, -1e30, back_product(rows_in, key) * score_scale)
            for key, bias in zip(keys, biases)
        ]
        summit = functools.reduce(jnp.maximum, [jnp.max(part, -1, keepdims=True) for part in scores])
        raised = [jnp.exp(part - summit) for part in scores]
        total = functools.reduce(jnp.add, [jnp.sum(part, -1, keepdims=True) for part in raised])
        inverse = 1.0 / total
        return [part * inverse for part in raised]

    def attend(q_ref, all_ref, segq_ref, seg_ref, o_ref):
        s, q, _ = place()
        for m in range(micro):
            biases = [allowed_pairs(segq_ref, seg_ref, m, at, s, q) for at in range(m + 1)]
            results = []
            for c in range(kv_local):
                keys = [keys_of(all_ref, at, c, 0) for at in range(m + 1)]
                weights = probabilities(query_rows(q_ref, m, c), keys, biases)
                total = functools.reduce(
                    jnp.add,
                    [product(weights[at].astype(HALF), keys_of(all_ref, at, c, 1)) for at in range(m + 1)],
                )
                results += [total[r * rows : (r + 1) * rows] for r in range(group)]
            o_ref[m * rows : (m + 1) * rows, :] = jnp.concatenate(results, -1).astype(HALF)

    (attended,) = call(
        attend,
        "attend",
        None,
        [((tokens, query_width), HALF)],
        [],
        [queries, all_pairs, local_segments, segment_ids],
        flops=2 * 10**9,
        moved=30 << 20,
    )

    def leave_attention(o_ref, wo_ref, m_ref, gain_ref, h2_ref, n4_ref, part, zslots, zs, zr, gs, gr):
        where = place()
        greet(head_peers(where, heads))
        part[...] = product(o_ref[...], wo_ref[...]).astype(HALF)
        copies = scatter_start(part, zslots, zs, zr, where, heads, own)
        hidden = m_ref[...] + scatter_sum(copies, part, zslots, where, own)
        h2_ref[...] = hidden
        n4_ref[rows_of(where[2], own), :] = norm_apply(hidden, gain_ref[1:2, :]).astype(HALF)
        wait_all(gather_start(n4_ref, gs, gr, where, heads, own))

    part_scratch = [pltpu.VMEM((tokens, width), HALF)]
    h2, n4 = call(
        leave_attention,
        "leave_attention",
        3,
        [((own, width), FLOAT), ((tokens, width), HALF)],
        part_scratch + zscratch + zsems,
        [attended, attn_out, middle, attn_gains],
        moved=60 << 20,
    )

    f2, a2, part_y = ffn_forward(n4, second_up, attn_down)
    gf2, part_g = ffn_backward(g, f2, second_up, attn_down)

    def turn_back(
        py_ref, pg_ref, h2_ref, g_ref, gain_ref, yout_ref, gh2_ref, low_ref, gg_ref,
        yslots, zslots, ys, yr, zs, zr, gs, gr, hs, hr,
    ):
        where = place()
        mine = rows_of(where[2], own)
        greet(head_peers(where, heads))
        copies = scatter_start(pg_ref, zslots, zs, zr, where, heads, own)
        later = scatter_start(py_ref, yslots, ys, yr, where, heads, own)
        hidden = h2_ref[...]
        grad_normed = scatter_sum(copies, pg_ref, zslots, where, own)
        grad_hidden, grad_gain = norm_back(hidden, gain_ref[1:2, :], grad_normed)
        grad = g_ref[mine, :].astype(FLOAT) + grad_hidden
        gh2_ref[...] = grad
        gg_ref[...] = grad_gain
        low_ref[mine, :] = grad.astype(HALF)
        gathers = gather_start(low_ref, gs, gr, where, heads, own)
        yout_ref[mine, :] = (hidden + scatter_sum(later, py_ref, yslots, where, own)).astype(HALF)
        gathers += gather_start(yout_ref, hs, hr, where, heads, own)
        wait_all(gathers)

    yout, gh2, gh2_low, grad_gain_attn1 = call(
        turn_back,
        "turn_back",
        4,
        [((tokens, width), HALF), ((own, width), FLOAT), ((tokens, width), HALF), ((1, width), FLOAT)],
        zscratch * 2 + zsems * 2,
        [part_y, part_g, h2, g, attn_gains],
        moved=90 << 20,
    )

    def attend_back(low_ref, wo_ref, q_ref, all_ref, segq_ref, seg_ref, gq_ref, gp_ref, grads, totals):
        s, q, _ = place()
        grads[...] = back_product(low_ref[...], wo_ref[...]).astype(HALF)
        for m in range(micro):
            biases = [allowed_pairs(segq_ref, seg_ref, m, at, s, q) for at in range(m + 1)]
            results = []
            for c in range(kv_local):
                keys = [keys_of(all_ref, at, c, 0) for at in range(m + 1)]
                values = [keys_of(all_ref, at, c, 1) for at in range(m + 1)]
                rows_in = query_rows(q_ref, m, c)
                grad_rows = query_rows(grads, m, c)
                chances = probabilities(rows_in, keys, biases)
                grad_chances = [back_product(grad_rows, value) for value in values]
                inner = functools.reduce(
                    jnp.add,
                    [jnp.sum(a * b, -1, keepdims=True) for a, b in zip(grad_chances, chances)],
                )
                total = None
                for at in range(m + 1):
                    grad_scores = (chances[at] * (grad_chances[at] - inner)).astype(HALF)
                    term = product(grad_scores, keys[at])
                    total = term if total is None else total + term
                    grad_key = outer_sum(grad_scores, rows_in) * score_scale
                    grad_value = outer_sum(chances[at].astype(HALF), grad_rows)
                    if at == m:
                        totals[at, c] = grad_key
                        totals[at, kv_local + c] = grad_value
                    else:
                        totals[at, c] += grad_key
                        totals[at, kv_local + c] += grad_value
                total = total * score_scale
                results += [total[r * rows : (r + 1) * rows] for r in range(group)]
            gq_ref[m * rows : (m + 1) * rows, :] = jnp.concatenate(results, -1)
        for at in range(micro):
            joined = jnp.concatenate([totals[at, k] for k in range(2 * kv_local)], -1).astype(HALF)
            gp_ref[:, at * rows : (at + 1) * rows, :] = joined.reshape(slots, rows, pair_width)

    grad_queries, grad_pairs = call(
        attend_back,
        "attend_back",
        None,
        [((tokens, query_width), FLOAT), ((slots, tokens, pair_width), HALF)],
        [
            pltpu.VMEM((tokens, query_width), HALF),
            pltpu.VMEM((micro, 2 * kv_local, block_tok, head_width), FLOAT),
        ],
        [gh2_low, attn_out, queries, all_pairs, local_segments, segment_ids],
        flops=5 * 10**9,
        moved=50 << 20,
    )

    def back_through_entry(
        gp_ref, gq_ref, qr_ref, r_ref, cos_ref, sin_ref, qg_ref, kg_ref, wq_ref, wp_ref, m_ref, gh2_ref, gain_ref,
        bq_ref, br_ref, low_ref, gg_ref, gqk_ref,
        pair_slots, part, zslots, ps, pr, zs, zr, gs, gr,
    ):
        where = place()
        s, q, h = where
        mine = rows_of(h, own)
        me = q * sections + s
        peers = [slot_peer(me, j, h) for j in range(1, slots)]
        greet(peers + head_peers(where, heads))
        copies = []
        for j, peer in enumerate(peers):
            slot = peer[1] * sections + peer[0]
            copy = remote(gp_ref.at[slot], pair_slots.at[j], ps.at[j], pr.at[j], peer)
            copy.start()
            copies.append(copy)
        cos, sin = cos_ref[...], sin_ref[...]
        gqk_ref[...] = jnp.zeros_like(gqk_ref)
        for start, size in chunks_of(query_width):
            span = slice(start, start + size)
            grad_raw, grad_gain = rotary_back(qr_ref[:, span], qg_ref[...], cos, sin, gq_ref[:, span])
            bq_ref[:, span] = grad_raw.astype(HALF)
            gqk_ref[0:1, :size] += grad_gain
        partial = back_product(bq_ref[...], wq_ref[...])
        wait_all(copies)
        grad_pair = gp_ref[me].astype(FLOAT)
        for j in range(slots - 1):
            grad_pair = grad_pair + pair_slots[j].astype(FLOAT)
        half_pair = pair_width // 2
        for start, size in chunks_of(half_pair):
            span = slice(start, start + size)
            grad_raw, grad_gain = rotary_back(r_ref[:, span], kg_ref[...], cos, sin, grad_pair[:, span])
            br_ref[:, span] = grad_raw.astype(HALF)
            gqk_ref[1:2, :size] += grad_gain
        br_ref[:, half_pair:] = grad_pair[:, half_pair:].astype(HALF)
        part[...] = (partial + back_product(br_ref[...], wp_ref[...])).astype(HALF)
        zcopies = scatter_start(part, zslots, zs, zr, where, heads, own)
        grad_normed = scatter_sum(zcopies, part, zslots, where, own)
        grad_entry, grad_gain = norm_back(m_ref[...], gain_ref[0:1, :], grad_normed)
        gg_ref[...] = grad_gain
        low_ref[mine, :] = (gh2_ref[...] + grad_entry).astype(HALF)
        wait_all(gather_start(low_ref, gs, gr, where, heads, own))

    bq, br, gm_low, grad_gain_attn0, grad_qk = call(
        back_through_entry,
        "back_through_entry",
        5,
        [
            ((tokens, query_width), HALF),
            ((tokens, pair_width), HALF),
            ((tokens, width), HALF),
            ((1, width), FLOAT),
            ((8, 128), FLOAT),
        ],
        [pltpu.VMEM((slots - 1, tokens, pair_width), HALF)]
        + part_scratch
        + zscratch
        + [dma(slots - 1), dma(slots - 1)]
        + zsems,
        [
            grad_pairs, grad_queries, query_raw, pair_raw, cosine, sine, query_gain, key_gain,
            w_query, w_pair, middle, gh2, attn_gains,
        ],
        flops=10**9,
        moved=90 << 20,
    )

    gf1, part = ffn_backward(gm_low, f1, first_up, conv_down)

    def back_through_ffn(part_ref, h1_ref, gm_ref, gain_ref, gh1_ref, low_ref, gg_ref, zslots, zs, zr, gs, gr):
        where = place()
        mine = rows_of(where[2], own)
        greet(head_peers(where, heads))
        copies = scatter_start(part_ref, zslots, zs, zr, where, heads, own)
        grad_normed = scatter_sum(copies, part_ref, zslots, where, own)
        grad_hidden, grad_gain = norm_back(h1_ref[...], gain_ref[1:2, :], grad_normed)
        gg_ref[...] = grad_gain
        grad = gm_ref[mine, :].astype(FLOAT) + grad_hidden
        gh1_ref[...] = grad
        low_ref[mine, :] = grad.astype(HALF)
        wait_all(gather_start(low_ref, gs, gr, where, heads, own))

    gh1, gh1_low, grad_gain_conv1 = call(
        back_through_ffn,
        "back_through_ffn",
        6,
        [((own, width), FLOAT), ((tokens, width), HALF), ((1, width), FLOAT)],
        zscratch + zsems,
        [part, h1, gm_low, conv_gains],
        moved=60 << 20,
    )

    def conv_backward(
        low_ref, gh1_ref, pc_ref, edge_ref, same_ref, kernel_ref, wout_ref, win_ref, x_ref, gain_ref, yout_ref,
        bp_ref, gk_ref, gg_ref, edges_ref,
        ext, spread, gz_ext, outgoing, arrived, full, part, zslots,
        edge_send, edge_recv, swap_send, swap_recv, zs, zr, gs, gr,
    ):
        where = place()
        s, q, h = where
        mine = rows_of(h, own)
        first = s == 0
        partner = (1 - s, q, h)
        preceding = (1 - s, jnp.where(first, lax.rem(q + seqs - 1, seqs), q), h)
        following = (1 - s, jnp.where(first, q, lax.rem(q + 1, seqs)), h)
        greet([partner, preceding, following] + head_peers(where, heads))
        gated = pc_ref[0] * pc_ref[2]
        grad_y = back_product(low_ref[...], wout_ref[...])
        gz = grad_y * pc_ref[1]
        zero = jnp.zeros((8, channels), FLOAT)
        for m in range(micro):
            span = slice(m * rows, (m + 1) * rows)
            one = jnp.where(same_ref[span, 0:1] > 0, gz[span], 0.0) * kernel_ref[1:2, :]
            two = jnp.where(same_ref[span, 1:2] > 0, gz[span], 0.0) * kernel_ref[0:1, :]
            gz_ext[0, m, 0:rows, :] = one
            gz_ext[0, m, rows : rows + 8, :] = zero
            gz_ext[1, m, 0:rows, :] = two
            gz_ext[1, m, rows : rows + 8, :] = zero
            outgoing[m] = zero
            outgoing[m, 0:1, :] = two[0:1]
            outgoing[m, 1:2, :] = one[0:1] + two[1:2]
        edge = remote(outgoing, arrived, edge_send.at[0], edge_recv.at[0], preceding)
        edge.start()
        taps = [None, None, None]
        for m in range(micro):
            span = slice(m * rows, (m + 1) * rows)
            ext[m, 0:8, :] = edge_ref[m]
            ext[m, 8 : 8 + rows, :] = gated[span]
            back_one = jnp.where(same_ref[span, 0:1] > 0, shifted_rows(ext, m, 1), 0.0)
            back_two = jnp.where(same_ref[span, 1:2] > 0, shifted_rows(ext, m, 2), 0.0)
            mixed = (
                kernel_ref[2:3, :] * gated[span]
                + kernel_ref[1:2, :] * back_one
                + kernel_ref[0:1, :] * back_two
            )
            bp_ref[span, channels : 2 * channels] = (grad_y[span] * mixed).astype(HALF)
            for k, value in enumerate((back_two, back_one, gated[span])):
                term = jnp.sum(value * gz[span], 0, keepdims=True)
                taps[k] = term if taps[k] is None else taps[k] + term
        gk_ref[...] = jnp.concatenate(taps + [jnp.zeros((5, channels), FLOAT)], 0)
        for m in range(micro):
            span = slice(m * rows, (m + 1) * rows)
            spread[m] = (
                kernel_ref[2:3, :] * gz[span]
                + gz_ext[0, m, 1 : rows + 1, :]
                + gz_ext[1, m, 2 : rows + 2, :]
            )
        edge.wait()
        wrap = (s == sections - 1) & (q == seqs - 1)
        for m in range(micro):
            follow = arrived[m + 1, 0:2, :] if m + 1 < micro else jnp.zeros((2, channels), FLOAT)
            spread[m, rows - 2 : rows, :] += jnp.where(wrap, follow, arrived[m, 0:2, :])
        for m in range(micro):
            span = slice(m * rows, (m + 1) * rows)
            bp_ref[span, 0:channels] = (spread[m] * pc_ref[2, span, :]).astype(HALF)
            bp_ref[span, 2 * channels :] = (spread[m] * pc_ref[0, span, :]).astype(HALF)
        total = back_product(bp_ref[:, 0:channels], win_ref[0])
        total = total + back_product(bp_ref[:, channels : 2 * channels], win_ref[1])
        total = total + back_product(bp_ref[:, 2 * channels :], win_ref[2])
        part[...] = total.astype(HALF)
        copies = scatter_start(part, zslots, zs, zr, where, heads, own)
        start = x_ref[mine, :].astype(FLOAT)
        grad_normed = scatter_sum(copies, part, zslots, where, own)
        grad_start, grad_gain = norm_back(start, gain_ref[0:1, :], grad_normed)
        gg_ref[...] = grad_gain
        full[mine, :] = (gh1_ref[...] + grad_start).astype(HALF)
        wait_all(gather_start(full, gs, gr, where, heads, own))
        keep = pl.ds(pl.multiple_of(s * rows, rows), rows)
        edges_ref[0, :, keep, :] = jnp.where(first, full[...], yout_ref[...]).reshape(micro, rows, width)
        part[...] = jnp.where(first, yout_ref[...], full[...])
        swaps = []
        for m in range(micro):
            copy = remote(
                part.at[m * rows : (m + 1) * rows], edges_ref.at[0, m, keep], swap_send.at[m], swap_recv.at[m], partner
            )
            copy.start()
            swaps.append(copy)
        wait_all(swaps)

    bp, grad_taps, grad_gain_conv0, section_edges = call(
        conv_backward,
        "conv_backward",
        7,
        [
            ((tokens, 3 * channels), HALF),
            ((8, channels), FLOAT),
            ((1, width), FLOAT),
            ((1, micro, local_rows, width), HALF),
        ],
        [
            pltpu.VMEM((micro, 8 + rows, channels), FLOAT),
            pltpu.VMEM((micro, rows, channels), FLOAT),
            pltpu.VMEM((2, micro, rows + 8, channels), FLOAT),
            pltpu.VMEM((micro, 8, channels), FLOAT),
            pltpu.VMEM((micro, 8, channels), FLOAT),
            pltpu.VMEM((tokens, width), HALF),
            pltpu.VMEM((tokens, width), HALF),
        ]
        + zscratch
        + [dma(1), dma(1), dma(micro), dma(micro)]
        + zsems,
        [gh1_low, gh1, projected, edge_gated, same, conv_kernel, conv_out, w_in, x, conv_gains, yout],
        flops=10**9,
        moved=80 << 20,
    )

    swap_pairs = [(i, sections - 1 - i) for i in range(sections)]

    def both_tokens(array):
        return jnp.concatenate([array, lax.ppermute(array, "section", swap_pairs)], 0)

    def half_of(array):
        low, high = array[:, :half_model], array[:, half_model:]
        kept = jnp.where(section == 0, low, high)
        given = jnp.where(section == 0, high, low)
        return jnp.concatenate([kept, lax.ppermute(given, "section", swap_pairs)], 0)

    def weight_grad(former_half, latter_all):
        summed = outer_sum(former_half, latter_all).astype(HALF)
        return lax.psum_scatter(summed, "seq", scatter_dimension=0, tiled=True).astype(FLOAT)

    n4_half, g_half = half_of(n4), half_of(g)
    grad_attn_down = weight_grad(g_half, both_tokens(a2)).T
    grad_attn_up = weight_grad(n4_half, both_tokens(gf2)).reshape(-1, 2, hidden_units)
    grad_attn_out = weight_grad(half_of(gh2_low), both_tokens(attended)).T
    n3_half = half_of(n3)
    grad_mixers = weight_grad(n3_half, both_tokens(jnp.concatenate([bq, br], 1)))
    grad_query = grad_mixers[:, :query_width]
    grad_keyval = grad_mixers[:, query_width:].reshape(-1, 2, pair_width // 2)
    grad_conv_down = weight_grad(half_of(gm_low), both_tokens(a1)).T
    grad_conv_up = weight_grad(half_of(n2), both_tokens(gf1)).reshape(-1, 2, hidden_units)
    grad_conv_out = weight_grad(half_of(gh1_low), both_tokens(mixed)).T
    grad_conv_in = weight_grad(half_of(n1), both_tokens(bp)).reshape(-1, 3, channels)

    folded = grad_qk[0:2, :head_width] + grad_qk[0:2, head_width : 2 * head_width]
    gain_rows = jnp.concatenate([grad_gain_conv0, grad_gain_conv1, grad_gain_attn0, grad_gain_attn1], 0)
    gain_rows, folded = lax.psum((gain_rows, folded), ("section", "seq", "head"))
    grad_taps = lax.psum(grad_taps[0:3], ("section", "seq"))
    share = width // (sections * seqs)
    gain_share = lax.dynamic_slice_in_dim(gain_rows, (section * seqs + seq) * share, share, 1)
    return (
        section_edges,
        gain_share[0:2],
        grad_conv_in,
        grad_taps,
        grad_conv_out,
        grad_conv_up,
        grad_conv_down,
        gain_share[2:4],
        grad_query,
        grad_keyval,
        folded,
        grad_attn_out,
        grad_attn_up,
        grad_attn_down,
    )


def solution(mesh):
    return jax.shard_map(
        per_device,
        mesh=mesh,
        in_specs=(
            P("section", None, "seq", None),
            P(),
            P(None, "seq"),
            P(),
            P(None, None, "head"),
            P(None, "head"),
            P("head", None),
            P(None, None, "head"),
            P("head", None),
            P(),
            P(None, "head"),
            P(None, None, "head"),
            P(),
            P("head", None),
            P(None, None, "head"),
            P("head", None),
        ),
        out_specs=(
            P("section", None, "seq", None),
            P(None, ("section", "seq")),
            P(("section", "seq"), None, "head"),
            P(None, "head"),
            P("head", ("section", "seq")),
            P(("section", "seq"), None, "head"),
            P("head", ("section", "seq")),
            P(None, ("section", "seq")),
            P(("section", "seq"), "head"),
            P(("section", "seq"), None, "head"),
            P(),
            P("head", ("section", "seq")),
            P(("section", "seq"), None, "head"),
            P("head", ("section", "seq")),
        ),
        check_vma=False,
    )
```

time: 1790 us -> 769 us (0.43)
  waiting for transfers between devices: 1040 us -> 171 us
  Pallas kernels: 0 us -> 392 us
  local copies, waits for them, and re-layouts: 340 us -> 42.7 us
  matrix products: 225 us -> 62.1 us
  other arithmetic: 103 us -> 16.3 us
  blocking collectives: 24.5 us -> 60.4 us
  starting transfers between devices: 25.5 us -> 5.16 us
    psum x7 -> x0, waiting for transfers between devices: 477 us -> none  [the longest x4 279 us: head_total(): lax.psum(partial_value.astype(jnp.bfloat16), 'head').astype(jnp.float32)]
    pallas_call x0 -> x10, Pallas kernels: none -> 392 us  [call(): pl.pallas_call(body, name=name, out_shape=[jax.ShapeDtypeStruct(shape, ki...]
    unnamed x23 -> x8, waiting for transfers between devices: 337 us -> 0.13 us
    unnamed x278 -> x74, local copies, waits for them, and re-layouts: 156 us -> 8.58 us
    convert_element_type x11 -> x3, local copies, waits for them, and re-layouts: 90.6 us -> 2.59 us  [the longest x2 2.51 us: ffn_forward(): active = swiglu(joined).astype(HALF)]
    dot_general x17 -> x4, matrix products: 81.6 us -> 15.5 us  [product(): return jnp.dot(former, latter, preferred_element_type=FLOAT)]
    dot_general x21 -> x4, matrix products: 76.3 us -> 19.8 us  [back_product(): lax.dot_general(former, latter, (((1,), (1,)), ((), ())), preferred_eleme...]
    convert_element_type x32 -> x3, other arithmetic: 46.5 us -> 0.78 us  [the longest x2 0.7 us: ffn_backward(): grad_joined = jax.vjp(swiglu, joined)[1](grad_active)[0].astype(HALF)]
  transfers between devices with their start and end apart: 23 -> 24, of which waited for: 18 -> 11; matrix products, arithmetic and copies ran while one was open for 12% -> 7% of each run, Pallas kernels for 0% -> 7%
where the time goes in v1:
time: 769 us; the launch traced here: 764 us
  Pallas kernels  392 us (51%)
  waiting for transfers between devices  171 us (22%)
  matrix products  62.1 us (8%)
  blocking collectives  60.4 us (8%)
  local copies, waits for them, and re-layouts  42.7 us (6%)
  other arithmetic  16.3 us (2%)
  between operations  14.8 us (2%)
    pallas_call x10, Pallas kernels, call(): pl.pallas_call(body, name=name, out_shape=[jax.ShapeDtypeStruct(shape, ki...  392 us
    reduce_scatter x8, waiting for transfers between devices, weight_grad(): lax.psum_scatter(summed, 'seq', scatter_dimension=0, tiled=True)  155 us
    psum x1, blocking collectives, per_device(): lax.psum((gain_rows, folded), ('section', 'seq', 'head'))  44.2 us
    dot_general x8, matrix products, outer_sum(): lax.dot_general(former, latter, (((0,), (0,)), ((), ())), preferred_eleme...  26.8 us
    dot_general x4, matrix products, back_product(): lax.dot_general(former, latter, (((1,), (1,)), ((), ())), preferred_eleme...  19.8 us
    psum x1, blocking collectives, per_device(): grad_taps = lax.psum(grad_taps[0:3], ('section', 'seq'))  16.2 us
    dot_general x4, matrix products, product(): return jnp.dot(former, latter, preferred_element_type=FLOAT)  15.5 us
  transfers between devices with their start and end apart: 24, of which 11 were waited for; matrix products, arithmetic and copies ran while one was open for 7% of the time, Pallas kernels for 7%

profile of v1, /device:TPU:0, one launch (start us, length us, event | category | flops | bytes accessed | tf_op | source)
XLA Modules:
  0.0 763.9 jit_solution(9582701160816586155)
XLA Ops:
  15.1 51.4 %conv_forward.1 = (bf16[256,1536]{1,0:T(8,128)(2,1)}, bf16[256,1536]{1,0:T(8,128)(2,1)}, bf16[256,1536]{1,0:T(8,128)(2,1)}, f32[3,256,384]{2,1,0:T(8,128)}, f32[...) custom-call(bf16[1,4,128,1536]{3,2,1,0:T(8,128)(2,1)} %in_ref.1, ...), custom_call_target="tpu_custom_call" | custom-call | flops 1000000000 | bytes 83886080 | tf_op jit(solution)/shard_map/conv_forward/pallas_call | solution.py:156
  66.5 6.7 fusion.66
  83.3 5.3 convolution_convert_fusion.8.part_ref
  88.6 38.2 %enter_attention.1 = (f32[64,1536]{1,0:T(8,128)}, bf16[256,1536]{1,0:T(8,128)(2,1)}) custom-call(bf16[256,1536]{1,0:T(8,128)(2,1)} %convolution_convert_fusion.8.part_ref, f32[64,1536]{1,0:T(8,128)} %get-tuple-element.49.h1_ref, f32[2,1536]{1,0:T(2,128)} %gain_ref.11), custom_call_target="tpu_custom_call" | custom-call | bytes 62914560 | tf_op jit(solution)/shard_map/enter_attention/pallas_call | solution.py:156
  126.8 16.3 %query_key.1 = (f32[256,384]{1,0:T(8,128)}, f32[256,256]{1,0:T(8,128)}, bf16[256,384]{1,0:T(8,128)(2,1)}, bf16[8,256,256]{2,1,0:T(8,128)(2,1)}) custom-call(bf16[256,1536]{1,0:T(8,128)(2,1)} %get-tuple-element.50.n3_ref, bf16[1536,384]{1,0:T(8,128)(2,1)} %wq_ref.3, bf16[1536,256]{1,0:T(8,128)(2,1)} %bitcast.57, f32[256,128]{1,0:T(8,128)} %copy.51.cos_ref, ...), custom_call_target="tpu_custom_call" | custom-call | flops 500000000 | bytes 41943040 | tf_op jit(solution)/shard_map/query_key/pallas_call | solution.py:156
  143.1 7.2 attend.1.o_ref
  150.4 42.4 %leave_attention.1 = (f32[64,1536]{1,0:T(8,128)}, bf16[256,1536]{1,0:T(8,128)(2,1)}) custom-call(bf16[256,384]{1,0:T(8,128)(2,1)} %attend.1.o_ref, bf16[384,1536]{1,0:T(8,128)(2,1)} %wo_ref.3, f32[64,1536]{1,0:T(8,128)} %get-tuple-element.53.m_ref, f32[2,1536]{1,0:T(2,128)} %gain_ref.11), custom_call_target="tpu_custom_call" | custom-call | bytes 62914560 | tf_op jit(solution)/shard_map/leave_attention/pallas_call | solution.py:156
  192.8 6.5 fusion.67
  207.9 74.5 %turn_back.1 = (bf16[256,1536]{1,0:T(8,128)(2,1)}, f32[64,1536]{1,0:T(8,128)}, bf16[256,1536]{1,0:T(8,128)(2,1)}, f32[1,1536]{1,0:T(1,128)}) custom-call(bf16[256,1536]{1,0:T(8,128)(2,1)} %convolution_convert_fusion.7.py_ref, bf16[256,1536]{1,0:T(8,128)(2,1)} %convolution_convert_fusion.6.pg_ref, f32[64,1536]{1,0:T(8,128)} %get-tuple-element.56.h2_ref, ...), custom_call_target="tpu_custom_call" | custom-call | bytes 94371840 | tf_op jit(solution)/shard_map/turn_back/pallas_call | solution.py:156
  282.4 14.1 %attend_back.1 = (f32[256,384]{1,0:T(8,128)}, bf16[8,256,256]{2,1,0:T(8,128)(2,1)}) custom-call(bf16[256,1536]{1,0:T(8,128)(2,1)} %get-tuple-element.57.low_ref, bf16[384,1536]{1,0:T(8,128)(2,1)} %wo_ref.3, bf16[256,384]{1,0:T(8,128)(2,1)} %get-tuple-element.51.q_ref, bf16[8,256,256]{2,1,0:T(8,128)(2,1)} %get-tuple-element.52.all_ref, ...), custom_call_target="tpu_custom_call" | custom-call | flops 5000000000 | bytes 52428800 | tf_op jit(solution)/shard_map/attend_back/pallas_call | solution.py:156
  296.6 55.2 %back_through_entry.1 = (bf16[256,384]{1,0:T(8,128)(2,1)}, bf16[256,256]{1,0:T(8,128)(2,1)}, bf16[256,1536]{1,0:T(8,128)(2,1)}, f32[1,1536]{1,0:T(1,128)}, f32[8,128]{1,0:T(8,128)}) custom-call(bf16[8,256,256]{2,1,0:T(8,128)(2,1)} %get-tuple-element.58.gp_ref, f32[256,384]{1,0:T(8,128)} %get-tuple-element.59.gq_ref, f32[256,384]{1,0:T(8,128)} %get-tuple-element.60.qr_ref, ...), custom_call_target="tpu_custom_call" | custom-call | flops 1000000000 | bytes 94371840 | tf_op jit(solution)/shard_map/back_through_entry/pallas_call | solution.py:156
  351.8 4.8 fusion.54
  360.9 42.0 %back_through_ffn.1 = (f32[64,1536]{1,0:T(8,128)}, bf16[256,1536]{1,0:T(8,128)(2,1)}, f32[1,1536]{1,0:T(1,128)}) custom-call(bf16[256,1536]{1,0:T(8,128)(2,1)} %convolution_convert_fusion.5.part_ref, f32[64,1536]{1,0:T(8,128)} %get-tuple-element.49.h1_ref, bf16[256,1536]{1,0:T(8,128)(2,1)} %get-tuple-element.63.gm_ref, f32[2,1536]{1,0:T(2,128)} %gain_ref.13), custom_call_target="tpu_custom_call" | custom-call | bytes 62914560 | tf_op jit(solution)/shard_map/back_through_ffn/pallas_call | solution.py:156
  416.1 50.3 %conv_backward.1 = (bf16[256,1152]{1,0:T(8,128)(2,1)}, f32[8,384]{1,0:T(8,128)}, f32[1,1536]{1,0:T(1,128)}, bf16[1,4,128,1536]{3,2,1,0:T(8,128)(2,1)}) custom-call(bf16[256,1536]{1,0:T(8,128)(2,1)} %get-tuple-element.64.low_ref, f32[64,1536]{1,0:T(8,128)} %get-tuple-element.65.gh1_ref, f32[3,256,384]{2,1,0:T(8,128)} %get-tuple-element.66.pc_ref, ...), custom_call_target="tpu_custom_call" | custom-call | flops 1000000000 | bytes 83886080 | tf_op jit(solution)/shard_map/conv_backward/pallas_call | solution.py:156
  480.0 4.5 convolution_convert_fusion.3
  500.8 4.8 convolution_convert_fusion.1
  511.4 4.8 convolution_convert_fusion
  516.9 16.2 %psum.22 = f32[3,384]{1,0:T(4,128)} all-reduce(f32[3,384]{1,0:T(4,128)S(1)} %slice.100), channel_id=1, replica_groups=mesh['section'=2,'seq'=4,'head'=4] {'section','seq'}, use_global_device_ids=true, to_apply=%region_2.3 | all-reduce | flops 1152 | bytes 9216 | tf_op jit(solution)/shard_map/psum | solution.py:814
  533.2 44.2 %all-reduce.5 = (f32[4,1536]{1,0:T(4,128)S(1)}, f32[2,64]{1,0:T(2,128)}) all-reduce(f32[4,1536]{1,0:T(4,128)S(1)} %pad_maximum_fusion, f32[2,64]{1,0:T(2,128)S(1)} %slice_add_fusion), channel_id=1, replica_groups=mesh['section'=2,'seq'=4,'head'=4] {'section','seq','head'}, use_global_device_ids=true, to_apply=%region_0.1 | all-reduce | flops 6272 | bytes 50176 | tf_op jit(solution)/shard_map/psum | solution.py:813
  589.0 32.0 %reduce-scatter.23.cloned.1.call-done = bf16[192,1728]{1,0:T(8,128)(2,1)} async-done(((bf16[768,1728]{1,0:T(8,128)(2,1)}), bf16[192,1728]{1,0:T(8,128)(2,1)}) %reduce-scatter.23.cloned.1.call-update) | async-done | bytes 663568 | tf_op jit(solution)/shard_map/reduce_scatter | solution.py:796
  623.3 62.8 %reduce-scatter.13.cloned.1.call-done = bf16[192,3456]{1,0:T(8,128)(2,1)} async-done(((bf16[768,3456]{1,0:T(8,128)(2,1)}), bf16[192,3456]{1,0:T(8,128)(2,1)}) %reduce-scatter.13.cloned.1.call-update) | async-done | bytes 1327120 | tf_op jit(solution)/shard_map/reduce_scatter | solution.py:796
  686.1 4.6 reshape.262
  690.7 60.4 %reduce-scatter.21.cloned.1.call-done = bf16[192,3456]{1,0:T(8,128)(2,1)} async-done(((bf16[768,3456]{1,0:T(8,128)(2,1)}), bf16[192,3456]{1,0:T(8,128)(2,1)}) %reduce-scatter.21.cloned.1.call-update) | async-done | bytes 1327120 | tf_op jit(solution)/shard_map/reduce_scatter | solution.py:796
  751.1 4.6 reshape.264
  (196 shorter events, 95.2 us)
Async XLA Ops:
  7.2 570.9 %reduce-scatter.11.cloned.1.call-start = ((), (), s32[]{:S(2)}) async-start(), calls=%async_computation.9 | async-start | bytes 737280 | tf_op jit(solution)/shard_map/reduce_scatter | solution.py:796
  404.1 2.1 collective-permute-start.2
  404.2 2.0 collective-permute-start.3
  407.6 172.1 %reduce-scatter.19.cloned.1.call-start = ((), (), s32[]{:S(2)}) async-start(), calls=%async_computation.13 | async-start | bytes 737280 | tf_op jit(solution)/shard_map/reduce_scatter | solution.py:796
  407.8 2.2 collective-permute-start.10
  408.5 1.4 collective-permute-start.11
  411.4 169.9 %reduce-scatter.17.cloned.1.call-start = ((), (), s32[]{:S(2)}) async-start(), calls=%async_computation.12 | async-start | bytes 1228800 | tf_op jit(solution)/shard_map/reduce_scatter | solution.py:796
  412.0 2.3 collective-permute-start.8
  412.4 1.8 collective-permute-start.9
  416.0 168.7 %reduce-scatter.9.cloned.1.call-start = ((), (), s32[]{:S(2)}) async-start(), calls=%async_computation.8 | async-start | bytes 2211840 | tf_op jit(solution)/shard_map/reduce_scatter | solution.py:796
  466.4 2.6 collective-permute-start.1
  466.8 2.2 collective-permute-start
  472.6 114.1 %reduce-scatter.15.cloned.1.call-start = ((), (), s32[]{:S(2)}) async-start(), calls=%async_computation.11 | async-start | bytes 3440640 | tf_op jit(solution)/shard_map/reduce_scatter | solution.py:796
  475.0 2.8 collective-permute-start.7
  476.3 3.7 collective-permute-start.6
  484.6 136.5 %reduce-scatter.23.cloned.1.call-start = ((), (), s32[]{:S(2)}) async-start(), calls=%async_computation.15 | async-start | bytes 3440640 | tf_op jit(solution)/shard_map/reduce_scatter | solution.py:796
  487.0 2.8 collective-permute-start.15
  488.2 3.8 collective-permute-start.14
  496.5 189.6 %reduce-scatter.13.cloned.1.call-start = ((), (), s32[]{:S(2)}) async-start(), calls=%async_computation.10 | async-start | bytes 6635520 | tf_op jit(solution)/shard_map/reduce_scatter | solution.py:796
  496.5 4.3 collective-permute-start.5
  497.6 3.2 collective-permute-start.4
  505.7 245.4 %reduce-scatter.21.cloned.1.call-start = ((), (), s32[]{:S(2)}) async-start(), calls=%async_computation.14 | async-start | bytes 6635520 | tf_op jit(solution)/shard_map/reduce_scatter | solution.py:796
  507.1 4.3 collective-permute-start.13
  507.5 3.9 collective-permute-start.12
  (35 other events, 426.1 us)
Sparse Core Ops, SparseCore 0:
  407.8 28.8 reduce-scatter.10
  439.7 25.0 reduce-scatter.18
  468.4 27.2 reduce-scatter.16
  498.6 32.9 reduce-scatter.8
  535.0 41.6 reduce-scatter.14
  580.1 40.9 reduce-scatter.22
  624.1 61.9 reduce-scatter.12
  689.1 61.9 reduce-scatter.20

commit v2 on v1

--- a/solution.py
+++ b/solution.py
@@ -13,6 +13,7 @@
 HALF = jnp.bfloat16
 MESH = pl.DeviceIdType.MESH
 VMEM = pl.BlockSpec(memory_space=pltpu.VMEM)
+ANY = pl.BlockSpec(memory_space=pl.ANY)
 
 
 def product(former, latter):
@@ -25,11 +26,6 @@
 
 def back_product(former, latter):
     return lax.dot_general(former, latter, (((1,), (1,)), ((), ())), preferred_element_type=FLOAT)
-
-
-def swiglu(joined):
-    half_width = joined.shape[1] // 2
-    return jax.nn.silu(joined[:, :half_width]) * joined[:, half_width:]
 
 
 def norm_apply(values, gain):
@@ -44,20 +40,12 @@
     return grad_values, jnp.sum(grad * values * scale, 0, keepdims=True)
 
 
+BLOCKS = 8
+LAG = 3
+
+
 def place():
     return lax.axis_index("section"), lax.axis_index("seq"), lax.axis_index("head")
-
-
-def greet(peers):
-    barrier = pltpu.get_barrier_semaphore()
-    for peer in peers:
-        pl.semaphore_signal(barrier, inc=1, device_id=peer, device_id_type=MESH)
-    pl.semaphore_wait(barrier, len(peers))
-
-
-def head_peers(where, size):
-    section, seq, head = where
-    return [(section, seq, lax.rem(head + k, size)) for k in range(1, size)]
 
 
 def remote(source, target, send, recv, peer):
@@ -71,41 +59,176 @@
     )
 
 
+def signal(peer):
+    pl.semaphore_signal(pltpu.get_barrier_semaphore(), inc=1, device_id=peer, device_id_type=MESH)
+
+
+def wait_greetings(count):
+    pl.semaphore_wait(pltpu.get_barrier_semaphore(), count)
+
+
+def greet(others, where=None, size=0):
+    for peer in others:
+        signal(peer)
+    if where is None:
+        wait_greetings(len(others))
+        return
+    section, seq, head = where
+    end = (head == 0) | (head == size - 1)
+
+    @pl.when(end)
+    def _():
+        signal((section, seq, jnp.where(head == 0, 1, size - 2)))
+        wait_greetings(len(others) + 1)
+
+    @pl.when(jnp.logical_not(end))
+    def _():
+        signal((section, seq, jnp.minimum(head + 1, size - 1)))
+        signal((section, seq, jnp.maximum(head - 1, 0)))
+        wait_greetings(len(others) + 2)
+
+
+def seq_peers(where, seqs):
+    section, seq, head = where
+    return [(section, lax.rem(seq + k, seqs), head) for k in range(1, seqs)]
+
+
 def rows_of(index, count):
     return pl.ds(pl.multiple_of(index * count, count), count)
-
-
-def scatter_start(part, slots, send, recv, where, size, count):
-    copies = []
-    for k, peer in enumerate(head_peers(where, size)):
-        copy = remote(part.at[rows_of(peer[2], count)], slots.at[k], send.at[k], recv.at[k], peer)
-        copy.start()
-        copies.append(copy)
-    return copies
-
-
-def scatter_sum(copies, part, slots, where, count):
-    total = part[rows_of(where[2], count), :].astype(FLOAT)
-    for copy in copies:
-        copy.wait()
-    for k in range(len(copies)):
-        total = total + slots[k].astype(FLOAT)
-    return total
-
-
-def gather_start(full, send, recv, where, size, count):
-    mine = full.at[rows_of(where[2], count)]
-    copies = []
-    for k, peer in enumerate(head_peers(where, size)):
-        copy = remote(mine, mine, send.at[k], recv.at[k], peer)
-        copy.start()
-        copies.append(copy)
-    return copies
 
 
 def wait_all(copies):
     for copy in copies:
         copy.wait()
+
+
+def start_all(copies):
+    for copy in copies:
+        copy.start()
+
+
+def loop(count, step):
+    def body(i, carried):
+        step(i)
+        return carried
+
+    lax.fori_loop(0, count, body, 0)
+
+
+def head_total(part, full, inbox, reduce_send, reduce_recv, gather_send, gather_recv, where, size, finish, filler=None, fillers=0):
+    section, seq, head = where
+    count = part.shape[0] // (2 * BLOCKS)
+    last = size - 1
+    end = (head == 0) | (head == last)
+
+    def rows(flow, i):
+        return rows_of(flow * BLOCKS + i, count)
+
+    def fill(t):
+        if filler is not None:
+
+            @pl.when(t < fillers)
+            def _():
+                filler(t)
+
+    def fill_rest(start):
+        if fillers > start:
+            loop(fillers - start, lambda i: filler(start + i))
+
+    def reduced(flow, i, peer):
+        return remote(part.at[rows(flow, i)], inbox.at[flow, i], reduce_send.at[flow, i], reduce_recv.at[flow, i], peer)
+
+    def gathered(flow, i, peer):
+        span = full.at[rows(flow, i)]
+        return remote(span, span, gather_send.at[flow, i], gather_recv.at[flow, i], peer)
+
+    @pl.when(end)
+    def _():
+        flow = jnp.where(head == 0, 0, 1)
+        inner = (section, seq, jnp.where(head == 0, 1, last - 1))
+        loop(BLOCKS, lambda i: reduced(1 - flow, i, inner).start())
+
+        def own(i):
+            reduced(flow, i, inner).wait_recv()
+            total = part[rows(flow, i), :].astype(FLOAT) + inbox[flow, i].astype(FLOAT)
+            full[rows(flow, i), :] = finish(flow, i, total)
+            gathered(flow, i, inner).start()
+            fill(i)
+
+        loop(BLOCKS, own)
+        fill_rest(BLOCKS)
+
+        def drain(i):
+            gathered(1 - flow, i, inner).wait_recv()
+            reduced(1 - flow, i, inner).wait_send()
+            gathered(flow, i, inner).wait_send()
+
+        loop(BLOCKS, drain)
+
+    @pl.when(jnp.logical_not(end))
+    def _():
+        low = head < size // 2
+        near = jnp.where(low, 1, 0)
+        ahead = (section, seq, jnp.where(low, head + 1, head - 1))
+        behind = (section, seq, jnp.where(low, head - 1, head + 1))
+
+        def add(flow, i, peer):
+            reduced(flow, i, peer).wait_recv()
+            span = rows(flow, i)
+            part[span, :] = (part[span, :].astype(FLOAT) + inbox[flow, i].astype(FLOAT)).astype(HALF)
+            reduced(flow, i, peer).start()
+
+        def forward(flow, i, peer):
+            gathered(flow, i, peer).wait_recv()
+            gathered(flow, i, peer).start()
+
+        def lagged(act, first, second, at):
+            def step(i):
+                fill(at + i)
+
+                @pl.when(i < BLOCKS)
+                def _():
+                    act(first, i, ahead)
+
+                @pl.when(i >= LAG)
+                def _():
+                    act(second, i - LAG, behind)
+
+            loop(BLOCKS + LAG, step)
+
+        lagged(add, near, 1 - near, 0)
+        lagged(forward, 1 - near, near, BLOCKS + LAG)
+        fill_rest(2 * (BLOCKS + LAG))
+
+        def drain(i):
+            reduced(near, i, ahead).wait_send()
+            reduced(1 - near, i, behind).wait_send()
+            gathered(1 - near, i, ahead).wait_send()
+            gathered(near, i, behind).wait_send()
+
+        loop(BLOCKS, drain)
+
+
+class Carried:
+    def __init__(self, sources, pieces, targets, sems):
+        self.sources, self.pieces, self.targets, self.sems = sources, pieces, targets, sems
+        self.copies = []
+
+    def peers(self, where, seqs):
+        return seq_peers(where, seqs) if self.pieces else []
+
+    def start(self, where, seqs, chosen=None):
+        for at, (array, kind, first, count) in enumerate(self.pieces):
+            if chosen is not None and at not in chosen:
+                continue
+            for k, peer in enumerate(seq_peers(where, seqs)):
+                source = self.sources[array].at[kind, peer[1], first : first + count]
+                copy = remote(source, self.targets[at].at[k], self.sems[0].at[at, k], self.sems[1].at[at, k], peer)
+                copy.start()
+                self.copies.append(copy)
+
+    def wait(self):
+        wait_all(self.copies)
 
 
 def turned(values):
@@ -149,20 +272,44 @@
     return grad_raw, jnp.sum(back * raw * scale, 0, keepdims=True)
 
 
-def call(body, name, collective, outs, scratch, args, flops=0, moved=0):
-    params = dict(vmem_limit_bytes=56 << 20)
+def call(body, name, collective, outs, scratch, args, carried=(), flops=0, moved=0):
+    params = dict(vmem_limit_bytes=60 << 20)
     if collective is not None:
         params.update(collective_id=collective, has_side_effects=True)
-    return pl.pallas_call(
-        body,
+    arrays = []
+    pieces = []
+    for array, kind, first, count in carried:
+        known = [i for i, other in enumerate(arrays) if other is array]
+        if not known:
+            arrays.append(array)
+        pieces.append((known[0] if known else len(arrays) - 1, kind, first, count))
+    n_in, n_out, n_arrays, n_pieces = len(args), len(outs), len(arrays), len(pieces)
+    seqs = arrays[0].shape[1] if arrays else 0
+
+    def whole(*refs):
+        ins, refs = refs[:n_in], refs[n_in:]
+        sources, refs = refs[:n_arrays], refs[n_arrays:]
+        results, refs = refs[:n_out], refs[n_out:]
+        targets, refs = refs[:n_pieces], refs[n_pieces:]
+        own, sems = refs[: len(scratch)], refs[len(scratch) :]
+        extra = [Carried(sources, pieces, targets, sems)] if collective is not None else []
+        body(*ins, *results, *own, *extra)
+
+    sems = [pltpu.SemaphoreType.DMA((n_pieces, seqs - 1))] * 2 if pieces else []
+    shapes = [jax.ShapeDtypeStruct(out[0], out[1]) for out in outs]
+    for at, _, _, count in pieces:
+        shapes.append(jax.ShapeDtypeStruct((seqs - 1, count, arrays[at].shape[3]), arrays[at].dtype))
+    results = pl.pallas_call(
+        whole,
         name=name,
-        out_shape=[jax.ShapeDtypeStruct(shape, kind) for shape, kind in outs],
-        in_specs=[VMEM] * len(args),
-        out_specs=[VMEM] * len(outs),
-        scratch_shapes=scratch,
+        out_shape=shapes,
+        in_specs=[arg[1] if isinstance(arg, tuple) else VMEM for arg in args] + [ANY] * n_arrays,
+        out_specs=[out[2] if len(out) > 2 else VMEM for out in outs] + [ANY] * n_pieces,
+        scratch_shapes=list(scratch) + sems,
         compiler_params=pltpu.CompilerParams(**params),
         cost_estimate=pl.CostEstimate(flops=flops, bytes_accessed=moved, transcendentals=0),
-    )(*args)
+    )(*[arg[0] if isinstance(arg, tuple) else arg for arg in args], *arrays)
+    return list(results[:n_out]), list(results[n_out:])
 
 
 def dma(count):
@@ -194,7 +341,8 @@
     micro, local_rows, width = incoming.shape[1:]
     rows = local_rows // sections
     tokens = micro * rows
-    own = tokens // heads
+    half_tokens = tokens // 2
+    step_rows = half_tokens // BLOCKS
     block_tok = segment_ids.shape[1]
     length = micro * block_tok
     slots = sections * seqs
@@ -207,51 +355,80 @@
     group = query_width // (kv_local * head_width)
     score_scale = head_width ** (-0.5)
     half_model = width // sections
-
-    local_order = (
-        jnp.arange(micro, dtype=jnp.int32)[:, None] * block_tok
-        + seq * local_rows
-        + section * rows
-        + jnp.arange(rows, dtype=jnp.int32)[None, :]
-    ).reshape(tokens)
+    share = width // (sections * seqs)
+
     segments = segment_ids.reshape(length)
-    padded = jnp.concatenate([jnp.full((2,), -1, jnp.int32), segments])
-    local_segments = segments[local_order]
-    same = jnp.stack(
-        [
-            (local_segments == padded[local_order + 1]).astype(FLOAT),
-            (local_segments == padded[local_order]).astype(FLOAT),
-        ],
-        1,
-    )
+
+    def own_tokens(per_token):
+        start = seq * local_rows + section * rows
+        return lax.dynamic_slice_in_dim(per_token.reshape(micro, block_tok), start, rows, 1).reshape(tokens)
+
+    def moved_back(by):
+        return jnp.concatenate([jnp.full((by,), -1, jnp.int32), segments[:-by]])
+
+    local_segments = own_tokens(segments)
+    same = jnp.stack([(local_segments == own_tokens(moved_back(by))).astype(FLOAT) for by in (1, 2)], 1)
     local_segments = local_segments[:, None]
-    angle_rates = THETA ** (-jnp.arange(0, head_width, 2).astype(FLOAT) / head_width)
+    pair_index = lax.broadcasted_iota(jnp.int32, (1, 2 * head_width), 1) % (head_width // 2)
+    angle_rates = THETA ** (-2.0 * pair_index.astype(FLOAT) / head_width)
     local_positions = lax.dynamic_slice_in_dim(positions, section * rows, rows, 1).reshape(tokens)
-    angles = local_positions.astype(FLOAT)[:, None] * angle_rates[None, :]
-    cosine = jnp.tile(jnp.cos(angles), (1, 4))
-    sine = jnp.tile(jnp.sin(angles), (1, 4))
+    angles = local_positions.astype(FLOAT)[:, None] * angle_rates
+    cosine, sine = jnp.cos(angles), jnp.sin(angles)
     query_gain = jnp.tile(qk_gains[0:1], (1, 2))
     key_gain = jnp.tile(qk_gains[1:2], (1, 2))
     w_in = conv_in.transpose(1, 0, 2)
     w_pair = w_keyval.reshape(width, pair_width)
-    first_up = conv_gate_up.transpose(1, 2, 0).reshape(2 * hidden_units, width)
-    second_up = attn_gate_up.transpose(1, 2, 0).reshape(2 * hidden_units, width)
+    first_up = conv_gate_up.transpose(1, 2, 0)
+    second_up = attn_gate_up.transpose(1, 2, 0)
+    slabs = [(start, min(512, hidden_units - start)) for start in range(0, hidden_units, 512)]
+    tile_width = 256
+    tiles = -(-hidden_units // tile_width)
+    padded_units = tiles * tile_width
 
     def shifted_rows(ext, micro_at, back):
         return ext[micro_at, 8 - back : 8 - back + rows, :]
 
+    def own_rows(flow, i):
+        return rows_of(flow * BLOCKS + i, step_rows)
+
+    def kept_rows(i):
+        return rows_of(i, step_rows)
+
+    total_scratch = [pltpu.VMEM((2, BLOCKS, step_rows, width), HALF)] + [
+        pltpu.SemaphoreType.DMA((2, BLOCKS)) for _ in range(4)
+    ]
+    part_scratch = [pltpu.VMEM((tokens, width), HALF)]
+
+    weight_scratch = [
+        pltpu.VMEM((2, hidden_units, width), HALF),
+        pltpu.VMEM((hidden_units, width), HALF),
+        dma(3 * len(slabs)),
+    ]
+
+    def weight_loads(up_hbm, down_hbm, up_ref, down_ref, sems):
+        copies = []
+        for j, (start, count) in enumerate(slabs):
+            span = slice(start, start + count)
+            pairs = [(up_hbm.at[0, span], up_ref.at[0, span]), (up_hbm.at[1, span], up_ref.at[1, span])]
+            pairs.append((down_hbm.at[span], down_ref.at[span]))
+            for k, (source, target) in enumerate(pairs):
+                copies.append(pltpu.make_async_copy(source, target, sems.at[3 * j + k]))
+        return copies
+
     def conv_forward(
-        in_ref, same_ref, gain_ref, win_ref, kernel_ref, wout_ref,
-        x_ref, g_ref, n1_ref, pc_ref, edge_ref, y_ref, h1_ref, n2_ref,
-        other, edges, normed_edges, ext, part, zslots,
-        swap_send, swap_recv, edge_send, edge_recv, zs, zr, gs, gr,
+        in_ref, same_ref, gain_ref, win_ref, kernel_ref, wout_ref, attn_gain_ref, up_hbm, down_hbm,
+        x_ref, g_ref, n1_ref, pc_ref, edge_ref, y_ref, h1_ref, n2_ref, f1_ref, a1_ref, m_ref, n3_ref,
+        other, edges, normed_edges, ext, swap_send, swap_recv, edge_send, edge_recv, up_ref, down_ref, weight_sems, acc,
+        part, inbox, rs, rr, gs, gr, inbox2, rs2, rr2, gs2, gr2, carry,
     ):
         where = place()
         s, q, h = where
         partner = (1 - s, q, h)
         following = (s, lax.rem(q + 1, seqs), h)
         preceding = (s, lax.rem(q + seqs - 1, seqs), h)
-        greet([partner, following, preceding] + head_peers(where, heads))
+        weights = weight_loads(up_hbm, down_hbm, up_ref, down_ref, weight_sems)
+        start_all(weights)
+        greet([partner, following, preceding], where, heads)
         give = pl.multiple_of((1 - s) * rows, rows)
         swap = remote(in_ref.at[0, :, pl.ds(give, rows)], other, swap_send.at[0], swap_recv.at[0], partner)
         swap.start()
@@ -296,16 +473,37 @@
             )
             y_ref[span, :] = (pc_ref[1, span, :] * mixed).astype(HALF)
         part[...] = product(y_ref[...], wout_ref[...]).astype(HALF)
-        copies = scatter_start(part, zslots, zs, zr, where, heads, own)
-        start = x_ref[rows_of(h, own), :].astype(FLOAT)
-        hidden = start + scatter_sum(copies, part, zslots, where, own)
-        h1_ref[...] = hidden
-        n2_ref[rows_of(h, own), :] = norm_apply(hidden, gain_ref[1:2, :]).astype(HALF)
-        wait_all(gather_start(n2_ref, gs, gr, where, heads, own))
-
-    zscratch = [pltpu.VMEM((heads - 1, own, width), HALF)]
-    zsems = [dma(heads - 1)] * 4
-    x, g, n1, projected, edge_gated, mixed, h1, n2 = call(
+
+        def finish(flow, i, total):
+            hidden = x_ref[own_rows(flow, i), :].astype(FLOAT) + total
+            h1_ref[kept_rows(i), :] = hidden
+            return norm_apply(hidden, gain_ref[1:2, :]).astype(HALF)
+
+        head_total(part, n2_ref, inbox, rs, rr, gs, gr, where, heads, finish)
+        for j, (start, count) in enumerate(slabs):
+            wait_all(weights[3 * j : 3 * j + 3])
+            span = slice(start, start + count)
+            gate = back_product(n2_ref[...], up_ref[0, span, :])
+            rise = back_product(n2_ref[...], up_ref[1, span, :])
+            f1_ref[0, :, span] = gate
+            f1_ref[1, :, span] = rise
+            active = (gate / (1.0 + jnp.exp(-gate)) * rise).astype(HALF)
+            a1_ref[:, span] = active
+            term = product(active, down_ref[span, :])
+            if j == 0:
+                acc[...] = term
+            else:
+                acc[...] += term
+        part[...] = acc[...].astype(HALF)
+
+        def finish_middle(flow, i, total):
+            middle = (h1_ref[kept_rows(i), :] + total).astype(HALF).astype(FLOAT)
+            m_ref[kept_rows(i), :] = middle
+            return norm_apply(middle, attn_gain_ref[0:1, :]).astype(HALF)
+
+        head_total(part, n3_ref, inbox2, rs2, rr2, gs2, gr2, where, heads, finish_middle)
+
+    (x, g, n1, projected, edge_gated, mixed, h1, n2, f1, a1, middle, n3), _ = call(
         conv_forward,
         "conv_forward",
         0,
@@ -316,7 +514,11 @@
             ((3, tokens, channels), FLOAT),
             ((micro, 8, channels), FLOAT),
             ((tokens, channels), HALF),
-            ((own, width), FLOAT),
+            ((half_tokens, width), FLOAT),
+            ((tokens, width), HALF),
+            ((2, tokens, hidden_units), FLOAT),
+            ((tokens, hidden_units), HALF),
+            ((half_tokens, width), FLOAT),
             ((tokens, width), HALF),
         ],
         [
@@ -324,52 +526,139 @@
             pltpu.VMEM((2, micro, 16, width), HALF),
             pltpu.VMEM((micro * 16, width), HALF),
             pltpu.VMEM((micro, 8 + rows, channels), FLOAT),
-            pltpu.VMEM((tokens, width), HALF),
+            dma(1),
+            dma(1),
+            dma(2),
+            dma(2),
         ]
-        + zscratch
-        + [dma(1), dma(1), dma(2), dma(2)]
-        + zsems,
-        [incoming, same, conv_gains, w_in, conv_kernel, conv_out],
-        flops=10**9,
-        moved=80 << 20,
+        + weight_scratch
+        + [pltpu.VMEM((tokens, width), FLOAT)]
+        + part_scratch
+        + total_scratch
+        + total_scratch,
+        [incoming, same, conv_gains, w_in, conv_kernel, conv_out, attn_gains, (first_up, ANY), (conv_down, ANY)],
+        flops=5 * 10**9,
+        moved=200 << 20,
     )
 
-    def ffn_forward(normed, up, down):
-        joined = back_product(normed, up)
-        active = swiglu(joined).astype(HALF)
-        return joined, active, product(active, down).astype(HALF)
-
-    def ffn_backward(grad_low, joined, up, down):
-        grad_active = back_product(grad_low, down)
-        grad_joined = jax.vjp(swiglu, joined)[1](grad_active)[0].astype(HALF)
-        return grad_joined, product(grad_joined, up).astype(HALF)
-
-    f1, a1, part = ffn_forward(n2, first_up, conv_down)
-
-    def enter_attention(part_ref, h1_ref, gain_ref, m_ref, n3_ref, zslots, zs, zr, gs, gr):
-        where = place()
-        greet(head_peers(where, heads))
-        copies = scatter_start(part_ref, zslots, zs, zr, where, heads, own)
-        middle = (h1_ref[...] + scatter_sum(copies, part_ref, zslots, where, own)).astype(HALF).astype(FLOAT)
-        m_ref[...] = middle
-        n3_ref[rows_of(where[2], own), :] = norm_apply(middle, gain_ref[0:1, :]).astype(HALF)
-        wait_all(gather_start(n3_ref, gs, gr, where, heads, own))
-
-    middle, n3 = call(
-        enter_attention,
-        "enter_attention",
-        1,
-        [((own, width), FLOAT), ((tokens, width), HALF)],
-        zscratch + zsems,
-        [part, h1, attn_gains],
-        moved=60 << 20,
-    )
+    swap_pairs = [(i, sections - 1 - i) for i in range(sections)]
+
+    def both_tokens(array):
+        return jnp.concatenate([array, lax.ppermute(array, "section", swap_pairs)], 0)
+
+    def half_of(array):
+        low, high = array[:, :half_model], array[:, half_model:]
+        kept = jnp.where(section == 0, low, high)
+        given = jnp.where(section == 0, high, low)
+        return jnp.concatenate([kept, lax.ppermute(given, "section", swap_pairs)], 0)
+
+    def weight_partial(former, latter):
+        return outer_sum(half_of(former), both_tokens(latter)).astype(HALF).reshape(1, seqs, share, -1)
+
+    def weight_total(piece, arrived):
+        partial_sums, kind, first, count = piece
+        total = lax.dynamic_index_in_dim(partial_sums[kind], seq, 0, False)[first : first + count].astype(FLOAT)
+        for k in range(seqs - 1):
+            total = total + arrived[k].astype(FLOAT)
+        return total
+
+    def transposed(array_ref, given_ref):
+        start = pl.multiple_of(lax.axis_index("section") * half_model, 128)
+        own = array_ref[:, pl.ds(start, half_model)]
+        both = jnp.concatenate([own, given_ref[...]], 0)
+        return both.astype(FLOAT).T.astype(HALF)
+
+    def half_swaps(arrays, targets, send, recv, where):
+        s, q, h = where
+        copies = []
+        for k, (array_ref, target) in enumerate(zip(arrays, targets)):
+            start = pl.multiple_of((1 - s) * half_model, 128)
+            copies.append(remote(array_ref.at[:, pl.ds(start, half_model)], target, send.at[k], recv.at[k], (1 - s, q, h)))
+        return copies
+
+    def latter_swap(latter, kind, start, count, send, recv, where):
+        s, q, h = where
+        return remote(
+            latter.at[kind, 0:tokens, start : start + count],
+            latter.at[kind, tokens : 2 * tokens, start : start + count],
+            send,
+            recv,
+            (1 - s, q, h),
+        )
+
+    def gradient_tiles(former, latter, stage, partial_hbm, first_in, local_sems, send, recv, where):
+        peers = seq_peers(where, seqs)
+
+        def split(t):
+            kind = lax.div(t, tiles)
+            at = lax.rem(t, tiles)
+            return kind, pl.ds(pl.multiple_of(at * tile_width, tile_width), tile_width)
+
+        def stored(t, dest):
+            kind, columns = split(t)
+            return pltpu.make_async_copy(
+                stage.at[kind, dest, :, columns], partial_hbm.at[kind, dest, :, columns], local_sems.at[t, dest]
+            )
+
+        def sent(t, k):
+            kind, columns = split(t)
+            return remote(
+                stage.at[kind, peers[k][1], :, columns], first_in.at[k, :, columns], send.at[t, k], recv.at[t, k], peers[k]
+            )
+
+        def tile(t):
+            kind, columns = split(t)
+            use = jnp.where(kind == 0, 0, 1)
+            result = product(former[use], latter[kind, :, columns]).astype(HALF)
+            stage[kind, :, :, columns] = result.reshape(seqs, share, tile_width)
+            for dest in range(seqs):
+                stored(t, dest).start()
+
+            @pl.when(kind == 0)
+            def _():
+                for k in range(seqs - 1):
+                    sent(t, k).start()
+
+        def finish():
+            def stored_all(t):
+                for dest in range(seqs):
+                    stored(t, dest).wait()
+
+            def sent_all(t):
+                for k in range(seqs - 1):
+                    sent(t, k).wait()
+
+            loop(3 * tiles, stored_all)
+            loop(tiles, sent_all)
+
+        return tile, finish
+
+    ffn_scratch = weight_scratch + [
+        pltpu.VMEM((tokens, width), FLOAT),
+        pltpu.VMEM((2, tokens, half_model), HALF),
+        pltpu.VMEM((2, half_model, 2 * tokens), HALF),
+        pltpu.VMEM((3, 2 * tokens, padded_units), HALF),
+        pltpu.VMEM((3, seqs, share, padded_units), HALF),
+        dma(2),
+        dma(2),
+        pltpu.SemaphoreType.DMA((3, len(slabs))),
+        pltpu.SemaphoreType.DMA((3, len(slabs))),
+        pltpu.SemaphoreType.DMA((3 * tiles, seqs)),
+        pltpu.SemaphoreType.DMA((tiles, seqs - 1)),
+        pltpu.SemaphoreType.DMA((tiles, seqs - 1)),
+    ]
+    partial_outs = [
+        ((3, seqs, share, padded_units), HALF, ANY),
+        ((seqs - 1, share, padded_units), HALF, ANY),
+    ]
 
     def slot_peer(me, j, h):
         other = lax.rem(me + j, slots)
         return (lax.rem(other, sections), lax.div(other, sections), h)
 
-    def query_key(n3_ref, wq_ref, wp_ref, cos_ref, sin_ref, qg_ref, kg_ref, qr_ref, r_ref, q_ref, all_ref, send, recv):
+    def query_key(
+        n3_ref, wq_ref, wp_ref, cos_ref, sin_ref, qg_ref, kg_ref, qr_ref, r_ref, q_ref, all_ref, send, recv, carry
+    ):
         s, q, h = place()
         me = q * sections + s
         peers = [slot_peer(me, j, h) for j in range(1, slots)]
@@ -392,7 +681,7 @@
             q_ref[:, span] = rotary(qr_ref[:, span], qg_ref[...], cos, sin).astype(HALF)
         wait_all(copies)
 
-    query_raw, pair_raw, queries, all_pairs = call(
+    (query_raw, pair_raw, queries, all_pairs), _ = call(
         query_key,
         "query_key",
         2,
@@ -456,7 +745,7 @@
                 results += [total[r * rows : (r + 1) * rows] for r in range(group)]
             o_ref[m * rows : (m + 1) * rows, :] = jnp.concatenate(results, -1).astype(HALF)
 
-    (attended,) = call(
+    (attended,), _ = call(
         attend,
         "attend",
         None,
@@ -467,64 +756,148 @@
         moved=30 << 20,
     )
 
-    def leave_attention(o_ref, wo_ref, m_ref, gain_ref, h2_ref, n4_ref, part, zslots, zs, zr, gs, gr):
+    def leave_attention(o_ref, wo_ref, m_ref, gain_ref, h2_ref, n4_ref, part, inbox, rs, rr, gs, gr, carry):
         where = place()
-        greet(head_peers(where, heads))
+        greet([], where, heads)
         part[...] = product(o_ref[...], wo_ref[...]).astype(HALF)
-        copies = scatter_start(part, zslots, zs, zr, where, heads, own)
-        hidden = m_ref[...] + scatter_sum(copies, part, zslots, where, own)
-        h2_ref[...] = hidden
-        n4_ref[rows_of(where[2], own), :] = norm_apply(hidden, gain_ref[1:2, :]).astype(HALF)
-        wait_all(gather_start(n4_ref, gs, gr, where, heads, own))
-
-    part_scratch = [pltpu.VMEM((tokens, width), HALF)]
-    h2, n4 = call(
+
+        def finish(flow, i, total):
+            hidden = m_ref[kept_rows(i), :] + total
+            h2_ref[kept_rows(i), :] = hidden
+            return norm_apply(hidden, gain_ref[1:2, :]).astype(HALF)
+
+        head_total(part, n4_ref, inbox, rs, rr, gs, gr, where, heads, finish)
+
+    (h2, n4), _ = call(
         leave_attention,
         "leave_attention",
         3,
-        [((own, width), FLOAT), ((tokens, width), HALF)],
-        part_scratch + zscratch + zsems,
+        [((half_tokens, width), FLOAT), ((tokens, width), HALF)],
+        part_scratch + total_scratch,
         [attended, attn_out, middle, attn_gains],
         moved=60 << 20,
     )
 
-    f2, a2, part_y = ffn_forward(n4, second_up, attn_down)
-    gf2, part_g = ffn_backward(g, f2, second_up, attn_down)
-
-    def turn_back(
-        py_ref, pg_ref, h2_ref, g_ref, gain_ref, yout_ref, gh2_ref, low_ref, gg_ref,
-        yslots, zslots, ys, yr, zs, zr, gs, gr, hs, hr,
+    def slab_width(start, count):
+        return min(-(-count // tile_width) * tile_width, padded_units - start)
+
+    def clear_padding(latter):
+        if padded_units > hidden_units:
+            latter[:, :, hidden_units:] = jnp.zeros((3, 2 * tokens, padded_units - hidden_units), HALF)
+
+    def second_ffn(
+        n4_ref, g_ref, h2_ref, gain_ref, up_hbm, down_hbm,
+        py_ref, gh2_ref, low_ref, gg_ref, partial_hbm, first_in,
+        acc_y, up_ref, down_ref, weight_sems, acc, given, former, latter, stage, hs, hr, ls, lr, local_sems, ts, tr,
+        part, inbox, rs, rr, gs, gr, carry,
     ):
         where = place()
-        mine = rows_of(where[2], own)
-        greet(head_peers(where, heads))
-        copies = scatter_start(pg_ref, zslots, zs, zr, where, heads, own)
-        later = scatter_start(py_ref, yslots, ys, yr, where, heads, own)
-        hidden = h2_ref[...]
-        grad_normed = scatter_sum(copies, pg_ref, zslots, where, own)
-        grad_hidden, grad_gain = norm_back(hidden, gain_ref[1:2, :], grad_normed)
-        grad = g_ref[mine, :].astype(FLOAT) + grad_hidden
-        gh2_ref[...] = grad
-        gg_ref[...] = grad_gain
-        low_ref[mine, :] = grad.astype(HALF)
-        gathers = gather_start(low_ref, gs, gr, where, heads, own)
-        yout_ref[mine, :] = (hidden + scatter_sum(later, py_ref, yslots, where, own)).astype(HALF)
-        gathers += gather_start(yout_ref, hs, hr, where, heads, own)
-        wait_all(gathers)
-
-    yout, gh2, gh2_low, grad_gain_attn1 = call(
-        turn_back,
-        "turn_back",
+        s, q, h = where
+        weights = weight_loads(up_hbm, down_hbm, up_ref, down_ref, weight_sems)
+        start_all(weights)
+        clear_padding(latter)
+        greet([(1 - s, q, h)] + seq_peers(where, seqs), where, heads)
+        halves = half_swaps([g_ref, n4_ref], [given.at[0], given.at[1]], hs, hr, where)
+        start_all(halves)
+        gg_ref[...] = jnp.zeros_like(gg_ref)
+        swaps = []
+        for j, (start, count) in enumerate(slabs):
+            wait_all(weights[3 * j : 3 * j + 3])
+            span = slice(start, start + count)
+            gate = back_product(n4_ref[...], up_ref[0, span, :])
+            rise = back_product(n4_ref[...], up_ref[1, span, :])
+            grad_active = back_product(g_ref[...], down_ref[span, :])
+            chance = 1.0 / (1.0 + jnp.exp(-gate))
+            silu = gate * chance
+            active = (silu * rise).astype(HALF)
+            grad_gate = (grad_active * rise * (chance * (1.0 + gate * (1.0 - chance)))).astype(HALF)
+            grad_rise = (grad_active * silu).astype(HALF)
+            latter[0, 0:tokens, span] = active
+            latter[1, 0:tokens, span] = grad_gate
+            latter[2, 0:tokens, span] = grad_rise
+            for kind in range(3):
+                swap = latter_swap(
+                    latter, kind, start, slab_width(start, count), ls.at[kind, j], lr.at[kind, j], where
+                )
+                swap.start()
+                swaps.append(swap)
+            term = product(grad_gate, up_ref[0, span, :]) + product(grad_rise, up_ref[1, span, :])
+            term_y = product(active, down_ref[span, :])
+            if j == 0:
+                acc[...] = term
+                acc_y[...] = term_y
+            else:
+                acc[...] += term
+                acc_y[...] += term_y
+        part[...] = acc[...].astype(HALF)
+
+        for flow, holder in ((0, 0), (1, heads - 1)):
+
+            @pl.when(h == holder)
+            def _(flow=flow):
+                acc_y[flow * half_tokens : (flow + 1) * half_tokens, :] += h2_ref[...]
+
+        py_ref[...] = acc_y[...].astype(HALF)
+        wait_all(halves)
+        former[0] = transposed(g_ref, given.at[0])
+        former[1] = transposed(n4_ref, given.at[1])
+        wait_all(swaps)
+        tile, tiles_done = gradient_tiles(
+            former, latter, stage, partial_hbm, first_in, local_sems, ts, tr, where
+        )
+
+        def finish(flow, i, total):
+            grad_hidden, grad_gain = norm_back(h2_ref[kept_rows(i), :], gain_ref[1:2, :], total)
+            grad = g_ref[own_rows(flow, i), :].astype(FLOAT) + grad_hidden
+            gh2_ref[kept_rows(i), :] = grad
+            gg_ref[...] += grad_gain
+            return grad.astype(HALF)
+
+        head_total(part, low_ref, inbox, rs, rr, gs, gr, where, heads, finish, tile, 3 * tiles)
+        tiles_done()
+
+    (part_y, gh2, gh2_low, grad_gain_attn1, partial2, down2_in), _ = call(
+        second_ffn,
+        "second_ffn",
         4,
-        [((tokens, width), HALF), ((own, width), FLOAT), ((tokens, width), HALF), ((1, width), FLOAT)],
-        zscratch * 2 + zsems * 2,
-        [part_y, part_g, h2, g, attn_gains],
-        moved=90 << 20,
+        [
+            ((tokens, width), HALF),
+            ((half_tokens, width), FLOAT),
+            ((tokens, width), HALF),
+            ((1, width), FLOAT),
+        ]
+        + partial_outs,
+        [pltpu.VMEM((tokens, width), FLOAT)] + ffn_scratch + part_scratch + total_scratch,
+        [n4, g, h2, attn_gains, (second_up, ANY), (attn_down, ANY)],
+        flops=12 * 10**9,
+        moved=150 << 20,
     )
-
-    def attend_back(low_ref, wo_ref, q_ref, all_ref, segq_ref, seg_ref, gq_ref, gp_ref, grads, totals):
-        s, q, _ = place()
-        grads[...] = back_product(low_ref[...], wo_ref[...]).astype(HALF)
+    yout = lax.psum(part_y, "head")
+    quarter = share // 4
+    up2_pieces = [
+        (partial2, 1, 0, 2 * quarter),
+        (partial2, 1, 2 * quarter, 2 * quarter),
+        (partial2, 2, 0, 2 * quarter),
+        (partial2, 2, 2 * quarter, 2 * quarter),
+    ]
+    out2 = weight_partial(gh2_low, attended)
+
+    def attention_backward(
+        glow_ref, wo_ref, q_ref, all_ref, segq_ref, seg_ref,
+        qr_ref, r_ref, cos_ref, sin_ref, qg_ref, kg_ref, wq_ref, wp_ref, m_ref, gh2_ref, gain_ref,
+        bq_ref, br_ref, low_ref, gg_ref, gqk_ref,
+        grads, totals, gq_ref, gp_ref, pair_slots, ps, pr,
+        part, inbox, rs, rr, gs, gr, carry,
+    ):
+        where = place()
+        s, q, h = where
+        me = q * sections + s
+        peers = [slot_peer(me, j, h) for j in range(1, slots)]
+        greet(peers, where, heads)
+        carry.start(where, seqs, [0])
+        gg_ref[...] = jnp.zeros_like(gg_ref)
+        gqk_ref[...] = jnp.zeros_like(gqk_ref)
+        grads[...] = back_product(glow_ref[...], wo_ref[...]).astype(HALF)
         for m in range(micro):
             biases = [allowed_pairs(segq_ref, seg_ref, m, at, s, q) for at in range(m + 1)]
             results = []
@@ -558,40 +931,14 @@
         for at in range(micro):
             joined = jnp.concatenate([totals[at, k] for k in range(2 * kv_local)], -1).astype(HALF)
             gp_ref[:, at * rows : (at + 1) * rows, :] = joined.reshape(slots, rows, pair_width)
-
-    grad_queries, grad_pairs = call(
-        attend_back,
-        "attend_back",
-        None,
-        [((tokens, query_width), FLOAT), ((slots, tokens, pair_width), HALF)],
-        [
-            pltpu.VMEM((tokens, query_width), HALF),
-            pltpu.VMEM((micro, 2 * kv_local, block_tok, head_width), FLOAT),
-        ],
-        [gh2_low, attn_out, queries, all_pairs, local_segments, segment_ids],
-        flops=5 * 10**9,
-        moved=50 << 20,
-    )
-
-    def back_through_entry(
-        gp_ref, gq_ref, qr_ref, r_ref, cos_ref, sin_ref, qg_ref, kg_ref, wq_ref, wp_ref, m_ref, gh2_ref, gain_ref,
-        bq_ref, br_ref, low_ref, gg_ref, gqk_ref,
-        pair_slots, part, zslots, ps, pr, zs, zr, gs, gr,
-    ):
-        where = place()
-        s, q, h = where
-        mine = rows_of(h, own)
-        me = q * sections + s
-        peers = [slot_peer(me, j, h) for j in range(1, slots)]
-        greet(peers + head_peers(where, heads))
         copies = []
         for j, peer in enumerate(peers):
             slot = peer[1] * sections + peer[0]
             copy = remote(gp_ref.at[slot], pair_slots.at[j], ps.at[j], pr.at[j], peer)
             copy.start()
             copies.append(copy)
+        carry.start(where, seqs, [1, 2])
         cos, sin = cos_ref[...], sin_ref[...]
-        gqk_ref[...] = jnp.zeros_like(gqk_ref)
         for start, size in chunks_of(query_width):
             span = slice(start, start + size)
             grad_raw, grad_gain = rotary_back(qr_ref[:, span], qg_ref[...], cos, sin, gq_ref[:, span])
@@ -610,16 +957,18 @@
             gqk_ref[1:2, :size] += grad_gain
         br_ref[:, half_pair:] = grad_pair[:, half_pair:].astype(HALF)
         part[...] = (partial + back_product(br_ref[...], wp_ref[...])).astype(HALF)
-        zcopies = scatter_start(part, zslots, zs, zr, where, heads, own)
-        grad_normed = scatter_sum(zcopies, part, zslots, where, own)
-        grad_entry, grad_gain = norm_back(m_ref[...], gain_ref[0:1, :], grad_normed)
-        gg_ref[...] = grad_gain
-        low_ref[mine, :] = (gh2_ref[...] + grad_entry).astype(HALF)
-        wait_all(gather_start(low_ref, gs, gr, where, heads, own))
-
-    bq, br, gm_low, grad_gain_attn0, grad_qk = call(
-        back_through_entry,
-        "back_through_entry",
+
+        def finish(flow, i, total):
+            grad_entry, grad_gain = norm_back(m_ref[kept_rows(i), :], gain_ref[0:1, :], total)
+            gg_ref[...] += grad_gain
+            return (gh2_ref[kept_rows(i), :] + grad_entry).astype(HALF)
+
+        head_total(part, low_ref, inbox, rs, rr, gs, gr, where, heads, finish)
+        carry.wait()
+
+    (bq, br, gm_low, grad_gain_attn0, grad_qk), up2_in = call(
+        attention_backward,
+        "attention_backward",
         5,
         [
             ((tokens, query_width), HALF),
@@ -628,58 +977,111 @@
             ((1, width), FLOAT),
             ((8, 128), FLOAT),
         ],
-        [pltpu.VMEM((slots - 1, tokens, pair_width), HALF)]
+        [
+            pltpu.VMEM((tokens, query_width), HALF),
+            pltpu.VMEM((micro, 2 * kv_local, block_tok, head_width), FLOAT),
+            pltpu.VMEM((tokens, query_width), FLOAT),
+            pltpu.VMEM((slots, tokens, pair_width), HALF),
+            pltpu.VMEM((slots - 1, tokens, pair_width), HALF),
+            dma(slots - 1),
+            dma(slots - 1),
+        ]
         + part_scratch
-        + zscratch
-        + [dma(slots - 1), dma(slots - 1)]
-        + zsems,
+        + total_scratch,
         [
-            grad_pairs, grad_queries, query_raw, pair_raw, cosine, sine, query_gain, key_gain,
-            w_query, w_pair, middle, gh2, attn_gains,
+            gh2_low, attn_out, queries, all_pairs, local_segments, segment_ids,
+            query_raw, pair_raw, cosine, sine, query_gain, key_gain, w_query, w_pair, middle, gh2, attn_gains,
         ],
-        flops=10**9,
-        moved=90 << 20,
+        up2_pieces[:3],
+        flops=6 * 10**9,
+        moved=130 << 20,
     )
 
-    gf1, part = ffn_backward(gm_low, f1, first_up, conv_down)
-
-    def back_through_ffn(part_ref, h1_ref, gm_ref, gain_ref, gh1_ref, low_ref, gg_ref, zslots, zs, zr, gs, gr):
+    def first_ffn_back(
+        gm_ref, n2_ref, f1_ref, a1_ref, h1_ref, gain_ref, up_hbm, down_hbm,
+        gh1_ref, low_ref, gg_ref, partial_hbm, first_in,
+        up_ref, down_ref, weight_sems, acc, given, former, latter, stage, hs, hr, ls, lr, local_sems, ts, tr,
+        part, inbox, rs, rr, gs, gr, carry,
+    ):
         where = place()
-        mine = rows_of(where[2], own)
-        greet(head_peers(where, heads))
-        copies = scatter_start(part_ref, zslots, zs, zr, where, heads, own)
-        grad_normed = scatter_sum(copies, part_ref, zslots, where, own)
-        grad_hidden, grad_gain = norm_back(h1_ref[...], gain_ref[1:2, :], grad_normed)
-        gg_ref[...] = grad_gain
-        grad = gm_ref[mine, :].astype(FLOAT) + grad_hidden
-        gh1_ref[...] = grad
-        low_ref[mine, :] = grad.astype(HALF)
-        wait_all(gather_start(low_ref, gs, gr, where, heads, own))
-
-    gh1, gh1_low, grad_gain_conv1 = call(
-        back_through_ffn,
-        "back_through_ffn",
+        s, q, h = where
+        weights = weight_loads(up_hbm, down_hbm, up_ref, down_ref, weight_sems)
+        start_all(weights)
+        clear_padding(latter)
+        latter[0, 0:tokens, 0:hidden_units] = a1_ref[...]
+        greet([(1 - s, q, h)] + seq_peers(where, seqs), where, heads)
+        halves = half_swaps([gm_ref, n2_ref], [given.at[0], given.at[1]], hs, hr, where)
+        start_all(halves)
+        gg_ref[...] = jnp.zeros_like(gg_ref)
+        swaps = []
+        for j, (start, count) in enumerate(slabs):
+            wait_all(weights[3 * j : 3 * j + 3])
+            span = slice(start, start + count)
+            gate = f1_ref[0, :, span]
+            rise = f1_ref[1, :, span]
+            grad_active = back_product(gm_ref[...], down_ref[span, :])
+            chance = 1.0 / (1.0 + jnp.exp(-gate))
+            grad_gate = (grad_active * rise * (chance * (1.0 + gate * (1.0 - chance)))).astype(HALF)
+            grad_rise = (grad_active * (gate * chance)).astype(HALF)
+            latter[1, 0:tokens, span] = grad_gate
+            latter[2, 0:tokens, span] = grad_rise
+            for kind in range(3):
+                swap = latter_swap(
+                    latter, kind, start, slab_width(start, count), ls.at[kind, j], lr.at[kind, j], where
+                )
+                swap.start()
+                swaps.append(swap)
+            term = product(grad_gate, up_ref[0, span, :]) + product(grad_rise, up_ref[1, span, :])
+            if j == 0:
+                acc[...] = term
+            else:
+                acc[...] += term
+        part[...] = acc[...].astype(HALF)
+        wait_all(halves)
+        former[0] = transposed(gm_ref, given.at[0])
+        former[1] = transposed(n2_ref, given.at[1])
+        wait_all(swaps)
+        tile, tiles_done = gradient_tiles(
+            former, latter, stage, partial_hbm, first_in, local_sems, ts, tr, where
+        )
+
+        def finish(flow, i, total):
+            grad_hidden, grad_gain = norm_back(h1_ref[kept_rows(i), :], gain_ref[1:2, :], total)
+            gg_ref[...] += grad_gain
+            grad = gm_ref[own_rows(flow, i), :].astype(FLOAT) + grad_hidden
+            gh1_ref[kept_rows(i), :] = grad
+            return grad.astype(HALF)
+
+        head_total(part, low_ref, inbox, rs, rr, gs, gr, where, heads, finish, tile, 3 * tiles)
+        tiles_done()
+
+    (gh1, gh1_low, grad_gain_conv1, partial1, down1_in), _ = call(
+        first_ffn_back,
+        "first_ffn_back",
         6,
-        [((own, width), FLOAT), ((tokens, width), HALF), ((1, width), FLOAT)],
-        zscratch + zsems,
-        [part, h1, gm_low, conv_gains],
-        moved=60 << 20,
+        [((half_tokens, width), FLOAT), ((tokens, width), HALF), ((1, width), FLOAT)] + partial_outs,
+        ffn_scratch + part_scratch + total_scratch,
+        [gm_low, n2, f1, a1, h1, conv_gains, (first_up, ANY), (conv_down, ANY)],
+        flops=9 * 10**9,
+        moved=150 << 20,
     )
+    mixers = weight_partial(n3, jnp.concatenate([bq, br], 1))
+    out2_piece, mixers_piece = (out2, 0, 0, share), (mixers, 0, 0, share)
 
     def conv_backward(
         low_ref, gh1_ref, pc_ref, edge_ref, same_ref, kernel_ref, wout_ref, win_ref, x_ref, gain_ref, yout_ref,
         bp_ref, gk_ref, gg_ref, edges_ref,
-        ext, spread, gz_ext, outgoing, arrived, full, part, zslots,
-        edge_send, edge_recv, swap_send, swap_recv, zs, zr, gs, gr,
+        ext, spread, gz_ext, outgoing, arrived, full, edge_send, edge_recv, swap_send, swap_recv,
+        part, inbox, rs, rr, gs, gr, carry,
     ):
         where = place()
         s, q, h = where
-        mine = rows_of(h, own)
         first = s == 0
         partner = (1 - s, q, h)
         preceding = (1 - s, jnp.where(first, lax.rem(q + seqs - 1, seqs), q), h)
         following = (1 - s, jnp.where(first, q, lax.rem(q + 1, seqs)), h)
-        greet([partner, preceding, following] + head_peers(where, heads))
+        greet([partner, preceding, following] + carry.peers(where, seqs), where, heads)
+        gg_ref[...] = jnp.zeros_like(gg_ref)
         gated = pc_ref[0] * pc_ref[2]
         grad_y = back_product(low_ref[...], wout_ref[...])
         gz = grad_y * pc_ref[1]
@@ -697,6 +1099,7 @@
             outgoing[m, 1:2, :] = one[0:1] + two[1:2]
         edge = remote(outgoing, arrived, edge_send.at[0], edge_recv.at[0], preceding)
         edge.start()
+        carry.start(where, seqs)
         taps = [None, None, None]
         for m in range(micro):
             span = slice(m * rows, (m + 1) * rows)
@@ -734,13 +1137,14 @@
         total = total + back_product(bp_ref[:, channels : 2 * channels], win_ref[1])
         total = total + back_product(bp_ref[:, 2 * channels :], win_ref[2])
         part[...] = total.astype(HALF)
-        copies = scatter_start(part, zslots, zs, zr, where, heads, own)
-        start = x_ref[mine, :].astype(FLOAT)
-        grad_normed = scatter_sum(copies, part, zslots, where, own)
-        grad_start, grad_gain = norm_back(start, gain_ref[0:1, :], grad_normed)
-        gg_ref[...] = grad_gain
-        full[mine, :] = (gh1_ref[...] + grad_start).astype(HALF)
-        wait_all(gather_start(full, gs, gr, where, heads, own))
+
+        def finish(flow, i, total):
+            start = x_ref[own_rows(flow, i), :].astype(FLOAT)
+            grad_start, grad_gain = norm_back(start, gain_ref[0:1, :], total)
+            gg_ref[...] += grad_gain
+            return (gh1_ref[kept_rows(i), :] + grad_start).astype(HALF)
+
+        head_total(part, full, inbox, rs, rr, gs, gr, where, heads, finish)
         keep = pl.ds(pl.multiple_of(s * rows, rows), rows)
         edges_ref[0, :, keep, :] = jnp.where(first, full[...], yout_ref[...]).reshape(micro, rows, width)
         part[...] = jnp.where(first, yout_ref[...], full[...])
@@ -752,8 +1156,9 @@
             copy.start()
             swaps.append(copy)
         wait_all(swaps)
-
-    bp, grad_taps, grad_gain_conv0, section_edges = call(
+        carry.wait()
+
+    (bp, grad_taps, grad_gain_conv0, section_edges), (up2_last_in, out2_in, mixers_in) = call(
         conv_backward,
         "conv_backward",
         7,
@@ -770,65 +1175,116 @@
             pltpu.VMEM((micro, 8, channels), FLOAT),
             pltpu.VMEM((micro, 8, channels), FLOAT),
             pltpu.VMEM((tokens, width), HALF),
-            pltpu.VMEM((tokens, width), HALF),
+            dma(1),
+            dma(1),
+            dma(micro),
+            dma(micro),
         ]
-        + zscratch
-        + [dma(1), dma(1), dma(micro), dma(micro)]
-        + zsems,
+        + part_scratch
+        + total_scratch,
         [gh1_low, gh1, projected, edge_gated, same, conv_kernel, conv_out, w_in, x, conv_gains, yout],
+        [up2_pieces[3], out2_piece, mixers_piece],
         flops=10**9,
-        moved=80 << 20,
+        moved=120 << 20,
     )
 
-    swap_pairs = [(i, sections - 1 - i) for i in range(sections)]
-
-    def both_tokens(array):
-        return jnp.concatenate([array, lax.ppermute(array, "section", swap_pairs)], 0)
-
-    def half_of(array):
-        low, high = array[:, :half_model], array[:, half_model:]
-        kept = jnp.where(section == 0, low, high)
-        given = jnp.where(section == 0, high, low)
-        return jnp.concatenate([kept, lax.ppermute(given, "section", swap_pairs)], 0)
-
-    def weight_grad(former_half, latter_all):
-        summed = outer_sum(former_half, latter_all).astype(HALF)
-        return lax.psum_scatter(summed, "seq", scatter_dimension=0, tiled=True).astype(FLOAT)
-
-    n4_half, g_half = half_of(n4), half_of(g)
-    grad_attn_down = weight_grad(g_half, both_tokens(a2)).T
-    grad_attn_up = weight_grad(n4_half, both_tokens(gf2)).reshape(-1, 2, hidden_units)
-    grad_attn_out = weight_grad(half_of(gh2_low), both_tokens(attended)).T
-    n3_half = half_of(n3)
-    grad_mixers = weight_grad(n3_half, both_tokens(jnp.concatenate([bq, br], 1)))
-    grad_query = grad_mixers[:, :query_width]
-    grad_keyval = grad_mixers[:, query_width:].reshape(-1, 2, pair_width // 2)
-    grad_conv_down = weight_grad(half_of(gm_low), both_tokens(a1)).T
-    grad_conv_up = weight_grad(half_of(n2), both_tokens(gf1)).reshape(-1, 2, hidden_units)
-    grad_conv_out = weight_grad(half_of(gh1_low), both_tokens(mixed)).T
-    grad_conv_in = weight_grad(half_of(n1), both_tokens(bp)).reshape(-1, 3, channels)
-
+    out1 = weight_partial(gh1_low, mixed)
+    in1 = weight_partial(n1, bp)
+    last_pieces = [(partial1, 1, 0, share), (partial1, 2, 0, share), (out1, 0, 0, share), (in1, 0, 0, share)]
     folded = grad_qk[0:2, :head_width] + grad_qk[0:2, head_width : 2 * head_width]
     gain_rows = jnp.concatenate([grad_gain_conv0, grad_gain_conv1, grad_gain_attn0, grad_gain_attn1], 0)
-    gain_rows, folded = lax.psum((gain_rows, folded), ("section", "seq", "head"))
-    grad_taps = lax.psum(grad_taps[0:3], ("section", "seq"))
-    share = width // (sections * seqs)
-    gain_share = lax.dynamic_slice_in_dim(gain_rows, (section * seqs + seq) * share, share, 1)
+    small_width = max(share, channels, 2 * head_width)
+
+    def to_width(array):
+        return jnp.pad(array, [(0, 0)] * (array.ndim - 1) + [(0, small_width - array.shape[-1])])
+
+    def to_all(array):
+        return jnp.broadcast_to(to_width(array), (slots,) + array.shape[:-1] + (small_width,))
+
+    small = jnp.concatenate(
+        [
+            to_width(gain_rows.reshape(4, slots, share).transpose(1, 0, 2)),
+            to_all(folded.reshape(1, 2 * head_width)),
+            to_all(grad_taps[0:3]),
+        ],
+        1,
+    )
+
+    def last_sums(small_ref, out_ref, boxes, summed, final, hs, hr, ss, sr, carry):
+        where = place()
+        s, q, h = where
+        others = [(s, q, lax.rem(h + k, heads)) for k in range(1, heads)]
+        me = q * sections + s
+        peers = [slot_peer(me, j, h) for j in range(1, slots)]
+        greet(others + peers)
+        copies = []
+        for k, peer in enumerate(others):
+            copy = remote(small_ref, boxes.at[k], hs.at[k], hr.at[k], peer)
+            copy.start()
+            copies.append(copy)
+        carry.start(where, seqs)
+        wait_all(copies)
+        over_heads = boxes[0]
+        for k in range(1, heads - 1):
+            over_heads = over_heads + boxes[k]
+        row = lax.broadcasted_iota(jnp.int32, over_heads.shape, 1)
+        summed[...] = small_ref[...] + jnp.where(row < 5, over_heads, 0.0)
+        copies = []
+        for j, peer in enumerate(peers):
+            copy = remote(summed.at[peer[0] * seqs + peer[1]], final.at[j], ss.at[j], sr.at[j], peer)
+            copy.start()
+            copies.append(copy)
+        total = summed[s * seqs + q]
+        wait_all(copies)
+        for j in range(slots - 1):
+            total = total + final[j]
+        out_ref[...] = total
+        carry.wait()
+
+    (sums,), (gate1_in, rise1_in, out1_in, in1_in) = call(
+        last_sums,
+        "last_sums",
+        8,
+        [((8, small_width), FLOAT)],
+        [
+            pltpu.VMEM((heads - 1, slots, 8, small_width), FLOAT),
+            pltpu.VMEM((slots, 8, small_width), FLOAT),
+            pltpu.VMEM((slots - 1, 8, small_width), FLOAT),
+            dma(heads - 1),
+            dma(heads - 1),
+            dma(slots - 1),
+            dma(slots - 1),
+        ],
+        [small],
+        last_pieces,
+        moved=150 << 20,
+    )
+
+    grad_mixers = weight_total(mixers_piece, mixers_in)
+    gate2, rise2 = [
+        jnp.concatenate([weight_total(p, a) for p, a in pairs], 0)[:, :hidden_units]
+        for pairs in (
+            list(zip(up2_pieces[:2], up2_in[:2])),
+            list(zip(up2_pieces[2:], [up2_in[2], up2_last_in])),
+        )
+    ]
+    gate1 = weight_total(last_pieces[0], gate1_in)[:, :hidden_units]
+    rise1 = weight_total(last_pieces[1], rise1_in)[:, :hidden_units]
     return (
         section_edges,
-        gain_share[0:2],
-        grad_conv_in,
-        grad_taps,
-        grad_conv_out,
-        grad_conv_up,
-        grad_conv_down,
-        gain_share[2:4],
-        grad_query,
-        grad_keyval,
-        folded,
-        grad_attn_out,
-        grad_attn_up,
-        grad_attn_down,
+        sums[0:2, :share],
+        weight_total(last_pieces[3], in1_in).reshape(-1, 3, channels),
+        sums[5:8, :channels],
+        weight_total(last_pieces[2], out1_in).T,
+        jnp.stack([gate1, rise1], 1),
+        weight_total((partial1, 0, 0, share), down1_in)[:, :hidden_units].T,
+        sums[2:4, :share],
+        grad_mixers[:, :query_width],
+        grad_mixers[:, query_width:].reshape(-1, 2, pair_width // 2),
+        sums[4, : 2 * head_width].reshape(2, head_width),
+        weight_total(out2_piece, out2_in).T,
+        jnp.stack([gate2, rise2], 1),
+        weight_total((partial2, 0, 0, share), down2_in)[:, :hidden_units].T,
     )
 
 

time: 769 us -> 561 us (0.73)
  waiting for transfers between devices: 171 us -> 0.04 us
  Pallas kernels: 392 us -> 455 us
  blocking collectives: 60.4 us -> 0 us
  matrix products: 62.1 us -> 11.8 us
    reduce_scatter x8 -> x0, waiting for transfers between devices: 155 us -> none  [weight_grad(): lax.psum_scatter(summed, 'seq', scatter_dimension=0, tiled=True)]
    pallas_call x10 -> x9, Pallas kernels: 392 us -> 455 us  [call(): pl.pallas_call(whole, name=name, out_shape=shapes, in_specs=[arg[1] if is...]
    psum x2 -> x0, blocking collectives: 60.4 us -> none  [the longest x1 44.2 us: per_device(): lax.psum((gain_rows, folded), ('section', 'seq', 'head'))]
    dot_general x8 -> x0, matrix products: 35.3 us -> none  [the longest x4 19.8 us: back_product(): lax.dot_general(former, latter, (((1,), (1,)), ((), ())), preferred_eleme...]
    unnamed x74 -> x79, local copies, waits for them, and re-layouts: 8.58 us -> 27.5 us
    dot_general x8 -> x4, matrix products: 26.8 us -> 11.8 us  [outer_sum(): lax.dot_general(former, latter, (((0,), (0,)), ((), ())), preferred_eleme...]
    slice x4 -> x8, local copies, waits for them, and re-layouts: 3.21 us -> 12.9 us  [the longest x2 8.84 us: weight_total(): partial_sums[kind]]
    reshape x4 -> x10, local copies, waits for them, and re-layouts: 11 us -> 2.04 us  [the longest x4 1.05 us: own_tokens(): lax.dynamic_slice_in_dim(per_token.reshape(micro, block_tok), start, rows...]
  transfers between devices with their start and end apart: 24 -> 9, of which waited for: 11 -> 0; matrix products, arithmetic and copies ran while one was open for 7% -> 10% of each run, Pallas kernels for 7% -> 51%
where the time goes in v2:
time: 561 us; the launch traced here: 555 us
  Pallas kernels  455 us (81%)
  local copies, waits for them, and re-layouts  46.5 us (8%)
  other arithmetic  23.8 us (4%)
  between operations  14.7 us (3%)
  matrix products  11.8 us (2%)
    pallas_call x9, Pallas kernels, call(): pl.pallas_call(whole, name=name, out_shape=shapes, in_specs=[arg[1] if is...  455 us
    unnamed x79, local copies, waits for them, and re-layouts  27.5 us
    dot_general x4, matrix products, outer_sum(): lax.dot_general(former, latter, (((0,), (0,)), ((), ())), preferred_eleme...  11.8 us
  transfers between devices with their start and end apart: 9, of which 0 were waited for; matrix products, arithmetic and copies ran while one was open for 10% of the time, Pallas kernels for 51%

profile of v2, /device:TPU:0, one launch (start us, length us, event | category | flops | bytes accessed | tf_op | source)
XLA Modules:
  0.0 554.8 jit_solution(4169098572714211061)
XLA Ops:
  10.1 80.7 %conv_forward.1 = (bf16[256,1536]{1,0:T(8,128)(2,1)}, bf16[256,1536]{1,0:T(8,128)(2,1)}, bf16[256,1536]{1,0:T(8,128)(2,1)}, f32[3,256,384]{2,1,0:T(8,128)}, f32[...) custom-call(bf16[1,4,128,1536]{3,2,1,0:T(8,128)(2,1)} %refs_0_.1, ...), custom_call_target="tpu_custom_call" | custom-call | flops 5000000000 | bytes 209715200 | tf_op jit(solution)/shard_map/conv_forward/pallas_call | solution.py:302
  90.9 2.1 broadcast_select_fusion.5
  97.8 17.4 %query_key.1 = (f32[256,384]{1,0:T(8,128)}, f32[256,256]{1,0:T(8,128)}, bf16[256,384]{1,0:T(8,128)(2,1)}, bf16[8,256,256]{2,1,0:T(8,128)(2,1)}) custom-call(bf16[256,1536]{1,0:T(8,128)(2,1)} %get-tuple-element.63.refs_0_, bf16[1536,384]{1,0:T(8,128)(2,1)} %refs_12_.1, bf16[1536,256]{1,0:T(8,128)(2,1)} %bitcast.156, ...), custom_call_target="tpu_custom_call" | custom-call | flops 500000000 | bytes 41943040 | tf_op jit(solution)/shard_map/query_key/pallas_call | solution.py:302
  115.2 7.2 %attend.1.refs_0_ = bf16[256,384]{1,0:T(8,128)(2,1)} custom-call(bf16[256,384]{1,0:T(8,128)(2,1)} %get-tuple-element.64.refs_0_.refs_2_, bf16[8,256,256]{2,1,0:T(8,128)(2,1)} %get-tuple-element.65.refs_1_.refs_3_, s32[256,1]{1,0:T(8,128)} %copy.44.refs_2_.refs_4_, s32[4,512]{1,0:T(4,128)} %refs_5_.7), custom_call_target="tpu_custom_call" | custom-call | flops 2000000000 | bytes 31457280 | tf_op jit(solution)/shard_map/attend/pallas_call | solution.py:302
  122.4 1.7 collective-permute-start.1
  124.2 30.8 %leave_attention.1 = (f32[128,1536]{1,0:T(8,128)}, bf16[256,1536]{1,0:T(8,128)(2,1)}) custom-call(bf16[256,384]{1,0:T(8,128)(2,1)} %attend.1.refs_0_, bf16[384,1536]{1,0:T(8,128)(2,1)} %refs_1_.5, f32[128,1536]{1,0:T(8,128)} %get-tuple-element.66.refs_2_.refs_14_, f32[2,1536]{1,0:T(2,128)} %refs_16_.1), custom_call_target="tpu_custom_call" | custom-call | bytes 62914560 | tf_op jit(solution)/shard_map/leave_attention/pallas_call | solution.py:302
  155.0 59.9 %second_ffn.1 = (bf16[256,1536]{1,0:T(8,128)(2,1)}, f32[128,1536]{1,0:T(8,128)}, bf16[256,1536]{1,0:T(8,128)(2,1)}, f32[1,1536]{1,0:T(1,128)}, bf16[3,4,192,1792...) custom-call(bf16[256,1536]{1,0:T(8,128)(2,1)} %get-tuple-element.67.refs_0_, ...), custom_call_target="tpu_custom_call" | custom-call | flops 12000000000 | bytes 157286400 | tf_op jit(solution)/shard_map/second_ffn/pallas_call | solution.py:302
  214.9 2.1 broadcast_select_fusion.7
  217.0 66.3 %attention_backward.1 = (bf16[256,384]{1,0:T(8,128)(2,1)}, bf16[256,256]{1,0:T(8,128)(2,1)}, bf16[256,1536]{1,0:T(8,128)(2,1)}, f32[1,1536]{1,0:T(1,128)}, f32[8...) custom-call(bf16[256,1536]{1,0:T(8,128)(2,1)} %get-tuple-element.70.ref, ...), custom_call_target="tpu_custom_call" | custom-call | flops 6000000000 | bytes 136314880 | tf_op jit(solution)/shard_map/attention_backward/pallas_call | solution.py:302
  283.3 57.0 %first_ffn_back.1 = (f32[128,1536]{1,0:T(8,128)}, bf16[256,1536]{1,0:T(8,128)(2,1)}, f32[1,1536]{1,0:T(1,128)}, bf16[3,4,192,1792]{3,2,1,0:T(8,128)(2,1)}, bf16[3,192,1792]{2,1,0:T(8,128)(2,1)}) custom-call(bf16[256,1536]{1,0:T(8,128)(2,1)} %get-tuple-element.75.refs_0_, bf16[256,1536]{1,0:T(8,128)(2,1)} %get-tuple-element.76.refs_1_, ...), custom_call_target="tpu_custom_call" | custom-call | flops 8999999488 | bytes 157286400 | tf_op jit(solution)/shard_map/first_ffn_back/pallas_call | solution.py:302
  340.3 2.1 broadcast_select_fusion.3
  342.3 5.4 fusion.39
  348.7 3.0 slice_bitcast_fusion.2
  351.7 3.5 slice_bitcast_fusion.5
  355.3 3.5 fusion.40
  371.0 2.7 convolution_convert_fusion.3
  373.7 2.5 convolution_convert_fusion.2
  376.3 2.9 convolution_convert_fusion.1
  379.2 42.9 %conv_backward.1 = (bf16[256,1152]{1,0:T(8,128)(2,1)}, f32[8,384]{1,0:T(8,128)}, f32[1,1536]{1,0:T(1,128)}, bf16[1,4,128,1536]{3,2,1,0:T(8,128)(2,1)}, bf16[3,96...) custom-call(bf16[256,1536]{1,0:T(8,128)(2,1)} %get-tuple-element.80.refs_0_, ...), custom_call_target="tpu_custom_call" | custom-call | flops 1000000000 | bytes 125829120 | tf_op jit(solution)/shard_map/conv_backward/pallas_call | solution.py:302
  422.2 2.0 convert_add_fusion.16
  427.4 3.7 copy.49
  434.4 3.6 convolution_convert_fusion
  438.0 92.8 %last_sums.1 = (f32[8,384]{1,0:T(8,128)}, bf16[3,192,1792]{2,1,0:T(8,128)(2,1)}, bf16[3,192,1792]{2,1,0:T(8,128)(2,1)}, bf16[3,192,384]{2,1,0:T(8,128)(2,1)}, bf16[3,192,1152]{2,1,0:T(8,128)(2,1)}) custom-call(f32[8,8,384]{2,1,0:T(8,128)} %fusion.30.refs_0_, bf16[3,4,192,1792]{3,2,1,0:T(8,128)(2,1)} %get-tuple-element.95.refs_1_, ...), custom_call_target="tpu_custom_call" | custom-call | bytes 157286400 | tf_op jit(solution)/shard_map/last_sums/pallas_call | solution.py:302
  541.3 3.7 copy.48
  (149 shorter events, 40.6 us)
Async XLA Ops:
  7.2 372.0 %all-reduce.5.cloned.1.call-start = ((), (), s32[]{:S(2)}) async-start(), calls=%async_computation | async-start | bytes 1572864 | tf_op jit(solution)/shard_map/psum | solution.py:875
  90.7 3.5 copy-start.29
  90.8 4.7 copy-start.27
  90.8 4.8 copy-start.12
  90.8 282.9 %collective-permute-start.5 = (bf16[256,384]{1,0:T(8,128)(2,1)}, bf16[256,384]{1,0:T(8,128)(2,1)}, u32[]{:S(2)}, u32[]{:S(2)}) collective-permute-start(bf16[256,384]{1,0:T(8,128)(2,1)} %get-tuple-element.96), channel_id=1, source_target_pairs={{0,16},{16,0},{1,17},{17,1},{2,18},{18,2},{3,19},{19,3},{4,20},{20... | collective-permute-start | bytes 589832 | tf_op jit(solution)/shard_map/ppermute | solution.py:547
  93.0 283.3 %collective-permute-start.2 = (bf16[256,768]{1,0:T(8,128)(2,1)}, bf16[256,768]{1,0:T(8,128)(2,1)}, u32[]{:S(2)}, u32[]{:S(2)}) collective-permute-start(bf16[256,768]{1,0:T(8,128)(2,1)} %get-tuple-element.181), channel_id=1, source_target_pairs={{0,16},{16,0},{1,17},{17,1},{2,18},{18,2},{3,19},{19,3},{4,20},{20... | collective-permute-start | bytes 1179656 | tf_op jit(solution)/shard_map/ppermute | solution.py:553
  122.4 247.8 %collective-permute-start.1 = (bf16[256,384]{1,0:T(8,128)(2,1)}, bf16[256,384]{1,0:T(8,128)(2,1)}, u32[]{:S(2)}, u32[]{:S(2)}) collective-permute-start(bf16[256,384]{1,0:T(8,128)(2,1)} %attend.1.refs_0_), channel_id=1, source_target_pairs={{0,16},{16,0},{1,17},{17,1},{2,18},{18,2},{3,19},{19,3},{4,20},{20... | collective-permute-start | bytes 589832 | tf_op jit(solution)/shard_map/ppermute | solution.py:547
  217.0 153.9 %collective-permute-start = (bf16[256,768]{1,0:T(8,128)(2,1)}, bf16[256,768]{1,0:T(8,128)(2,1)}, u32[]{:S(2)}, u32[]{:S(2)}) collective-permute-start(bf16[256,768]{1,0:T(8,128)(2,1)} %get-tuple-element.183), channel_id=1, source_target_pairs={{0,16},{16,0},{1,17},{17,1},{2,18},{18,2},{3,19},{19,3},{4,20},{20... | collective-permute-start | bytes 1179656 | tf_op jit(solution)/shard_map/ppermute | solution.py:553
  342.3 31.4 %collective-permute-start.4 = (bf16[256,768]{1,0:T(8,128)(2,1)}, bf16[256,768]{1,0:T(8,128)(2,1)}, u32[]{:S(2)}, u32[]{:S(2)}) collective-permute-start(bf16[256,768]{1,0:T(8,128)(2,1)} %get-tuple-element.179), channel_id=1, source_target_pairs={{0,16},{16,0},{1,17},{17,1},{2,18},{18,2},{3,19},{19,3},{4,20},{20... | collective-permute-start | bytes 1179656 | tf_op jit(solution)/shard_map/ppermute | solution.py:553
  342.3 5.4 copy-start.13
  348.7 6.6 %copy-start = (bf16[3,4,192,1792]{3,2,1,0:T(8,128)(2,1)S(1)}, bf16[3,4,192,1792]{3,2,1,0:T(8,128)(2,1)}, u32[]{:S(2)}) copy-start(bf16[3,4,192,1792]{3,2,1,0:T(8,128)(2,1)} %get-tuple-element.95.refs_1_) | copy-start | bytes 24772612
  367.4 3.3 copy-start.28
  370.2 6.1 %collective-permute-start.3 = (bf16[256,640]{1,0:T(8,128)(2,1)}, bf16[256,640]{1,0:T(8,128)(2,1)}, u32[]{:S(2)}, u32[]{:S(2)}) collective-permute-start(bf16[256,640]{1,0:T(8,128)(2,1)} %constant_dynamic-update-slice_fusion), channel_id=1, source_target_pairs={{0,16},{16,0},{1,17},{17,1},{2,18},{18,2},{3,19},{19,3},{4,20},{20... | collective-permute-start | bytes 983048 | tf_op jit(solution)/shard_map/ppermute | solution.py:547
  370.9 63.4 %collective-permute-start.6 = (bf16[256,768]{1,0:T(8,128)(2,1)}, bf16[256,768]{1,0:T(8,128)(2,1)}, u32[]{:S(2)}, u32[]{:S(2)}) collective-permute-start(bf16[256,768]{1,0:T(8,128)(2,1)} %get-tuple-element.177), channel_id=1, source_target_pairs={{0,16},{16,0},{1,17},{17,1},{2,18},{18,2},{3,19},{19,3},{4,20},{20... | collective-permute-start | bytes 1179656 | tf_op jit(solution)/shard_map/ppermute | solution.py:553
  371.0 2.7 copy-start.19
  371.0 2.7 copy-start.31
  373.7 2.6 copy-start.17
  422.2 12.2 %collective-permute-start.7 = (bf16[256,1152]{1,0:T(8,128)(2,1)}, bf16[256,1152]{1,0:T(8,128)(2,1)}, u32[]{:S(2)}, u32[]{:S(2)}) collective-permute-start(bf16[256,1152]{1,0:T(8,128)(2,1)} %get-tuple-element.98), channel_id=1, source_target_pairs={{0,16},{16,0},{1,17},{17,1},{2,18},{18,2},{3,19},{19,3},{4,20},{20... | collective-permute-start | bytes 1769480 | tf_op jit(solution)/shard_map/ppermute | solution.py:547
  427.4 3.7 copy-start.26
  427.4 5.3 copy-start.15
  431.0 3.3 copy-start.18
  431.1 3.3 copy-start.30
  541.3 3.7 copy-start.16
  541.3 5.4 copy-start.9
  (17 other events, 30.6 us)
Sparse Core Ops, SparseCore 0:
  215.0 42.0 all-reduce.4

commit v3 on v2

--- a/solution.py
+++ b/solution.py
@@ -218,11 +218,11 @@
         return seq_peers(where, seqs) if self.pieces else []
 
     def start(self, where, seqs, chosen=None):
-        for at, (array, kind, first, count) in enumerate(self.pieces):
+        for at, (array, kind, first, count, left, wide) in enumerate(self.pieces):
             if chosen is not None and at not in chosen:
                 continue
             for k, peer in enumerate(seq_peers(where, seqs)):
-                source = self.sources[array].at[kind, peer[1], first : first + count]
+                source = self.sources[array].at[kind, peer[1], first : first + count, left : left + wide]
                 copy = remote(source, self.targets[at].at[k], self.sems[0].at[at, k], self.sems[1].at[at, k], peer)
                 copy.start()
                 self.copies.append(copy)
@@ -278,11 +278,11 @@
         params.update(collective_id=collective, has_side_effects=True)
     arrays = []
     pieces = []
-    for array, kind, first, count in carried:
+    for array, kind, first, count, left, wide in carried:
         known = [i for i, other in enumerate(arrays) if other is array]
         if not known:
             arrays.append(array)
-        pieces.append((known[0] if known else len(arrays) - 1, kind, first, count))
+        pieces.append((known[0] if known else len(arrays) - 1, kind, first, count, left, wide))
     n_in, n_out, n_arrays, n_pieces = len(args), len(outs), len(arrays), len(pieces)
     seqs = arrays[0].shape[1] if arrays else 0
 
@@ -297,8 +297,8 @@
 
     sems = [pltpu.SemaphoreType.DMA((n_pieces, seqs - 1))] * 2 if pieces else []
     shapes = [jax.ShapeDtypeStruct(out[0], out[1]) for out in outs]
-    for at, _, _, count in pieces:
-        shapes.append(jax.ShapeDtypeStruct((seqs - 1, count, arrays[at].shape[3]), arrays[at].dtype))
+    for at, _, _, count, _, wide in pieces:
+        shapes.append(jax.ShapeDtypeStruct((seqs - 1, count, wide), arrays[at].dtype))
     results = pl.pallas_call(
         whole,
         name=name,
@@ -541,26 +541,6 @@
         moved=200 << 20,
     )
 
-    swap_pairs = [(i, sections - 1 - i) for i in range(sections)]
-
-    def both_tokens(array):
-        return jnp.concatenate([array, lax.ppermute(array, "section", swap_pairs)], 0)
-
-    def half_of(array):
-        low, high = array[:, :half_model], array[:, half_model:]
-        kept = jnp.where(section == 0, low, high)
-        given = jnp.where(section == 0, high, low)
-        return jnp.concatenate([kept, lax.ppermute(given, "section", swap_pairs)], 0)
-
-    def weight_partial(former, latter):
-        return outer_sum(half_of(former), both_tokens(latter)).astype(HALF).reshape(1, seqs, share, -1)
-
-    def weight_total(piece, arrived):
-        partial_sums, kind, first, count = piece
-        total = lax.dynamic_index_in_dim(partial_sums[kind], seq, 0, False)[first : first + count].astype(FLOAT)
-        for k in range(seqs - 1):
-            total = total + arrived[k].astype(FLOAT)
-        return total
 
     def transposed(array_ref, given_ref):
         start = pl.multiple_of(lax.axis_index("section") * half_model, 128)
@@ -586,7 +566,7 @@
             (1 - s, q, h),
         )
 
-    def gradient_tiles(former, latter, stage, partial_hbm, first_in, local_sems, send, recv, where):
+    def gradient_tiles(former, latter, stage, partial_hbm, first_in, local_sems, send, recv, where, at_once):
         peers = seq_peers(where, seqs)
 
         def split(t):
@@ -614,7 +594,7 @@
             for dest in range(seqs):
                 stored(t, dest).start()
 
-            @pl.when(kind == 0)
+            @pl.when(t < at_once)
             def _():
                 for k in range(seqs - 1):
                     sent(t, k).start()
@@ -629,7 +609,7 @@
                     sent(t, k).wait()
 
             loop(3 * tiles, stored_all)
-            loop(tiles, sent_all)
+            loop(at_once, sent_all)
 
         return tile, finish
 
@@ -647,55 +627,17 @@
         pltpu.SemaphoreType.DMA((tiles, seqs - 1)),
         pltpu.SemaphoreType.DMA((tiles, seqs - 1)),
     ]
-    partial_outs = [
-        ((3, seqs, share, padded_units), HALF, ANY),
-        ((seqs - 1, share, padded_units), HALF, ANY),
-    ]
+    few_tiles = (tiles + 1) // 2
+
+    def partial_outs(at_once):
+        return [
+            ((3, seqs, share, padded_units), HALF, ANY),
+            ((seqs - 1, share, at_once * tile_width), HALF, ANY),
+        ]
 
     def slot_peer(me, j, h):
         other = lax.rem(me + j, slots)
         return (lax.rem(other, sections), lax.div(other, sections), h)
-
-    def query_key(
-        n3_ref, wq_ref, wp_ref, cos_ref, sin_ref, qg_ref, kg_ref, qr_ref, r_ref, q_ref, all_ref, send, recv, carry
-    ):
-        s, q, h = place()
-        me = q * sections + s
-        peers = [slot_peer(me, j, h) for j in range(1, slots)]
-        greet(peers)
-        cos, sin = cos_ref[...], sin_ref[...]
-        r_ref[...] = product(n3_ref[...], wp_ref[...])
-        half_pair = pair_width // 2
-        for start, size in chunks_of(half_pair):
-            span = slice(start, start + size)
-            all_ref[me, :, span] = rotary(r_ref[:, span], kg_ref[...], cos, sin).astype(HALF)
-        all_ref[me, :, half_pair:] = r_ref[:, half_pair:].astype(HALF)
-        copies = []
-        for j, peer in enumerate(peers):
-            copy = remote(all_ref.at[me], all_ref.at[me], send.at[j], recv.at[j], peer)
-            copy.start()
-            copies.append(copy)
-        qr_ref[...] = product(n3_ref[...], wq_ref[...])
-        for start, size in chunks_of(query_width):
-            span = slice(start, start + size)
-            q_ref[:, span] = rotary(qr_ref[:, span], qg_ref[...], cos, sin).astype(HALF)
-        wait_all(copies)
-
-    (query_raw, pair_raw, queries, all_pairs), _ = call(
-        query_key,
-        "query_key",
-        2,
-        [
-            ((tokens, query_width), FLOAT),
-            ((tokens, pair_width), FLOAT),
-            ((tokens, query_width), HALF),
-            ((slots, tokens, pair_width), HALF),
-        ],
-        [dma(slots - 1), dma(slots - 1)],
-        [n3, w_query, w_pair, cosine, sine, query_gain, key_gain],
-        flops=5 * 10**8,
-        moved=40 << 20,
-    )
 
     def query_rows(ref, m, c):
         block = ref[m * rows : (m + 1) * rows, :]
@@ -730,8 +672,50 @@
         inverse = 1.0 / total
         return [part * inverse for part in raised]
 
-    def attend(q_ref, all_ref, segq_ref, seg_ref, o_ref):
-        s, q, _ = place()
+    def gather_pairs(all_ref, me, where, send, recv, near_send, near_recv):
+        s, q, h = where
+        partner = (1 - s, q, h)
+        far = []
+        for k, peer in enumerate(seq_peers(where, seqs)):
+            copy = remote(all_ref.at[me], all_ref.at[me], send.at[k], recv.at[k], peer)
+            copy.start()
+            far.append(copy)
+        near = [remote(all_ref.at[me], all_ref.at[me], near_send.at[0], near_recv.at[0], partner)]
+        near[0].start()
+
+        def pass_on():
+            for k in range(1, seqs):
+                far[k - 1].wait()
+                slot = lax.rem(q + seqs - k, seqs) * sections + s
+                copy = remote(all_ref.at[slot], all_ref.at[slot], near_send.at[k], near_recv.at[k], partner)
+                copy.start()
+                near.append(copy)
+            wait_all(near)
+
+        return pass_on
+
+    def attention_forward(
+        n3_ref, wq_ref, wp_ref, cos_ref, sin_ref, qg_ref, kg_ref, segq_ref, seg_ref, wo_ref, m_ref, gain_ref,
+        qr_ref, r_ref, q_ref, all_ref, o_ref, h2_ref, n4_ref,
+        send, recv, near_send, near_recv, part, inbox, rs, rr, gs, gr, carry,
+    ):
+        where = place()
+        s, q, h = where
+        me = q * sections + s
+        greet([(1 - s, q, h)] + seq_peers(where, seqs), where, heads)
+        cos, sin = cos_ref[...], sin_ref[...]
+        r_ref[...] = product(n3_ref[...], wp_ref[...])
+        half_pair = pair_width // 2
+        for start, size in chunks_of(half_pair):
+            span = slice(start, start + size)
+            all_ref[me, :, span] = rotary(r_ref[:, span], kg_ref[...], cos, sin).astype(HALF)
+        all_ref[me, :, half_pair:] = r_ref[:, half_pair:].astype(HALF)
+        pass_on = gather_pairs(all_ref, me, where, send, recv, near_send, near_recv)
+        qr_ref[...] = product(n3_ref[...], wq_ref[...])
+        for start, size in chunks_of(query_width):
+            span = slice(start, start + size)
+            q_ref[:, span] = rotary(qr_ref[:, span], qg_ref[...], cos, sin).astype(HALF)
+        pass_on()
         for m in range(micro):
             biases = [allowed_pairs(segq_ref, seg_ref, m, at, s, q) for at in range(m + 1)]
             results = []
@@ -744,21 +728,6 @@
                 )
                 results += [total[r * rows : (r + 1) * rows] for r in range(group)]
             o_ref[m * rows : (m + 1) * rows, :] = jnp.concatenate(results, -1).astype(HALF)
-
-    (attended,), _ = call(
-        attend,
-        "attend",
-        None,
-        [((tokens, query_width), HALF)],
-        [],
-        [queries, all_pairs, local_segments, segment_ids],
-        flops=2 * 10**9,
-        moved=30 << 20,
-    )
-
-    def leave_attention(o_ref, wo_ref, m_ref, gain_ref, h2_ref, n4_ref, part, inbox, rs, rr, gs, gr, carry):
-        where = place()
-        greet([], where, heads)
         part[...] = product(o_ref[...], wo_ref[...]).astype(HALF)
 
         def finish(flow, i, total):
@@ -768,14 +737,26 @@
 
         head_total(part, n4_ref, inbox, rs, rr, gs, gr, where, heads, finish)
 
-    (h2, n4), _ = call(
-        leave_attention,
-        "leave_attention",
-        3,
-        [((half_tokens, width), FLOAT), ((tokens, width), HALF)],
-        part_scratch + total_scratch,
-        [attended, attn_out, middle, attn_gains],
-        moved=60 << 20,
+    (query_raw, pair_raw, queries, all_pairs, attended, h2, n4), _ = call(
+        attention_forward,
+        "attention_forward",
+        2,
+        [
+            ((tokens, query_width), FLOAT),
+            ((tokens, pair_width), FLOAT),
+            ((tokens, query_width), HALF),
+            ((slots, tokens, pair_width), HALF),
+            ((tokens, query_width), HALF),
+            ((half_tokens, width), FLOAT),
+            ((tokens, width), HALF),
+        ],
+        [dma(seqs - 1), dma(seqs - 1), dma(seqs), dma(seqs)] + part_scratch + total_scratch,
+        [
+            n3, w_query, w_pair, cosine, sine, query_gain, key_gain, local_segments, segment_ids,
+            attn_out, middle, attn_gains,
+        ],
+        flops=4 * 10**9,
+        moved=150 << 20,
     )
 
     def slab_width(start, count):
@@ -843,7 +824,7 @@
         former[1] = transposed(n4_ref, given.at[1])
         wait_all(swaps)
         tile, tiles_done = gradient_tiles(
-            former, latter, stage, partial_hbm, first_in, local_sems, ts, tr, where
+            former, latter, stage, partial_hbm, first_in, local_sems, ts, tr, where, few_tiles
         )
 
         def finish(flow, i, total):
@@ -866,34 +847,32 @@
             ((tokens, width), HALF),
             ((1, width), FLOAT),
         ]
-        + partial_outs,
+        + partial_outs(few_tiles),
         [pltpu.VMEM((tokens, width), FLOAT)] + ffn_scratch + part_scratch + total_scratch,
         [n4, g, h2, attn_gains, (second_up, ANY), (attn_down, ANY)],
         flops=12 * 10**9,
         moved=150 << 20,
     )
     yout = lax.psum(part_y, "head")
-    quarter = share // 4
+    half_share = share // 2
+    few_wide = few_tiles * tile_width
     up2_pieces = [
-        (partial2, 1, 0, 2 * quarter),
-        (partial2, 1, 2 * quarter, 2 * quarter),
-        (partial2, 2, 0, 2 * quarter),
-        (partial2, 2, 2 * quarter, 2 * quarter),
+        (partial2, kind, first, half_share, 0, padded_units) for kind in (1, 2) for first in (0, half_share)
     ]
-    out2 = weight_partial(gh2_low, attended)
+    down2_piece = (partial2, 0, 0, share, few_wide, padded_units - few_wide)
 
     def attention_backward(
         glow_ref, wo_ref, q_ref, all_ref, segq_ref, seg_ref,
         qr_ref, r_ref, cos_ref, sin_ref, qg_ref, kg_ref, wq_ref, wp_ref, m_ref, gh2_ref, gain_ref,
         bq_ref, br_ref, low_ref, gg_ref, gqk_ref,
-        grads, totals, gq_ref, gp_ref, pair_slots, ps, pr,
+        grads, totals, gq_ref, gp_ref, near_slots, pair_slots, ns, nr, ps, pr,
         part, inbox, rs, rr, gs, gr, carry,
     ):
         where = place()
         s, q, h = where
-        me = q * sections + s
-        peers = [slot_peer(me, j, h) for j in range(1, slots)]
-        greet(peers, where, heads)
+        partner = (1 - s, q, h)
+        peers = seq_peers(where, seqs)
+        greet([partner] + peers, where, heads)
         carry.start(where, seqs, [0])
         gg_ref[...] = jnp.zeros_like(gg_ref)
         gqk_ref[...] = jnp.zeros_like(gqk_ref)
@@ -931,14 +910,22 @@
         for at in range(micro):
             joined = jnp.concatenate([totals[at, k] for k in range(2 * kv_local)], -1).astype(HALF)
             gp_ref[:, at * rows : (at + 1) * rows, :] = joined.reshape(slots, rows, pair_width)
+        near = []
+        for other in range(seqs):
+            copy = remote(gp_ref.at[other * sections + 1 - s], near_slots.at[other], ns.at[other], nr.at[other], partner)
+            copy.start()
+            near.append(copy)
+        cos, sin = cos_ref[...], sin_ref[...]
         copies = []
-        for j, peer in enumerate(peers):
-            slot = peer[1] * sections + peer[0]
-            copy = remote(gp_ref.at[slot], pair_slots.at[j], ps.at[j], pr.at[j], peer)
+        wait_all(near)
+        for other in range(seqs):
+            mine = gp_ref[other * sections + s].astype(FLOAT)
+            near_slots[other] = (mine + near_slots[other].astype(FLOAT)).astype(HALF)
+        for k, peer in enumerate(peers):
+            copy = remote(near_slots.at[peer[1]], pair_slots.at[k], ps.at[k], pr.at[k], peer)
             copy.start()
             copies.append(copy)
-        carry.start(where, seqs, [1, 2])
-        cos, sin = cos_ref[...], sin_ref[...]
+        carry.start(where, seqs, [1, 2, 3])
         for start, size in chunks_of(query_width):
             span = slice(start, start + size)
             grad_raw, grad_gain = rotary_back(qr_ref[:, span], qg_ref[...], cos, sin, gq_ref[:, span])
@@ -946,8 +933,8 @@
             gqk_ref[0:1, :size] += grad_gain
         partial = back_product(bq_ref[...], wq_ref[...])
         wait_all(copies)
-        grad_pair = gp_ref[me].astype(FLOAT)
-        for j in range(slots - 1):
+        grad_pair = near_slots[q].astype(FLOAT)
+        for j in range(seqs - 1):
             grad_pair = grad_pair + pair_slots[j].astype(FLOAT)
         half_pair = pair_width // 2
         for start, size in chunks_of(half_pair):
@@ -982,9 +969,12 @@
             pltpu.VMEM((micro, 2 * kv_local, block_tok, head_width), FLOAT),
             pltpu.VMEM((tokens, query_width), FLOAT),
             pltpu.VMEM((slots, tokens, pair_width), HALF),
-            pltpu.VMEM((slots - 1, tokens, pair_width), HALF),
-            dma(slots - 1),
-            dma(slots - 1),
+            pltpu.VMEM((seqs, tokens, pair_width), HALF),
+            pltpu.VMEM((seqs - 1, tokens, pair_width), HALF),
+            dma(seqs),
+            dma(seqs),
+            dma(seqs - 1),
+            dma(seqs - 1),
         ]
         + part_scratch
         + total_scratch,
@@ -992,7 +982,7 @@
             gh2_low, attn_out, queries, all_pairs, local_segments, segment_ids,
             query_raw, pair_raw, cosine, sine, query_gain, key_gain, w_query, w_pair, middle, gh2, attn_gains,
         ],
-        up2_pieces[:3],
+        up2_pieces[:3] + [down2_piece],
         flops=6 * 10**9,
         moved=130 << 20,
     )
@@ -1010,6 +1000,7 @@
         clear_padding(latter)
         latter[0, 0:tokens, 0:hidden_units] = a1_ref[...]
         greet([(1 - s, q, h)] + seq_peers(where, seqs), where, heads)
+        carry.start(where, seqs)
         halves = half_swaps([gm_ref, n2_ref], [given.at[0], given.at[1]], hs, hr, where)
         start_all(halves)
         gg_ref[...] = jnp.zeros_like(gg_ref)
@@ -1042,7 +1033,7 @@
         former[1] = transposed(n2_ref, given.at[1])
         wait_all(swaps)
         tile, tiles_done = gradient_tiles(
-            former, latter, stage, partial_hbm, first_in, local_sems, ts, tr, where
+            former, latter, stage, partial_hbm, first_in, local_sems, ts, tr, where, tiles
         )
 
         def finish(flow, i, total):
@@ -1054,24 +1045,32 @@
 
         head_total(part, low_ref, inbox, rs, rr, gs, gr, where, heads, finish, tile, 3 * tiles)
         tiles_done()
-
-    (gh1, gh1_low, grad_gain_conv1, partial1, down1_in), _ = call(
+        carry.wait()
+
+    (gh1, gh1_low, grad_gain_conv1, partial1, down1_in), up2_last_in = call(
         first_ffn_back,
         "first_ffn_back",
         6,
-        [((half_tokens, width), FLOAT), ((tokens, width), HALF), ((1, width), FLOAT)] + partial_outs,
+        [((half_tokens, width), FLOAT), ((tokens, width), HALF), ((1, width), FLOAT)] + partial_outs(tiles),
         ffn_scratch + part_scratch + total_scratch,
         [gm_low, n2, f1, a1, h1, conv_gains, (first_up, ANY), (conv_down, ANY)],
+        up2_pieces[3:],
         flops=9 * 10**9,
         moved=150 << 20,
     )
-    mixers = weight_partial(n3, jnp.concatenate([bq, br], 1))
-    out2_piece, mixers_piece = (out2, 0, 0, share), (mixers, 0, 0, share)
+    small_width = max(share, channels, 2 * head_width)
+    widths = [query_width, query_width + pair_width, channels, 3 * channels]
 
     def conv_backward(
         low_ref, gh1_ref, pc_ref, edge_ref, same_ref, kernel_ref, wout_ref, win_ref, x_ref, gain_ref, yout_ref,
-        bp_ref, gk_ref, gg_ref, edges_ref,
-        ext, spread, gz_ext, outgoing, arrived, full, edge_send, edge_recv, swap_send, swap_recv,
+        ghlow_ref, n3_ref, n1_ref, o_ref, bq_ref, br_ref, mixed_ref, small_in,
+        partial1, partial2, down1_in, down2_a, gate2_a, gate2_b, rise2_a, down2_b, rise2_b,
+        edges_ref, sums_ref, gout2_ref, gmix_ref, gout1_ref, gin_ref, gdown2, gup2, gdown1, gup1,
+        bp_ref, ext, spread, gz_ext, outgoing, arrived, full, gg_ref, edge_send, edge_recv, swap_send, swap_recv,
+        given, former, latter0, latter1, latter2, latter3, stage0, stage1, stage2, stage3, in0, in1, in2, in3,
+        hs, hr, ls, lr, ms, mr, bulk_in, bulk_own, bs, br_sem, own_sem,
+        bufs, buf_sems, down_stage, up_stage, out_sems,
+        packed, boxes, summed, final, zs, zr, ss, sr,
         part, inbox, rs, rr, gs, gr, carry,
     ):
         where = place()
@@ -1080,7 +1079,45 @@
         partner = (1 - s, q, h)
         preceding = (1 - s, jnp.where(first, lax.rem(q + seqs - 1, seqs), q), h)
         following = (1 - s, jnp.where(first, q, lax.rem(q + 1, seqs)), h)
-        greet([partner, preceding, following] + carry.peers(where, seqs), where, heads)
+        others = [(s, q, lax.rem(h + k, heads)) for k in range(1, heads)]
+        me = q * sections + s
+        slot_peers = [slot_peer(me, j, h) for j in range(1, slots)]
+        peers = seq_peers(where, seqs)
+        latters, stages, incomes = [latter0, latter1, latter2, latter3], [stage0, stage1, stage2, stage3], [in0, in1, in2, in3]
+        own_bulk = [pltpu.make_async_copy(partial1.at[kind + 1, q], bulk_own.at[kind], own_sem.at[kind]) for kind in range(2)]
+        start_all(own_bulk)
+
+        def load(slot, own, pieces):
+            copies = [pltpu.make_async_copy(own, bufs.at[slot, 0], buf_sems.at[slot, 0])]
+            for k, (piece, start, count, left, wide) in enumerate(pieces):
+                target = bufs.at[slot, 1:seqs, start : start + count, left : left + wide]
+                copies.append(pltpu.make_async_copy(piece, target, buf_sems.at[slot, 1 + k]))
+            start_all(copies)
+            return copies
+
+        halves_of = ((0, half_share, 0, padded_units), (half_share, half_share, 0, padded_units))
+        loads = [
+            load(
+                0,
+                partial2.at[0, q],
+                [(down2_a, 0, share, 0, few_wide), (down2_b, 0, share, few_wide, padded_units - few_wide)],
+            ),
+            load(1, partial2.at[1, q], [(gate2_a, *halves_of[0]), (gate2_b, *halves_of[1])]),
+            load(2, partial2.at[2, q], [(rise2_a, *halves_of[0]), (rise2_b, *halves_of[1])]),
+            load(3, partial1.at[0, q], [(down1_in, 0, share, 0, padded_units)]),
+        ]
+        greet([partner, preceding, following] + others + slot_peers, where, heads)
+        latters[0][0:tokens, :] = o_ref[...]
+        latters[1][0:tokens, 0:query_width] = bq_ref[...]
+        latters[1][0:tokens, query_width:] = br_ref[...]
+        latters[2][0:tokens, :] = mixed_ref[...]
+        former_refs = [ghlow_ref, n3_ref, low_ref, n1_ref]
+        halves = half_swaps(former_refs, [given.at[k] for k in range(4)], hs, hr, where)
+        start_all(halves)
+        swaps = [
+            remote(latters[k].at[0:tokens], latters[k].at[tokens : 2 * tokens], ls.at[k], lr.at[k], partner) for k in range(4)
+        ]
+        start_all(swaps[:3])
         gg_ref[...] = jnp.zeros_like(gg_ref)
         gated = pc_ref[0] * pc_ref[2]
         grad_y = back_product(low_ref[...], wout_ref[...])
@@ -1099,7 +1136,13 @@
             outgoing[m, 1:2, :] = one[0:1] + two[1:2]
         edge = remote(outgoing, arrived, edge_send.at[0], edge_recv.at[0], preceding)
         edge.start()
-        carry.start(where, seqs)
+        bulk = []
+        for kind in range(2):
+            for k, peer in enumerate(peers):
+                bulk.append(
+                    remote(partial1.at[kind + 1, peer[1]], bulk_in.at[kind, k], bs.at[kind, k], br_sem.at[kind, k], peer)
+                )
+        start_all(bulk)
         taps = [None, None, None]
         for m in range(micro):
             span = slice(m * rows, (m + 1) * rows)
@@ -1116,7 +1159,6 @@
             for k, value in enumerate((back_two, back_one, gated[span])):
                 term = jnp.sum(value * gz[span], 0, keepdims=True)
                 taps[k] = term if taps[k] is None else taps[k] + term
-        gk_ref[...] = jnp.concatenate(taps + [jnp.zeros((5, channels), FLOAT)], 0)
         for m in range(micro):
             span = slice(m * rows, (m + 1) * rows)
             spread[m] = (
@@ -1133,6 +1175,8 @@
             span = slice(m * rows, (m + 1) * rows)
             bp_ref[span, 0:channels] = (spread[m] * pc_ref[2, span, :]).astype(HALF)
             bp_ref[span, 2 * channels :] = (spread[m] * pc_ref[0, span, :]).astype(HALF)
+        latters[3][0:tokens, :] = bp_ref[...]
+        swaps[3].start()
         total = back_product(bp_ref[:, 0:channels], win_ref[0])
         total = total + back_product(bp_ref[:, channels : 2 * channels], win_ref[1])
         total = total + back_product(bp_ref[:, 2 * channels :], win_ref[2])
@@ -1148,105 +1192,166 @@
         keep = pl.ds(pl.multiple_of(s * rows, rows), rows)
         edges_ref[0, :, keep, :] = jnp.where(first, full[...], yout_ref[...]).reshape(micro, rows, width)
         part[...] = jnp.where(first, yout_ref[...], full[...])
-        swaps = []
+        edge_swaps = []
         for m in range(micro):
             copy = remote(
                 part.at[m * rows : (m + 1) * rows], edges_ref.at[0, m, keep], swap_send.at[m], swap_recv.at[m], partner
             )
             copy.start()
-            swaps.append(copy)
-        wait_all(swaps)
-        carry.wait()
-
-    (bp, grad_taps, grad_gain_conv0, section_edges), (up2_last_in, out2_in, mixers_in) = call(
+            edge_swaps.append(copy)
+        packed[...] = small_in[...]
+        packed[:, 5:8, 0:channels] = jnp.broadcast_to(jnp.concatenate(taps, 0)[None], (slots, 3, channels))
+        for d in range(slots):
+            packed[d, 0:1, 0:share] = gg_ref[:, d * share : (d + 1) * share]
+        over = []
+        for k, peer in enumerate(others):
+            copy = remote(packed, boxes.at[k], zs.at[k], zr.at[k], peer)
+            copy.start()
+            over.append(copy)
+        wait_all(halves)
+        sends = []
+        for k in range(4):
+            former[...] = transposed(former_refs[k], given.at[k])
+            swaps[k].wait()
+            result = product(former[...], latters[k][...]).astype(HALF)
+            stages[k][...] = result.reshape(seqs, share, widths[k])
+            for j, peer in enumerate(peers):
+                copy = remote(stages[k].at[peer[1]], incomes[k].at[j], ms.at[k, j], mr.at[k, j], peer)
+                copy.start()
+                sends.append(copy)
+            if k == 0:
+                wait_all(over)
+                over_heads = boxes[0]
+                for j in range(1, heads - 1):
+                    over_heads = over_heads + boxes[j]
+                row = lax.broadcasted_iota(jnp.int32, over_heads.shape, 1)
+                summed[...] = packed[...] + jnp.where(row < 5, over_heads, 0.0)
+                across = []
+                for j, peer in enumerate(slot_peers):
+                    copy = remote(summed.at[peer[0] * seqs + peer[1]], final.at[j], ss.at[j], sr.at[j], peer)
+                    copy.start()
+                    across.append(copy)
+
+        def summed_up(own, arrivals):
+            total = own.astype(FLOAT)
+            for piece in arrivals:
+                total = total + piece.astype(FLOAT)
+            return total[:, :hidden_units]
+
+        outs = []
+
+        def leave(source, target, at):
+            copy = pltpu.make_async_copy(source, target, out_sems.at[at])
+            copy.start()
+            outs.append(copy)
+
+        def from_buffer(slot):
+            wait_all(loads[slot])
+            return summed_up(bufs[slot, 0], [bufs[slot, k] for k in range(1, seqs)])
+
+        down_stage[0] = from_buffer(0).astype(HALF)
+        leave(down_stage.at[0], gdown2, 0)
+        up_stage[0, 0] = from_buffer(1).astype(HALF)
+        up_stage[0, 1] = from_buffer(2).astype(HALF)
+        leave(up_stage.at[0], gup2, 1)
+        down_stage[1] = from_buffer(3).astype(HALF)
+        leave(down_stage.at[1], gdown1, 2)
+        wait_all(own_bulk)
+        for kind in range(2):
+            wait_all(bulk[kind * (seqs - 1) : (kind + 1) * (seqs - 1)])
+            up_stage[1, kind] = summed_up(bulk_own[kind], [bulk_in[kind, k] for k in range(seqs - 1)]).astype(HALF)
+        leave(up_stage.at[1], gup1, 3)
+        wait_all(edge_swaps)
+        wait_all(across)
+        total = summed[s * seqs + q]
+        for j in range(slots - 1):
+            total = total + final[j]
+        sums_ref[...] = total
+        wait_all(sends)
+        for k, target in enumerate((gout2_ref, gmix_ref, gout1_ref, None)):
+            total = stages[k][q].astype(FLOAT)
+            for j in range(seqs - 1):
+                total = total + incomes[k][j].astype(FLOAT)
+            if target is None:
+                for c in range(3):
+                    gin_ref[c] = total[:, c * channels : (c + 1) * channels].astype(HALF)
+            else:
+                target[...] = total.astype(HALF)
+        wait_all(outs)
+
+    folded = grad_qk[0:2, :head_width] + grad_qk[0:2, head_width : 2 * head_width]
+    gain_rows = jnp.concatenate(
+        [jnp.zeros_like(grad_gain_conv1), grad_gain_conv1, grad_gain_attn0, grad_gain_attn1], 0
+    )
+
+    def to_width(array):
+        return jnp.pad(array, [(0, 0)] * (array.ndim - 1) + [(0, small_width - array.shape[-1])])
+
+    small = jnp.concatenate(
+        [
+            to_width(gain_rows.reshape(4, slots, share).transpose(1, 0, 2)),
+            jnp.broadcast_to(to_width(folded.reshape(1, 1, 2 * head_width)), (slots, 1, small_width)),
+            jnp.zeros((slots, 3, small_width), FLOAT),
+        ],
+        1,
+    )
+
+    def dma_grid(*shape):
+        return pltpu.SemaphoreType.DMA(shape)
+
+    (section_edges, sums, gout2, gmix, gout1, gin, gdown2, gup2, gdown1, gup1), _ = call(
         conv_backward,
         "conv_backward",
         7,
         [
-            ((tokens, 3 * channels), HALF),
-            ((8, channels), FLOAT),
-            ((1, width), FLOAT),
             ((1, micro, local_rows, width), HALF),
+            ((8, small_width), FLOAT),
+            ((share, widths[0]), HALF),
+            ((share, widths[1]), HALF),
+            ((share, widths[2]), HALF),
+            ((3, share, channels), HALF),
+            ((share, hidden_units), HALF, ANY),
+            ((2, share, hidden_units), HALF, ANY),
+            ((share, hidden_units), HALF, ANY),
+            ((2, share, hidden_units), HALF, ANY),
         ],
         [
+            pltpu.VMEM((tokens, 3 * channels), HALF),
             pltpu.VMEM((micro, 8 + rows, channels), FLOAT),
             pltpu.VMEM((micro, rows, channels), FLOAT),
             pltpu.VMEM((2, micro, rows + 8, channels), FLOAT),
             pltpu.VMEM((micro, 8, channels), FLOAT),
             pltpu.VMEM((micro, 8, channels), FLOAT),
             pltpu.VMEM((tokens, width), HALF),
+            pltpu.VMEM((1, width), FLOAT),
             dma(1),
             dma(1),
             dma(micro),
             dma(micro),
+            pltpu.VMEM((4, tokens, half_model), HALF),
+            pltpu.VMEM((half_model, 2 * tokens), HALF),
         ]
-        + part_scratch
-        + total_scratch,
-        [gh1_low, gh1, projected, edge_gated, same, conv_kernel, conv_out, w_in, x, conv_gains, yout],
-        [up2_pieces[3], out2_piece, mixers_piece],
-        flops=10**9,
-        moved=120 << 20,
-    )
-
-    out1 = weight_partial(gh1_low, mixed)
-    in1 = weight_partial(n1, bp)
-    last_pieces = [(partial1, 1, 0, share), (partial1, 2, 0, share), (out1, 0, 0, share), (in1, 0, 0, share)]
-    folded = grad_qk[0:2, :head_width] + grad_qk[0:2, head_width : 2 * head_width]
-    gain_rows = jnp.concatenate([grad_gain_conv0, grad_gain_conv1, grad_gain_attn0, grad_gain_attn1], 0)
-    small_width = max(share, channels, 2 * head_width)
-
-    def to_width(array):
-        return jnp.pad(array, [(0, 0)] * (array.ndim - 1) + [(0, small_width - array.shape[-1])])
-
-    def to_all(array):
-        return jnp.broadcast_to(to_width(array), (slots,) + array.shape[:-1] + (small_width,))
-
-    small = jnp.concatenate(
-        [
-            to_width(gain_rows.reshape(4, slots, share).transpose(1, 0, 2)),
-            to_all(folded.reshape(1, 2 * head_width)),
-            to_all(grad_taps[0:3]),
-        ],
-        1,
-    )
-
-    def last_sums(small_ref, out_ref, boxes, summed, final, hs, hr, ss, sr, carry):
-        where = place()
-        s, q, h = where
-        others = [(s, q, lax.rem(h + k, heads)) for k in range(1, heads)]
-        me = q * sections + s
-        peers = [slot_peer(me, j, h) for j in range(1, slots)]
-        greet(others + peers)
-        copies = []
-        for k, peer in enumerate(others):
-            copy = remote(small_ref, boxes.at[k], hs.at[k], hr.at[k], peer)
-            copy.start()
-            copies.append(copy)
-        carry.start(where, seqs)
-        wait_all(copies)
-        over_heads = boxes[0]
-        for k in range(1, heads - 1):
-            over_heads = over_heads + boxes[k]
-        row = lax.broadcasted_iota(jnp.int32, over_heads.shape, 1)
-        summed[...] = small_ref[...] + jnp.where(row < 5, over_heads, 0.0)
-        copies = []
-        for j, peer in enumerate(peers):
-            copy = remote(summed.at[peer[0] * seqs + peer[1]], final.at[j], ss.at[j], sr.at[j], peer)
-            copy.start()
-            copies.append(copy)
-        total = summed[s * seqs + q]
-        wait_all(copies)
-        for j in range(slots - 1):
-            total = total + final[j]
-        out_ref[...] = total
-        carry.wait()
-
-    (sums,), (gate1_in, rise1_in, out1_in, in1_in) = call(
-        last_sums,
-        "last_sums",
-        8,
-        [((8, small_width), FLOAT)],
-        [
+        + [pltpu.VMEM((2 * tokens, size), HALF) for size in widths]
+        + [pltpu.VMEM((seqs, share, size), HALF) for size in widths]
+        + [pltpu.VMEM((seqs - 1, share, size), HALF) for size in widths]
+        + [
+            dma(4),
+            dma(4),
+            dma(4),
+            dma(4),
+            dma_grid(4, seqs - 1),
+            dma_grid(4, seqs - 1),
+            pltpu.VMEM((2, seqs - 1, share, padded_units), HALF),
+            pltpu.VMEM((2, share, padded_units), HALF),
+            dma_grid(2, seqs - 1),
+            dma_grid(2, seqs - 1),
+            dma(2),
+            pltpu.VMEM((4, seqs, share, padded_units), HALF),
+            dma_grid(4, 3),
+            pltpu.VMEM((2, share, hidden_units), HALF),
+            pltpu.VMEM((2, 2, share, hidden_units), HALF),
+            dma(4),
+            pltpu.VMEM((slots, 8, small_width), FLOAT),
             pltpu.VMEM((heads - 1, slots, 8, small_width), FLOAT),
             pltpu.VMEM((slots, 8, small_width), FLOAT),
             pltpu.VMEM((slots - 1, 8, small_width), FLOAT),
@@ -1254,37 +1359,110 @@
             dma(heads - 1),
             dma(slots - 1),
             dma(slots - 1),
+        ]
+        + part_scratch
+        + total_scratch,
+        [
+            gh1_low, gh1, projected, edge_gated, same, conv_kernel, conv_out, w_in, x, conv_gains, yout,
+            gh2_low, n3, n1, attended, bq, br, mixed, small,
+        ]
+        + [(array, ANY) for array in [partial1, partial2, down1_in, down2_in] + up2_in + up2_last_in],
+        flops=5 * 10**9,
+        moved=300 << 20,
+    )
+    def results(
+        edges_in, sums_in, gout2_in, gmix_in, gout1_in, gin_in, gdown2_in, gup2_in, gdown1_in, gup1_in,
+        edges_out, cgain_out, gin_out, taps_out, gout1_out, gup1_out, gdown1_out,
+        again_out, gq_out, gkv_out, gqk_out, gout2_out, gup2_out, gdown2_out,
+        down_in, up_in, down_stage, up_stage, edges_held, in_sems, out_sems, edge_sem,
+    ):
+        edges_load = pltpu.make_async_copy(edges_in, edges_held, edge_sem.at[0])
+        edges_load.start()
+        loads = [
+            pltpu.make_async_copy(source, target, in_sems.at[k])
+            for k, (source, target) in enumerate(
+                [(gdown1_in, down_in.at[0]), (gup1_in, up_in.at[0]), (gdown2_in, down_in.at[1]), (gup2_in, up_in.at[1])]
+            )
+        ]
+        start_all(loads)
+        stores = []
+        for k, (down_out, up_out) in enumerate(((gdown1_out, gup1_out), (gdown2_out, gup2_out))):
+            loads[2 * k].wait()
+            down_stage[k] = down_in[k].astype(FLOAT)
+            stores.append(pltpu.make_async_copy(down_stage.at[k], down_out, out_sems.at[2 * k]))
+            stores[-1].start()
+            loads[2 * k + 1].wait()
+            for kind in range(2):
+                up_stage[k, :, kind, :] = up_in[k, kind].astype(FLOAT)
+            stores.append(pltpu.make_async_copy(up_stage.at[k], up_out, out_sems.at[2 * k + 1]))
+            stores[-1].start()
+        cgain_out[...] = sums_in[0:2, 0:share]
+        again_out[...] = sums_in[2:4, 0:share]
+        taps_out[...] = sums_in[5:8, 0:channels]
+        for kind in range(2):
+            gqk_out[kind : kind + 1, :] = sums_in[4:5, kind * head_width : (kind + 1) * head_width]
+            start = query_width + kind * (pair_width // 2)
+            gkv_out[:, kind, :] = gmix_in[:, start : start + pair_width // 2].astype(FLOAT)
+        gq_out[...] = gmix_in[:, 0:query_width].astype(FLOAT)
+        gout1_out[...] = gout1_in[...].astype(FLOAT)
+        gout2_out[...] = gout2_in[...].astype(FLOAT)
+        gin_out[...] = gin_in[...].astype(FLOAT)
+        edges_load.wait()
+        stores.append(pltpu.make_async_copy(edges_held, edges_out, edge_sem.at[1]))
+        stores[-1].start()
+        wait_all(stores)
+
+    (
+        section_edges, cgain, gin, taps, gout1, gup1, gdown1, again, gq, gkv, gqk, gout2, gup2, gdown2,
+    ), _ = call(
+        results,
+        "results",
+        None,
+        [
+            ((1, micro, local_rows, width), HALF, ANY),
+            ((2, share), FLOAT),
+            ((3, share, channels), FLOAT),
+            ((3, channels), FLOAT),
+            ((share, channels), FLOAT),
+            ((share, 2, hidden_units), FLOAT, ANY),
+            ((share, hidden_units), FLOAT, ANY),
+            ((2, share), FLOAT),
+            ((share, query_width), FLOAT),
+            ((share, 2, pair_width // 2), FLOAT),
+            ((2, head_width), FLOAT),
+            ((share, query_width), FLOAT),
+            ((share, 2, hidden_units), FLOAT, ANY),
+            ((share, hidden_units), FLOAT, ANY),
         ],
-        [small],
-        last_pieces,
-        moved=150 << 20,
+        [
+            pltpu.VMEM((2, share, hidden_units), HALF),
+            pltpu.VMEM((2, 2, share, hidden_units), HALF),
+            pltpu.VMEM((2, share, hidden_units), FLOAT),
+            pltpu.VMEM((2, share, 2, hidden_units), FLOAT),
+            pltpu.VMEM((1, micro, local_rows, width), HALF),
+            dma(4),
+            dma(4),
+            dma(2),
+        ],
+        [(section_edges, ANY), sums, gout2, gmix, gout1, gin]
+        + [(array, ANY) for array in (gdown2, gup2, gdown1, gup1)],
+        moved=25 << 20,
     )
-
-    grad_mixers = weight_total(mixers_piece, mixers_in)
-    gate2, rise2 = [
-        jnp.concatenate([weight_total(p, a) for p, a in pairs], 0)[:, :hidden_units]
-        for pairs in (
-            list(zip(up2_pieces[:2], up2_in[:2])),
-            list(zip(up2_pieces[2:], [up2_in[2], up2_last_in])),
-        )
-    ]
-    gate1 = weight_total(last_pieces[0], gate1_in)[:, :hidden_units]
-    rise1 = weight_total(last_pieces[1], rise1_in)[:, :hidden_units]
     return (
         section_edges,
-        sums[0:2, :share],
-        weight_total(last_pieces[3], in1_in).reshape(-1, 3, channels),
-        sums[5:8, :channels],
-        weight_total(last_pieces[2], out1_in).T,
-        jnp.stack([gate1, rise1], 1),
-        weight_total((partial1, 0, 0, share), down1_in)[:, :hidden_units].T,
-        sums[2:4, :share],
-        grad_mixers[:, :query_width],
-        grad_mixers[:, query_width:].reshape(-1, 2, pair_width // 2),
-        sums[4, : 2 * head_width].reshape(2, head_width),
-        weight_total(out2_piece, out2_in).T,
-        jnp.stack([gate2, rise2], 1),
-        weight_total((partial2, 0, 0, share), down2_in)[:, :hidden_units].T,
+        cgain,
+        gin.transpose(1, 0, 2),
+        taps,
+        gout1.T,
+        gup1,
+        gdown1.T,
+        again,
+        gq,
+        gkv,
+        gqk,
+        gout2.T,
+        gup2,
+        gdown2.T,
     )
 
 

time: 561 us -> 461 us (0.82)
  local copies, waits for them, and re-layouts: 46.5 us -> 7.31 us
  Pallas kernels: 455 us -> 428 us
  other arithmetic: 23.8 us -> 4.32 us
  matrix products: 11.8 us -> 0 us
    pallas_call x9 -> x7, Pallas kernels: 455 us -> 428 us  [call(): pl.pallas_call(whole, name=name, out_shape=shapes, in_specs=[arg[1] if is...]
    unnamed x79 -> x8, local copies, waits for them, and re-layouts: 27.5 us -> 2.83 us
    slice x8 -> x0, local copies, waits for them, and re-layouts: 12.9 us -> none  [the longest x2 8.84 us: weight_total(): partial_sums[kind]]
    dot_general x4 -> x0, matrix products: 11.8 us -> none  [outer_sum(): lax.dot_general(former, latter, (((0,), (0,)), ((), ())), preferred_eleme...]
    select_n x4 -> x0, other arithmetic: 7.25 us -> none  [half_of(): kept = jnp.where(section == 0, low, high)]
    transpose x4 -> x0, other arithmetic: 6.21 us -> none  [the longest x1 1.7 us: per_device(): weight_total(last_pieces[2], out1_in)]
    add x4 -> x0, other arithmetic: 6.11 us -> none  [weight_total(): total = total + arrived[k].astype(FLOAT)]
  transfers between devices with their start and end apart: 9 -> 1, of which waited for: 0 -> 0; matrix products, arithmetic and copies ran while one was open for 10% -> 0% of each run, Pallas kernels for 51% -> 28%
where the time goes in v3:
time: 461 us; the launch traced here: 454 us
  Pallas kernels  428 us (93%)
  between operations  14.6 us (3%)
  local copies, waits for them, and re-layouts  7.31 us (2%)
    pallas_call x7, Pallas kernels, call(): pl.pallas_call(whole, name=name, out_shape=shapes, in_specs=[arg[1] if is...  428 us
  transfers between devices with their start and end apart: 1, of which 0 were waited for; matrix products, arithmetic and copies ran while one was open for 0% of the time, Pallas kernels for 28%

profile of v3, /device:TPU:0, one launch (start us, length us, event | category | flops | bytes accessed | tf_op | source)
XLA Modules:
  0.0 454.5 jit_solution(4740859120331693188)
XLA Ops:
  7.2 0.7 copy.41
  8.1 0.8 constant_dynamic-slice_fusion.2
  9.0 0.1 reshape.141
  9.2 0.8 copy.38.refs_7_.refs_4_
  10.0 0.2 copy.37
  10.2 0.7 stack.8.refs_1_.refs_4_
  10.9 0.8 dynamic-slice_convert_fusion
  11.6 0.1 convert_element_type.39
  11.7 0.8 slice_bitcast_fusion
  12.5 0.6 tile.24.refs_5_.refs_10_
  13.1 0.6 tile.27.refs_6_.refs_11_
  13.7 2.1 copy.45
  15.8 1.2 multiply_sine_fusion
  17.0 80.7 %conv_forward.1 = (bf16[256,1536]{1,0:T(8,128)(2,1)}, bf16[256,1536]{1,0:T(8,128)(2,1)}, bf16[256,1536]{1,0:T(8,128)(2,1)}, f32[3,256,384]{2,1,0:T(8,128)}, f32[...) custom-call(bf16[1,4,128,1536]{3,2,1,0:T(8,128)(2,1)} %refs_0_.1, ...), custom_call_target="tpu_custom_call" | custom-call | flops 5000000000 | bytes 209715200 | tf_op jit(solution)/shard_map/conv_forward/pallas_call | solution.py:302
  97.7 48.5 %attention_forward.1 = (f32[256,384]{1,0:T(8,128)}, f32[256,256]{1,0:T(8,128)}, bf16[256,384]{1,0:T(8,128)(2,1)}, bf16[8,256,256]{2,1,0:T(8,128)(2,1)}, bf16[256...) custom-call(bf16[256,1536]{1,0:T(8,128)(2,1)} %get-tuple-element.78.refs_0_.refs_12_, ...), custom_call_target="tpu_custom_call" | custom-call | flops 4000000000 | bytes 157286400 | tf_op jit(solution)/shard_map/attention_forward/pallas_call | solution.py:302
  146.2 47.0 %second_ffn.1 = (bf16[256,1536]{1,0:T(8,128)(2,1)}, f32[128,1536]{1,0:T(8,128)}, bf16[256,1536]{1,0:T(8,128)(2,1)}, f32[1,1536]{1,0:T(1,128)}, bf16[3,4,192,1792...) custom-call(bf16[256,1536]{1,0:T(8,128)(2,1)} %get-tuple-element.80.refs_0_, ...), custom_call_target="tpu_custom_call" | custom-call | flops 12000000000 | bytes 157286400 | tf_op jit(solution)/shard_map/second_ffn/pallas_call | solution.py:302
  193.3 70.7 %attention_backward.1 = (bf16[256,384]{1,0:T(8,128)(2,1)}, bf16[256,256]{1,0:T(8,128)(2,1)}, bf16[256,1536]{1,0:T(8,128)(2,1)}, f32[1,1536]{1,0:T(1,128)}, f32[8...) custom-call(bf16[256,1536]{1,0:T(8,128)(2,1)} %get-tuple-element.83., ...), custom_call_target="tpu_custom_call" | custom-call | flops 6000000000 | bytes 136314880 | tf_op jit(solution)/shard_map/attention_backward/pallas_call | solution.py:302
  264.0 56.9 %first_ffn_back.1 = (f32[128,1536]{1,0:T(8,128)}, bf16[256,1536]{1,0:T(8,128)(2,1)}, f32[1,1536]{1,0:T(1,128)}, bf16[3,4,192,1792]{3,2,1,0:T(8,128)(2,1)}, bf16[...) custom-call(bf16[256,1536]{1,0:T(8,128)(2,1)} %get-tuple-element.90.refs_0_, ...), custom_call_target="tpu_custom_call" | custom-call | flops 8999999488 | bytes 157286400 | tf_op jit(solution)/shard_map/first_ffn_back/pallas_call | solution.py:302
  320.9 0.8 pad_maximum_fusion
  321.7 0.1 reshape.145
  321.9 0.1 reshape.146
  322.1 0.7 fusion.refs_18_
  322.8 115.7 %conv_backward.1 = (bf16[1,4,128,1536]{3,2,1,0:T(8,128)(2,1)}, f32[8,384]{1,0:T(8,128)}, bf16[192,384]{1,0:T(8,128)(2,1)}, bf16[192,640]{1,0:T(8,128)(2,1)}, bf1...) custom-call(bf16[256,1536]{1,0:T(8,128)(2,1)} %get-tuple-element.95., ...), custom_call_target="tpu_custom_call" | custom-call | flops 5000000000 | bytes 314572800 | tf_op jit(solution)/shard_map/conv_backward/pallas_call | solution.py:302
  438.5 8.7 %results.1 = (bf16[1,4,128,1536]{3,2,1,0:T(8,128)(2,1)}, f32[2,192]{1,0:T(2,128)}, f32[3,192,384]{2,1,0:T(8,128)}, f32[3,384]{1,0:T(4,128)}, f32[192,384]{1,0:T(...) custom-call(bf16[1,4,128,1536]{3,2,1,0:T(8,128)(2,1)} %get-tuple-ele, ...), custom_call_target="tpu_custom_call" | custom-call | bytes 26214400 | tf_op jit(solution)/shard_map/results/pallas_call | solution.py:302
  (28 shorter events, 0.7 us)
Async XLA Ops:
  7.2 315.6 %all-reduce.5.cloned.1.call-start = ((), (), s32[]{:S(2)}) async-start(), calls=%async_computation | async-start | bytes 1572864 | tf_op jit(solution)/shard_map/psum | solution.py:856
  263.9 57.0 %copy-start = (f32[1,1536]{1,0:T(1,128)S(1)}, f32[1,1536]{1,0:T(1,128)}, u32[]{:S(2)}) copy-start(f32[1,1536]{1,0:T(1,128)} %get-tuple-element.108) | copy-start | bytes 18436
  263.9 57.0 %copy-start.1 = (f32[1,1536]{1,0:T(1,128)S(1)}, f32[1,1536]{1,0:T(1,128)}, u32[]{:S(2)}) copy-start(f32[1,1536]{1,0:T(1,128)} %get-tuple-element.107) | copy-start | bytes 18436
  263.9 57.8 %copy-start.2 = (f32[8,128]{1,0:T(8,128)S(1)}, f32[8,128]{1,0:T(8,128)}, u32[]{:S(2)}) copy-start(f32[8,128]{1,0:T(8,128)} %get-tuple-element.109) | copy-start | bytes 12292
Sparse Core Ops, SparseCore 0:
  193.4 50.2 all-reduce.4

commit v4 on v3

--- a/solution.py
+++ b/solution.py
@@ -42,6 +42,8 @@
 
 BLOCKS = 8
 LAG = 3
+END_FIRST = 10
+MIDDLE_FIRST = 3
 
 
 def place():
@@ -131,9 +133,10 @@
             def _():
                 filler(t)
 
-    def fill_rest(start):
-        if fillers > start:
-            loop(fillers - start, lambda i: filler(start + i))
+    def fill_rest(start, stop=fillers):
+        stop = min(stop, fillers)
+        if stop > start:
+            loop(stop - start, lambda i: filler(start + i))
 
     def reduced(flow, i, peer):
         return remote(part.at[rows(flow, i)], inbox.at[flow, i], reduce_send.at[flow, i], reduce_recv.at[flow, i], peer)
@@ -147,16 +150,17 @@
         flow = jnp.where(head == 0, 0, 1)
         inner = (section, seq, jnp.where(head == 0, 1, last - 1))
         loop(BLOCKS, lambda i: reduced(1 - flow, i, inner).start())
+        fill_rest(0, END_FIRST)
 
         def own(i):
             reduced(flow, i, inner).wait_recv()
             total = part[rows(flow, i), :].astype(FLOAT) + inbox[flow, i].astype(FLOAT)
             full[rows(flow, i), :] = finish(flow, i, total)
             gathered(flow, i, inner).start()
-            fill(i)
+            fill(END_FIRST + i)
 
         loop(BLOCKS, own)
-        fill_rest(BLOCKS)
+        fill_rest(END_FIRST + BLOCKS)
 
         def drain(i):
             gathered(1 - flow, i, inner).wait_recv()
@@ -196,9 +200,10 @@
 
             loop(BLOCKS + LAG, step)
 
-        lagged(add, near, 1 - near, 0)
-        lagged(forward, 1 - near, near, BLOCKS + LAG)
-        fill_rest(2 * (BLOCKS + LAG))
+        fill_rest(0, MIDDLE_FIRST)
+        lagged(add, near, 1 - near, MIDDLE_FIRST)
+        lagged(forward, 1 - near, near, MIDDLE_FIRST + BLOCKS + LAG)
+        fill_rest(MIDDLE_FIRST + 2 * (BLOCKS + LAG))
 
         def drain(i):
             reduced(near, i, ahead).wait_send()
@@ -207,28 +212,6 @@
             gathered(near, i, behind).wait_send()
 
         loop(BLOCKS, drain)
-
-
-class Carried:
-    def __init__(self, sources, pieces, targets, sems):
-        self.sources, self.pieces, self.targets, self.sems = sources, pieces, targets, sems
-        self.copies = []
-
-    def peers(self, where, seqs):
-        return seq_peers(where, seqs) if self.pieces else []
-
-    def start(self, where, seqs, chosen=None):
-        for at, (array, kind, first, count, left, wide) in enumerate(self.pieces):
-            if chosen is not None and at not in chosen:
-                continue
-            for k, peer in enumerate(seq_peers(where, seqs)):
-                source = self.sources[array].at[kind, peer[1], first : first + count, left : left + wide]
-                copy = remote(source, self.targets[at].at[k], self.sems[0].at[at, k], self.sems[1].at[at, k], peer)
-                copy.start()
-                self.copies.append(copy)
-
-    def wait(self):
-        wait_all(self.copies)
 
 
 def turned(values):
@@ -272,44 +255,21 @@
     return grad_raw, jnp.sum(back * raw * scale, 0, keepdims=True)
 
 
-def call(body, name, collective, outs, scratch, args, carried=(), flops=0, moved=0):
+def call(body, name, collective, outs, scratch, args, flops=0, moved=0):
     params = dict(vmem_limit_bytes=60 << 20)
     if collective is not None:
         params.update(collective_id=collective, has_side_effects=True)
-    arrays = []
-    pieces = []
-    for array, kind, first, count, left, wide in carried:
-        known = [i for i, other in enumerate(arrays) if other is array]
-        if not known:
-            arrays.append(array)
-        pieces.append((known[0] if known else len(arrays) - 1, kind, first, count, left, wide))
-    n_in, n_out, n_arrays, n_pieces = len(args), len(outs), len(arrays), len(pieces)
-    seqs = arrays[0].shape[1] if arrays else 0
-
-    def whole(*refs):
-        ins, refs = refs[:n_in], refs[n_in:]
-        sources, refs = refs[:n_arrays], refs[n_arrays:]
-        results, refs = refs[:n_out], refs[n_out:]
-        targets, refs = refs[:n_pieces], refs[n_pieces:]
-        own, sems = refs[: len(scratch)], refs[len(scratch) :]
-        extra = [Carried(sources, pieces, targets, sems)] if collective is not None else []
-        body(*ins, *results, *own, *extra)
-
-    sems = [pltpu.SemaphoreType.DMA((n_pieces, seqs - 1))] * 2 if pieces else []
-    shapes = [jax.ShapeDtypeStruct(out[0], out[1]) for out in outs]
-    for at, _, _, count, _, wide in pieces:
-        shapes.append(jax.ShapeDtypeStruct((seqs - 1, count, wide), arrays[at].dtype))
     results = pl.pallas_call(
-        whole,
+        body,
         name=name,
-        out_shape=shapes,
-        in_specs=[arg[1] if isinstance(arg, tuple) else VMEM for arg in args] + [ANY] * n_arrays,
-        out_specs=[out[2] if len(out) > 2 else VMEM for out in outs] + [ANY] * n_pieces,
-        scratch_shapes=list(scratch) + sems,
+        out_shape=[jax.ShapeDtypeStruct(out[0], out[1]) for out in outs],
+        in_specs=[arg[1] if isinstance(arg, tuple) else VMEM for arg in args],
+        out_specs=[out[2] if len(out) > 2 else VMEM for out in outs],
+        scratch_shapes=list(scratch),
         compiler_params=pltpu.CompilerParams(**params),
         cost_estimate=pl.CostEstimate(flops=flops, bytes_accessed=moved, transcendentals=0),
-    )(*[arg[0] if isinstance(arg, tuple) else arg for arg in args], *arrays)
-    return list(results[:n_out]), list(results[n_out:])
+    )(*[arg[0] if isinstance(arg, tuple) else arg for arg in args])
+    return list(results)
 
 
 def dma(count):
@@ -419,7 +379,7 @@
         in_ref, same_ref, gain_ref, win_ref, kernel_ref, wout_ref, attn_gain_ref, up_hbm, down_hbm,
         x_ref, g_ref, n1_ref, pc_ref, edge_ref, y_ref, h1_ref, n2_ref, f1_ref, a1_ref, m_ref, n3_ref,
         other, edges, normed_edges, ext, swap_send, swap_recv, edge_send, edge_recv, up_ref, down_ref, weight_sems, acc,
-        part, inbox, rs, rr, gs, gr, inbox2, rs2, rr2, gs2, gr2, carry,
+        part, inbox, rs, rr, gs, gr, inbox2, rs2, rr2, gs2, gr2,
     ):
         where = place()
         s, q, h = where
@@ -503,7 +463,7 @@
 
         head_total(part, n3_ref, inbox2, rs2, rr2, gs2, gr2, where, heads, finish_middle)
 
-    (x, g, n1, projected, edge_gated, mixed, h1, n2, f1, a1, middle, n3), _ = call(
+    (x, g, n1, projected, edge_gated, mixed, h1, n2, f1, a1, middle, n3) = call(
         conv_forward,
         "conv_forward",
         0,
@@ -542,6 +502,102 @@
     )
 
 
+    grid_rows = seqs // 2
+    first_blocks = 3 * grid_rows - 2
+    half_share = share // 2
+
+    def grid_place(q):
+        return lax.div(q, 2), lax.rem(q, 2)
+
+    def first_stage(source, target, send, recv, where):
+        s, q, h = where
+        a, b = grid_place(q)
+        copies = []
+        for row in range(grid_rows):
+            copies.append((source(row * 2 + 1 - b, 0), row, (s, a * 2 + 1 - b, h)))
+        for k in range(1, grid_rows):
+            row = lax.rem(a + k, grid_rows)
+            for column in range(2):
+                copies.append((source(row * 2 + column, 1), grid_rows + 2 * (k - 1) + column, (s, row * 2 + b, h)))
+        return [remote(block, target(i), send.at[i], recv.at[i], peer) for block, i, peer in copies]
+
+    def passed_blocks(where):
+        s, q, h = where
+        a, b = grid_place(q)
+        blocks = []
+        for k in range(1, grid_rows):
+            row = lax.rem(a + k, grid_rows)
+            blocks.append((row * 2 + b, 0, [row], (s, row * 2 + b, h)))
+        arrived = [grid_rows + 2 * j + 1 - b for j in range(grid_rows - 1)]
+        blocks.append((a * 2 + 1 - b, 1, arrived, (s, a * 2 + 1 - b, h)))
+        return blocks
+
+    def half_rows(side):
+        return slice(side * half_share, (side + 1) * half_share)
+
+    def combine(passing, arrived, where):
+        for i, (_, _, sources, _) in enumerate(passed_blocks(where)):
+            total = passing(i)[...].astype(FLOAT)
+            for source in sources:
+                total = total + arrived[source].astype(FLOAT)
+            passing(i)[...] = total.astype(HALF)
+
+    def second_stage(passing, target, send, recv, where):
+        return [
+            remote(passing(i), target.at[i], send.at[i], recv.at[i], peer)
+            for i, (_, _, _, peer) in enumerate(passed_blocks(where))
+        ]
+
+    def load_passing(partial, passing, sems, where):
+        return [
+            pltpu.make_async_copy(partial.at[dest, half_rows(side)], passing.at[i], sems.at[i])
+            for i, (dest, side, _, _) in enumerate(passed_blocks(where))
+        ]
+
+    def two_halves(own, arrived, passed, where):
+        a, b = grid_place(where[1])
+        upper = own[half_rows(0), :].astype(FLOAT) + arrived[a].astype(FLOAT)
+        for k in range(grid_rows - 1):
+            upper = upper + passed[k].astype(FLOAT)
+        lower = own[half_rows(1), :].astype(FLOAT) + passed[grid_rows - 1].astype(FLOAT)
+        for j in range(grid_rows - 1):
+            lower = lower + arrived[grid_rows + 2 * j + b].astype(FLOAT)
+        return upper, lower
+
+    def dma_grid(*shape):
+        return pltpu.SemaphoreType.DMA(shape)
+
+    def first_shape(count):
+        return ((count, first_blocks, half_share, padded_units), HALF, ANY)
+
+    def second_shape(count):
+        return ((count, grid_rows, half_share, padded_units), HALF, ANY)
+
+    def passing_scratch(count):
+        return [
+            pltpu.VMEM((count, grid_rows, half_share, padded_units), HALF),
+            pltpu.VMEM((count, first_blocks, half_share, padded_units), HALF),
+            dma_grid(count, grid_rows + 1),
+            dma_grid(count, grid_rows),
+            dma_grid(count, grid_rows),
+        ]
+
+    def pass_loads(partial, kinds, arrived, passing, held, sems, where):
+        copies = []
+        for k, kind in enumerate(kinds):
+            copies += load_passing(partial.at[kind], passing.at[k], sems.at[k], where)
+            copies.append(pltpu.make_async_copy(arrived.at[k], held.at[k], sems.at[k, grid_rows]))
+        return copies
+
+    def pass_sends(count, passing, held, target, send, recv, where):
+        copies = []
+        for k in range(count):
+            combine(lambda i, k=k: passing.at[k, i], held.at[k], where)
+            sends = second_stage(lambda i, k=k: passing.at[k, i], target.at[k], send.at[k], recv.at[k], where)
+            start_all(sends)
+            copies += sends
+        return copies
+
     def transposed(array_ref, given_ref):
         start = pl.multiple_of(lax.axis_index("section") * half_model, 128)
         own = array_ref[:, pl.ds(start, half_model)]
@@ -566,9 +622,7 @@
             (1 - s, q, h),
         )
 
-    def gradient_tiles(former, latter, stage, partial_hbm, first_in, local_sems, send, recv, where, at_once):
-        peers = seq_peers(where, seqs)
-
+    def gradient_tiles(former, latter, stage, partial_hbm, first_in, local_sems, send, recv, where):
         def split(t):
             kind = lax.div(t, tiles)
             at = lax.rem(t, tiles)
@@ -580,10 +634,14 @@
                 stage.at[kind, dest, :, columns], partial_hbm.at[kind, dest, :, columns], local_sems.at[t, dest]
             )
 
-        def sent(t, k):
+        def sent(t):
             kind, columns = split(t)
-            return remote(
-                stage.at[kind, peers[k][1], :, columns], first_in.at[k, :, columns], send.at[t, k], recv.at[t, k], peers[k]
+            return first_stage(
+                lambda dest, side: stage.at[kind, dest, half_rows(side), columns],
+                lambda i: first_in.at[kind, i, :, columns],
+                send.at[t],
+                recv.at[t],
+                where,
             )
 
         def tile(t):
@@ -591,25 +649,21 @@
             use = jnp.where(kind == 0, 0, 1)
             result = product(former[use], latter[kind, :, columns]).astype(HALF)
             stage[kind, :, :, columns] = result.reshape(seqs, share, tile_width)
+
+            @pl.when(t < 2 * tiles)
+            def _():
+                start_all(sent(t))
+
             for dest in range(seqs):
                 stored(t, dest).start()
-
-            @pl.when(t < at_once)
-            def _():
-                for k in range(seqs - 1):
-                    sent(t, k).start()
 
         def finish():
             def stored_all(t):
                 for dest in range(seqs):
                     stored(t, dest).wait()
 
-            def sent_all(t):
-                for k in range(seqs - 1):
-                    sent(t, k).wait()
-
             loop(3 * tiles, stored_all)
-            loop(at_once, sent_all)
+            loop(2 * tiles, lambda t: wait_all(sent(t)))
 
         return tile, finish
 
@@ -624,16 +678,11 @@
         pltpu.SemaphoreType.DMA((3, len(slabs))),
         pltpu.SemaphoreType.DMA((3, len(slabs))),
         pltpu.SemaphoreType.DMA((3 * tiles, seqs)),
-        pltpu.SemaphoreType.DMA((tiles, seqs - 1)),
-        pltpu.SemaphoreType.DMA((tiles, seqs - 1)),
+        pltpu.SemaphoreType.DMA((2 * tiles, first_blocks)),
+        pltpu.SemaphoreType.DMA((2 * tiles, first_blocks)),
     ]
-    few_tiles = (tiles + 1) // 2
-
-    def partial_outs(at_once):
-        return [
-            ((3, seqs, share, padded_units), HALF, ANY),
-            ((seqs - 1, share, at_once * tile_width), HALF, ANY),
-        ]
+    partial_outs = [((3, seqs, share, padded_units), HALF, ANY), first_shape(2)]
+
 
     def slot_peer(me, j, h):
         other = lax.rem(me + j, slots)
@@ -697,7 +746,7 @@
     def attention_forward(
         n3_ref, wq_ref, wp_ref, cos_ref, sin_ref, qg_ref, kg_ref, segq_ref, seg_ref, wo_ref, m_ref, gain_ref,
         qr_ref, r_ref, q_ref, all_ref, o_ref, h2_ref, n4_ref,
-        send, recv, near_send, near_recv, part, inbox, rs, rr, gs, gr, carry,
+        send, recv, near_send, near_recv, part, inbox, rs, rr, gs, gr,
     ):
         where = place()
         s, q, h = where
@@ -737,7 +786,7 @@
 
         head_total(part, n4_ref, inbox, rs, rr, gs, gr, where, heads, finish)
 
-    (query_raw, pair_raw, queries, all_pairs, attended, h2, n4), _ = call(
+    (query_raw, pair_raw, queries, all_pairs, attended, h2, n4) = call(
         attention_forward,
         "attention_forward",
         2,
@@ -770,7 +819,7 @@
         n4_ref, g_ref, h2_ref, gain_ref, up_hbm, down_hbm,
         py_ref, gh2_ref, low_ref, gg_ref, partial_hbm, first_in,
         acc_y, up_ref, down_ref, weight_sems, acc, given, former, latter, stage, hs, hr, ls, lr, local_sems, ts, tr,
-        part, inbox, rs, rr, gs, gr, carry,
+        part, inbox, rs, rr, gs, gr,
     ):
         where = place()
         s, q, h = where
@@ -819,13 +868,23 @@
                 acc_y[flow * half_tokens : (flow + 1) * half_tokens, :] += h2_ref[...]
 
         py_ref[...] = acc_y[...].astype(HALF)
-        wait_all(halves)
-        former[0] = transposed(g_ref, given.at[0])
-        former[1] = transposed(n4_ref, given.at[1])
-        wait_all(swaps)
         tile, tiles_done = gradient_tiles(
-            former, latter, stage, partial_hbm, first_in, local_sems, ts, tr, where, few_tiles
+            former, latter, stage, partial_hbm, first_in, local_sems, ts, tr, where
         )
+
+        def filler(t):
+            for k, array_ref in enumerate((g_ref, n4_ref)):
+
+                @pl.when(t == k)
+                def _(k=k, array_ref=array_ref):
+                    halves[k].wait()
+                    if k:
+                        wait_all(swaps)
+                    former[k] = transposed(array_ref, given.at[k])
+
+            @pl.when(t >= 2)
+            def _():
+                tile(t - 2)
 
         def finish(flow, i, total):
             grad_hidden, grad_gain = norm_back(h2_ref[kept_rows(i), :], gain_ref[1:2, :], total)
@@ -834,10 +893,10 @@
             gg_ref[...] += grad_gain
             return grad.astype(HALF)
 
-        head_total(part, low_ref, inbox, rs, rr, gs, gr, where, heads, finish, tile, 3 * tiles)
+        head_total(part, low_ref, inbox, rs, rr, gs, gr, where, heads, finish, filler, 3 * tiles + 2)
         tiles_done()
 
-    (part_y, gh2, gh2_low, grad_gain_attn1, partial2, down2_in), _ = call(
+    (part_y, gh2, gh2_low, grad_gain_attn1, partial2, first2) = call(
         second_ffn,
         "second_ffn",
         4,
@@ -847,33 +906,30 @@
             ((tokens, width), HALF),
             ((1, width), FLOAT),
         ]
-        + partial_outs(few_tiles),
+        + partial_outs,
         [pltpu.VMEM((tokens, width), FLOAT)] + ffn_scratch + part_scratch + total_scratch,
         [n4, g, h2, attn_gains, (second_up, ANY), (attn_down, ANY)],
         flops=12 * 10**9,
         moved=150 << 20,
     )
     yout = lax.psum(part_y, "head")
-    half_share = share // 2
-    few_wide = few_tiles * tile_width
-    up2_pieces = [
-        (partial2, kind, first, half_share, 0, padded_units) for kind in (1, 2) for first in (0, half_share)
-    ]
-    down2_piece = (partial2, 0, 0, share, few_wide, padded_units - few_wide)
-
     def attention_backward(
         glow_ref, wo_ref, q_ref, all_ref, segq_ref, seg_ref,
-        qr_ref, r_ref, cos_ref, sin_ref, qg_ref, kg_ref, wq_ref, wp_ref, m_ref, gh2_ref, gain_ref,
-        bq_ref, br_ref, low_ref, gg_ref, gqk_ref,
+        qr_ref, r_ref, cos_ref, sin_ref, qg_ref, kg_ref, wq_ref, wp_ref, m_ref, gh2_ref, gain_ref, partial2_hbm, first2_hbm,
+        bq_ref, br_ref, low_ref, gg_ref, gqk_ref, second_in, first_in,
         grads, totals, gq_ref, gp_ref, near_slots, pair_slots, ns, nr, ps, pr,
-        part, inbox, rs, rr, gs, gr, carry,
+        passing, held, load_sems, vs, vr, fs, fr,
+        part, inbox, rs, rr, gs, gr,
     ):
         where = place()
         s, q, h = where
         partner = (1 - s, q, h)
         peers = seq_peers(where, seqs)
+        loads = pass_loads(partial2_hbm, (0, 1), first2_hbm, passing, held, load_sems, where)
+        start_all(loads)
         greet([partner] + peers, where, heads)
-        carry.start(where, seqs, [0])
+        wait_all(loads)
+        travelling = pass_sends(2, passing, held, second_in, vs, vr, where)
         gg_ref[...] = jnp.zeros_like(gg_ref)
         gqk_ref[...] = jnp.zeros_like(gqk_ref)
         grads[...] = back_product(glow_ref[...], wo_ref[...]).astype(HALF)
@@ -925,7 +981,11 @@
             copy = remote(near_slots.at[peer[1]], pair_slots.at[k], ps.at[k], pr.at[k], peer)
             copy.start()
             copies.append(copy)
-        carry.start(where, seqs, [1, 2, 3])
+        later = first_stage(
+            lambda dest, side: partial2_hbm.at[2, dest, half_rows(side)], lambda i: first_in.at[0, i], fs, fr, where
+        )
+        start_all(later)
+        travelling += later
         for start, size in chunks_of(query_width):
             span = slice(start, start + size)
             grad_raw, grad_gain = rotary_back(qr_ref[:, span], qg_ref[...], cos, sin, gq_ref[:, span])
@@ -951,9 +1011,9 @@
             return (gh2_ref[kept_rows(i), :] + grad_entry).astype(HALF)
 
         head_total(part, low_ref, inbox, rs, rr, gs, gr, where, heads, finish)
-        carry.wait()
-
-    (bq, br, gm_low, grad_gain_attn0, grad_qk), up2_in = call(
+        wait_all(travelling)
+
+    (bq, br, gm_low, grad_gain_attn0, grad_qk, second2, first2_last) = call(
         attention_backward,
         "attention_backward",
         5,
@@ -963,6 +1023,8 @@
             ((tokens, width), HALF),
             ((1, width), FLOAT),
             ((8, 128), FLOAT),
+            second_shape(2),
+            first_shape(1),
         ],
         [
             pltpu.VMEM((tokens, query_width), HALF),
@@ -976,31 +1038,37 @@
             dma(seqs - 1),
             dma(seqs - 1),
         ]
+        + passing_scratch(2)
+        + [dma(first_blocks), dma(first_blocks)]
         + part_scratch
         + total_scratch,
         [
             gh2_low, attn_out, queries, all_pairs, local_segments, segment_ids,
             query_raw, pair_raw, cosine, sine, query_gain, key_gain, w_query, w_pair, middle, gh2, attn_gains,
+            (partial2, ANY), (first2, ANY),
         ],
-        up2_pieces[:3] + [down2_piece],
         flops=6 * 10**9,
         moved=130 << 20,
     )
 
     def first_ffn_back(
-        gm_ref, n2_ref, f1_ref, a1_ref, h1_ref, gain_ref, up_hbm, down_hbm,
-        gh1_ref, low_ref, gg_ref, partial_hbm, first_in,
+        gm_ref, n2_ref, f1_ref, a1_ref, h1_ref, gain_ref, up_hbm, down_hbm, partial2_hbm, first2_hbm,
+        gh1_ref, low_ref, gg_ref, partial_hbm, first_in, second_in,
         up_ref, down_ref, weight_sems, acc, given, former, latter, stage, hs, hr, ls, lr, local_sems, ts, tr,
-        part, inbox, rs, rr, gs, gr, carry,
+        passing, held, load_sems, vs, vr,
+        part, inbox, rs, rr, gs, gr,
     ):
         where = place()
         s, q, h = where
         weights = weight_loads(up_hbm, down_hbm, up_ref, down_ref, weight_sems)
+        loads = pass_loads(partial2_hbm, (2,), first2_hbm, passing, held, load_sems, where)
+        start_all(loads)
         start_all(weights)
         clear_padding(latter)
         latter[0, 0:tokens, 0:hidden_units] = a1_ref[...]
         greet([(1 - s, q, h)] + seq_peers(where, seqs), where, heads)
-        carry.start(where, seqs)
+        wait_all(loads)
+        travelling = pass_sends(1, passing, held, second_in, vs, vr, where)
         halves = half_swaps([gm_ref, n2_ref], [given.at[0], given.at[1]], hs, hr, where)
         start_all(halves)
         gg_ref[...] = jnp.zeros_like(gg_ref)
@@ -1028,13 +1096,23 @@
             else:
                 acc[...] += term
         part[...] = acc[...].astype(HALF)
-        wait_all(halves)
-        former[0] = transposed(gm_ref, given.at[0])
-        former[1] = transposed(n2_ref, given.at[1])
-        wait_all(swaps)
         tile, tiles_done = gradient_tiles(
-            former, latter, stage, partial_hbm, first_in, local_sems, ts, tr, where, tiles
+            former, latter, stage, partial_hbm, first_in, local_sems, ts, tr, where
         )
+
+        def filler(t):
+            for k, array_ref in enumerate((gm_ref, n2_ref)):
+
+                @pl.when(t == k)
+                def _(k=k, array_ref=array_ref):
+                    halves[k].wait()
+                    if k:
+                        wait_all(swaps)
+                    former[k] = transposed(array_ref, given.at[k])
+
+            @pl.when(t >= 2)
+            def _():
+                tile(t - 2)
 
         def finish(flow, i, total):
             grad_hidden, grad_gain = norm_back(h1_ref[kept_rows(i), :], gain_ref[1:2, :], total)
@@ -1043,18 +1121,17 @@
             gh1_ref[kept_rows(i), :] = grad
             return grad.astype(HALF)
 
-        head_total(part, low_ref, inbox, rs, rr, gs, gr, where, heads, finish, tile, 3 * tiles)
+        head_total(part, low_ref, inbox, rs, rr, gs, gr, where, heads, finish, filler, 3 * tiles + 2)
         tiles_done()
-        carry.wait()
-
-    (gh1, gh1_low, grad_gain_conv1, partial1, down1_in), up2_last_in = call(
+        wait_all(travelling)
+
+    (gh1, gh1_low, grad_gain_conv1, partial1, first1, second2_last) = call(
         first_ffn_back,
         "first_ffn_back",
         6,
-        [((half_tokens, width), FLOAT), ((tokens, width), HALF), ((1, width), FLOAT)] + partial_outs(tiles),
-        ffn_scratch + part_scratch + total_scratch,
-        [gm_low, n2, f1, a1, h1, conv_gains, (first_up, ANY), (conv_down, ANY)],
-        up2_pieces[3:],
+        [((half_tokens, width), FLOAT), ((tokens, width), HALF), ((1, width), FLOAT)] + partial_outs + [second_shape(1)],
+        ffn_scratch + passing_scratch(1) + part_scratch + total_scratch,
+        [gm_low, n2, f1, a1, h1, conv_gains, (first_up, ANY), (conv_down, ANY), (partial2, ANY), (first2_last, ANY)],
         flops=9 * 10**9,
         moved=150 << 20,
     )
@@ -1064,14 +1141,14 @@
     def conv_backward(
         low_ref, gh1_ref, pc_ref, edge_ref, same_ref, kernel_ref, wout_ref, win_ref, x_ref, gain_ref, yout_ref,
         ghlow_ref, n3_ref, n1_ref, o_ref, bq_ref, br_ref, mixed_ref, small_in,
-        partial1, partial2, down1_in, down2_a, gate2_a, gate2_b, rise2_a, down2_b, rise2_b,
+        partial1, partial2, first1, first2, first2_last, second2, second2_last,
         edges_ref, sums_ref, gout2_ref, gmix_ref, gout1_ref, gin_ref, gdown2, gup2, gdown1, gup1,
         bp_ref, ext, spread, gz_ext, outgoing, arrived, full, gg_ref, edge_send, edge_recv, swap_send, swap_recv,
-        given, former, latter0, latter1, latter2, latter3, stage0, stage1, stage2, stage3, in0, in1, in2, in3,
-        hs, hr, ls, lr, ms, mr, bulk_in, bulk_own, bs, br_sem, own_sem,
-        bufs, buf_sems, down_stage, up_stage, out_sems,
+        given, former, latter0, latter1, latter2, latter3, stage0, stage1, stage2, stage3,
+        in0, in1, in2, in3, turn0, turn1, turn2, turn3, hs, hr, ls, lr, ms, mr, us, ur,
+        own_buf, first_buf, second_buf, passing, item_sems, vs, vr, fs, fr, down_stage, up_stage, out_sems,
         packed, boxes, summed, final, zs, zr, ss, sr,
-        part, inbox, rs, rr, gs, gr, carry,
+        part, inbox, rs, rr, gs, gr,
     ):
         where = place()
         s, q, h = where
@@ -1083,29 +1160,28 @@
         me = q * sections + s
         slot_peers = [slot_peer(me, j, h) for j in range(1, slots)]
         peers = seq_peers(where, seqs)
-        latters, stages, incomes = [latter0, latter1, latter2, latter3], [stage0, stage1, stage2, stage3], [in0, in1, in2, in3]
-        own_bulk = [pltpu.make_async_copy(partial1.at[kind + 1, q], bulk_own.at[kind], own_sem.at[kind]) for kind in range(2)]
-        start_all(own_bulk)
-
-        def load(slot, own, pieces):
-            copies = [pltpu.make_async_copy(own, bufs.at[slot, 0], buf_sems.at[slot, 0])]
-            for k, (piece, start, count, left, wide) in enumerate(pieces):
-                target = bufs.at[slot, 1:seqs, start : start + count, left : left + wide]
-                copies.append(pltpu.make_async_copy(piece, target, buf_sems.at[slot, 1 + k]))
+        latters, stages = [latter0, latter1, latter2, latter3], [stage0, stage1, stage2, stage3]
+        incomes, turns = [in0, in1, in2, in3], [turn0, turn1, turn2, turn3]
+        loads = []
+        sources = [
+            (partial2.at[0], first2.at[0], second2.at[0]),
+            (partial2.at[1], first2.at[1], second2.at[1]),
+            (partial2.at[2], first2_last.at[0], second2_last.at[0]),
+            (partial1.at[0], first1.at[0], None),
+            (partial1.at[1], first1.at[1], None),
+            (partial1.at[2], None, None),
+        ]
+        for n, (partial, arrived_hbm, passed_hbm) in enumerate(sources):
+            copies = [pltpu.make_async_copy(partial.at[q], own_buf.at[n], item_sems.at[n, 0])]
+            if arrived_hbm is not None:
+                copies.append(pltpu.make_async_copy(arrived_hbm, first_buf.at[n], item_sems.at[n, 1]))
+            if passed_hbm is not None:
+                copies.append(pltpu.make_async_copy(passed_hbm, second_buf.at[n], item_sems.at[n, 2]))
+            else:
+                copies += load_passing(partial, passing.at[n - 3], item_sems.at[n, pl.ds(3, grid_rows)], where)
+            loads.append(copies)
+        for copies in loads[3:] + loads[:3]:
             start_all(copies)
-            return copies
-
-        halves_of = ((0, half_share, 0, padded_units), (half_share, half_share, 0, padded_units))
-        loads = [
-            load(
-                0,
-                partial2.at[0, q],
-                [(down2_a, 0, share, 0, few_wide), (down2_b, 0, share, few_wide, padded_units - few_wide)],
-            ),
-            load(1, partial2.at[1, q], [(gate2_a, *halves_of[0]), (gate2_b, *halves_of[1])]),
-            load(2, partial2.at[2, q], [(rise2_a, *halves_of[0]), (rise2_b, *halves_of[1])]),
-            load(3, partial1.at[0, q], [(down1_in, 0, share, 0, padded_units)]),
-        ]
         greet([partner, preceding, following] + others + slot_peers, where, heads)
         latters[0][0:tokens, :] = o_ref[...]
         latters[1][0:tokens, 0:query_width] = bq_ref[...]
@@ -1137,12 +1213,18 @@
         edge = remote(outgoing, arrived, edge_send.at[0], edge_recv.at[0], preceding)
         edge.start()
         bulk = []
-        for kind in range(2):
-            for k, peer in enumerate(peers):
-                bulk.append(
-                    remote(partial1.at[kind + 1, peer[1]], bulk_in.at[kind, k], bs.at[kind, k], br_sem.at[kind, k], peer)
-                )
-        start_all(bulk)
+        for n in (3, 4):
+            wait_all(loads[n])
+            combine(lambda i, n=n: passing.at[n - 3, i], first_buf.at[n], where)
+            sends = second_stage(
+                lambda i, n=n: passing.at[n - 3, i], second_buf.at[n], vs.at[n - 3], vr.at[n - 3], where
+            )
+            start_all(sends)
+            bulk.append(sends)
+        last_first = first_stage(
+            lambda dest, side: partial1.at[2, dest, half_rows(side)], lambda i: first_buf.at[5, i], fs, fr, where
+        )
+        start_all(last_first)
         taps = [None, None, None]
         for m in range(micro):
             span = slice(m * rows, (m + 1) * rows)
@@ -1188,7 +1270,33 @@
             gg_ref[...] += grad_gain
             return (gh1_ref[kept_rows(i), :] + grad_start).astype(HALF)
 
-        head_total(part, full, inbox, rs, rr, gs, gr, where, heads, finish)
+        mixer_sends = [
+            first_stage(
+                lambda dest, side, k=k: stages[k].at[dest, half_rows(side)],
+                lambda i, k=k: incomes[k].at[i],
+                ms.at[k],
+                mr.at[k],
+                where,
+            )
+            for k in range(4)
+        ]
+
+        def mixer_step(t):
+            for k in range(4):
+
+                @pl.when(t == 2 * k)
+                def _(k=k):
+                    halves[k].wait()
+                    former[...] = transposed(former_refs[k], given.at[k])
+
+                @pl.when(t == 2 * k + 1)
+                def _(k=k):
+                    swaps[k].wait()
+                    result = product(former[...], latters[k][...]).astype(HALF)
+                    stages[k][...] = result.reshape(seqs, share, widths[k])
+                    start_all(mixer_sends[k])
+
+        head_total(part, full, inbox, rs, rr, gs, gr, where, heads, finish, mixer_step, 8)
         keep = pl.ds(pl.multiple_of(s * rows, rows), rows)
         edges_ref[0, :, keep, :] = jnp.where(first, full[...], yout_ref[...]).reshape(micro, rows, width)
         part[...] = jnp.where(first, yout_ref[...], full[...])
@@ -1208,36 +1316,28 @@
             copy = remote(packed, boxes.at[k], zs.at[k], zr.at[k], peer)
             copy.start()
             over.append(copy)
-        wait_all(halves)
-        sends = []
-        for k in range(4):
-            former[...] = transposed(former_refs[k], given.at[k])
-            swaps[k].wait()
-            result = product(former[...], latters[k][...]).astype(HALF)
-            stages[k][...] = result.reshape(seqs, share, widths[k])
-            for j, peer in enumerate(peers):
-                copy = remote(stages[k].at[peer[1]], incomes[k].at[j], ms.at[k, j], mr.at[k, j], peer)
-                copy.start()
-                sends.append(copy)
-            if k == 0:
-                wait_all(over)
-                over_heads = boxes[0]
-                for j in range(1, heads - 1):
-                    over_heads = over_heads + boxes[j]
-                row = lax.broadcasted_iota(jnp.int32, over_heads.shape, 1)
-                summed[...] = packed[...] + jnp.where(row < 5, over_heads, 0.0)
-                across = []
-                for j, peer in enumerate(slot_peers):
-                    copy = remote(summed.at[peer[0] * seqs + peer[1]], final.at[j], ss.at[j], sr.at[j], peer)
-                    copy.start()
-                    across.append(copy)
-
-        def summed_up(own, arrivals):
-            total = own.astype(FLOAT)
-            for piece in arrivals:
-                total = total + piece.astype(FLOAT)
-            return total[:, :hidden_units]
-
+        def passed_on(n):
+            sends = second_stage(
+                lambda i: passing.at[n - 3, i], second_buf.at[n], vs.at[n - 3], vr.at[n - 3], where
+            )
+            start_all(sends)
+            bulk.append(sends)
+
+        wait_all(last_first)
+        wait_all(loads[5])
+        combine(lambda i: passing.at[2, i], first_buf.at[5], where)
+        passed_on(5)
+        wait_all(over)
+        over_heads = boxes[0]
+        for j in range(1, heads - 1):
+            over_heads = over_heads + boxes[j]
+        row = lax.broadcasted_iota(jnp.int32, over_heads.shape, 1)
+        summed[...] = packed[...] + jnp.where(row < 5, over_heads, 0.0)
+        across = []
+        for j, peer in enumerate(slot_peers):
+            copy = remote(summed.at[peer[0] * seqs + peer[1]], final.at[j], ss.at[j], sr.at[j], peer)
+            copy.start()
+            across.append(copy)
         outs = []
 
         def leave(source, target, at):
@@ -1245,21 +1345,41 @@
             copy.start()
             outs.append(copy)
 
-        def from_buffer(slot):
-            wait_all(loads[slot])
-            return summed_up(bufs[slot, 0], [bufs[slot, k] for k in range(1, seqs)])
-
-        down_stage[0] = from_buffer(0).astype(HALF)
-        leave(down_stage.at[0], gdown2, 0)
-        up_stage[0, 0] = from_buffer(1).astype(HALF)
-        up_stage[0, 1] = from_buffer(2).astype(HALF)
-        leave(up_stage.at[0], gup2, 1)
-        down_stage[1] = from_buffer(3).astype(HALF)
-        leave(down_stage.at[1], gdown1, 2)
-        wait_all(own_bulk)
-        for kind in range(2):
-            wait_all(bulk[kind * (seqs - 1) : (kind + 1) * (seqs - 1)])
-            up_stage[1, kind] = summed_up(bulk_own[kind], [bulk_in[kind, k] for k in range(seqs - 1)]).astype(HALF)
+        def fill_stage(n, target):
+            upper, lower = two_halves(own_buf.at[n], first_buf.at[n], second_buf.at[n], where)
+            target[half_rows(0), :] = upper[:, :hidden_units].astype(HALF)
+            target[half_rows(1), :] = lower[:, :hidden_units].astype(HALF)
+
+        def second_half_items():
+            for n in range(3):
+                wait_all(loads[n])
+            fill_stage(0, down_stage.at[0])
+            leave(down_stage.at[0], gdown2, 0)
+            for kind in range(2):
+                fill_stage(1 + kind, up_stage.at[0, kind])
+            leave(up_stage.at[0], gup2, 1)
+
+        mixer_turns = []
+        for k in range(4):
+            wait_all(mixer_sends[k])
+            blocks = passed_blocks(where)
+
+            def passing_block(i, k=k):
+                return stages[k].at[blocks[i][0], half_rows(blocks[i][1])]
+
+            combine(passing_block, incomes[k], where)
+            sends = second_stage(passing_block, turns[k], us.at[k], ur.at[k], where)
+            start_all(sends)
+            mixer_turns.append(sends)
+            if k == 1:
+                second_half_items()
+        for n in (3, 4, 5):
+            wait_all(bulk[n - 3])
+            if n == 3:
+                fill_stage(3, down_stage.at[1])
+                leave(down_stage.at[1], gdown1, 2)
+            else:
+                fill_stage(n, up_stage.at[1, n - 4])
         leave(up_stage.at[1], gup1, 3)
         wait_all(edge_swaps)
         wait_all(across)
@@ -1267,16 +1387,15 @@
         for j in range(slots - 1):
             total = total + final[j]
         sums_ref[...] = total
-        wait_all(sends)
         for k, target in enumerate((gout2_ref, gmix_ref, gout1_ref, None)):
-            total = stages[k][q].astype(FLOAT)
-            for j in range(seqs - 1):
-                total = total + incomes[k][j].astype(FLOAT)
-            if target is None:
-                for c in range(3):
-                    gin_ref[c] = total[:, c * channels : (c + 1) * channels].astype(HALF)
-            else:
-                target[...] = total.astype(HALF)
+            wait_all(mixer_turns[k])
+            for side, value in enumerate(two_halves(stages[k].at[q], incomes[k], turns[k], where)):
+                value = value.astype(HALF)
+                if target is None:
+                    for c in range(3):
+                        gin_ref[c, half_rows(side), :] = value[:, c * channels : (c + 1) * channels]
+                else:
+                    target[half_rows(side), :] = value
         wait_all(outs)
 
     folded = grad_qk[0:2, :head_width] + grad_qk[0:2, head_width : 2 * head_width]
@@ -1296,10 +1415,7 @@
         1,
     )
 
-    def dma_grid(*shape):
-        return pltpu.SemaphoreType.DMA(shape)
-
-    (section_edges, sums, gout2, gmix, gout1, gin, gdown2, gup2, gdown1, gup1), _ = call(
+    (section_edges, sums, gout2, gmix, gout1, gin, gdown2, gup2, gdown1, gup1) = call(
         conv_backward,
         "conv_backward",
         7,
@@ -1333,21 +1449,26 @@
         ]
         + [pltpu.VMEM((2 * tokens, size), HALF) for size in widths]
         + [pltpu.VMEM((seqs, share, size), HALF) for size in widths]
-        + [pltpu.VMEM((seqs - 1, share, size), HALF) for size in widths]
+        + [pltpu.VMEM((first_blocks, half_share, size), HALF) for size in widths]
+        + [pltpu.VMEM((grid_rows, half_share, size), HALF) for size in widths]
         + [
             dma(4),
             dma(4),
             dma(4),
             dma(4),
-            dma_grid(4, seqs - 1),
-            dma_grid(4, seqs - 1),
-            pltpu.VMEM((2, seqs - 1, share, padded_units), HALF),
-            pltpu.VMEM((2, share, padded_units), HALF),
-            dma_grid(2, seqs - 1),
-            dma_grid(2, seqs - 1),
-            dma(2),
-            pltpu.VMEM((4, seqs, share, padded_units), HALF),
-            dma_grid(4, 3),
+            dma_grid(4, first_blocks),
+            dma_grid(4, first_blocks),
+            dma_grid(4, grid_rows),
+            dma_grid(4, grid_rows),
+            pltpu.VMEM((6, share, padded_units), HALF),
+            pltpu.VMEM((6, first_blocks, half_share, padded_units), HALF),
+            pltpu.VMEM((6, grid_rows, half_share, padded_units), HALF),
+            pltpu.VMEM((3, grid_rows, half_share, padded_units), HALF),
+            dma_grid(6, 3 + grid_rows),
+            dma_grid(3, grid_rows),
+            dma_grid(3, grid_rows),
+            dma(first_blocks),
+            dma(first_blocks),
             pltpu.VMEM((2, share, hidden_units), HALF),
             pltpu.VMEM((2, 2, share, hidden_units), HALF),
             dma(4),
@@ -1366,7 +1487,7 @@
             gh1_low, gh1, projected, edge_gated, same, conv_kernel, conv_out, w_in, x, conv_gains, yout,
             gh2_low, n3, n1, attended, bq, br, mixed, small,
         ]
-        + [(array, ANY) for array in [partial1, partial2, down1_in, down2_in] + up2_in + up2_last_in],
+        + [(array, ANY) for array in (partial1, partial2, first1, first2, first2_last, second2, second2_last)],
         flops=5 * 10**9,
         moved=300 << 20,
     )
@@ -1414,7 +1535,7 @@
 
     (
         section_edges, cgain, gin, taps, gout1, gup1, gdown1, again, gq, gkv, gqk, gout2, gup2, gdown2,
-    ), _ = call(
+    ) = call(
         results,
         "results",
         None,

time: 461 us -> 426 us (0.924)
  Pallas kernels: 428 us -> 394 us
    pallas_call x7, Pallas kernels: 428 us -> 394 us  [call(): pl.pallas_call(body, name=name, out_shape=[jax.ShapeDtypeStruct(out[0], o...]
  transfers between devices with their start and end apart: 1 -> 1, of which waited for: 0 -> 0; matrix products, arithmetic and copies ran while one was open for 0% -> 0% of each run, Pallas kernels for 28% -> 29%
where the time goes in v4:
time: 426 us; the launch traced here: 420 us
  Pallas kernels  394 us (92%)
  between operations  14.4 us (3%)
  local copies, waits for them, and re-layouts  7.31 us (2%)
  other arithmetic  4.32 us (1%)
    pallas_call x7, Pallas kernels, call(): pl.pallas_call(body, name=name, out_shape=[jax.ShapeDtypeStruct(out[0], o...  394 us
  transfers between devices with their start and end apart: 1, of which 0 were waited for; matrix products, arithmetic and copies ran while one was open for 0% of the time, Pallas kernels for 29%

profile of v4, /device:TPU:0, one launch (start us, length us, event | category | flops | bytes accessed | tf_op | source)
XLA Modules:
  0.0 419.8 jit_solution(7659196704687041202)
XLA Ops:
  7.2 0.7 copy.41
  8.1 0.8 constant_dynamic-slice_fusion.2
  9.0 0.1 reshape.141
  9.2 0.8 copy.38.segq_ref
  10.0 0.2 copy.37
  10.2 0.7 stack.8.same_ref
  10.9 0.8 dynamic-slice_convert_fusion
  11.6 0.1 convert_element_type.39
  11.7 0.8 slice_bitcast_fusion
  12.5 0.6 tile.24.qg_ref
  13.1 0.6 tile.27.kg_ref
  13.7 2.1 copy.45
  15.8 1.2 multiply_sine_fusion
  17.0 80.5 %conv_forward.1 = (bf16[256,1536]{1,0:T(8,128)(2,1)}, bf16[256,1536]{1,0:T(8,128)(2,1)}, bf16[256,1536]{1,0:T(8,128)(2,1)}, f32[3,256,384]{2,1,0:T(8,128)}, f32[...) custom-call(bf16[1,4,128,1536]{3,2,1,0:T(8,128)(2,1)} %in_ref.1, ...), custom_call_target="tpu_custom_call" | custom-call | flops 5000000000 | bytes 209715200 | tf_op jit(solution)/shard_map/conv_forward/pallas_call | solution.py:262
  97.5 48.7 %attention_forward.1 = (f32[256,384]{1,0:T(8,128)}, f32[256,256]{1,0:T(8,128)}, bf16[256,384]{1,0:T(8,128)(2,1)}, bf16[8,256,256]{2,1,0:T(8,128)(2,1)}, bf16[256...) custom-call(bf16[256,1536]{1,0:T(8,128)(2,1)} %get-tuple-element.76.n3_ref, ...), custom_call_target="tpu_custom_call" | custom-call | flops 4000000000 | bytes 157286400 | tf_op jit(solution)/shard_map/attention_forward/pallas_call | solution.py:262
  146.2 52.1 %second_ffn.1 = (bf16[256,1536]{1,0:T(8,128)(2,1)}, f32[128,1536]{1,0:T(8,128)}, bf16[256,1536]{1,0:T(8,128)(2,1)}, f32[1,1536]{1,0:T(1,128)}, bf16[3,4,192,1792...) custom-call(bf16[256,1536]{1,0:T(8,128)(2,1)} %get-tuple-element.78.n4_ref, ...), custom_call_target="tpu_custom_call" | custom-call | flops 12000000000 | bytes 157286400 | tf_op jit(solution)/shard_map/second_ffn/pallas_call | solution.py:262
  198.3 67.2 %attention_backward.1 = (bf16[256,384]{1,0:T(8,128)(2,1)}, bf16[256,256]{1,0:T(8,128)(2,1)}, bf16[256,1536]{1,0:T(8,128)(2,1)}, f32[1,1536]{1,0:T(1,128)}, f32[8...) custom-call(bf16[256,1536]{1,0:T(8,128)(2,1)} %get-tuple-element.81.glow_ref.ghlow_ref, ...), custom_call_target="tpu_custom_call" | custom-call | flops 6000000000 | bytes 136314880 | tf_op jit(solution)/shard_map/attention_backward/pallas_call | solution.py:262
  265.6 53.3 %first_ffn_back.1 = (f32[128,1536]{1,0:T(8,128)}, bf16[256,1536]{1,0:T(8,128)(2,1)}, f32[1,1536]{1,0:T(1,128)}, bf16[3,4,192,1792]{3,2,1,0:T(8,128)(2,1)}, bf16[...) custom-call(bf16[256,1536]{1,0:T(8,128)(2,1)} %get-tuple-element.89.gm_ref, ...), custom_call_target="tpu_custom_call" | custom-call | flops 8999999488 | bytes 157286400 | tf_op jit(solution)/shard_map/first_ffn_back/pallas_call | solution.py:262
  318.9 0.8 pad_maximum_fusion
  319.6 0.1 reshape.145
  319.8 0.1 reshape.146
  320.0 0.7 fusion.small_in
  320.8 83.2 %conv_backward.1 = (bf16[1,4,128,1536]{3,2,1,0:T(8,128)(2,1)}, f32[8,384]{1,0:T(8,128)}, bf16[192,384]{1,0:T(8,128)(2,1)}, bf16[192,640]{1,0:T(8,128)(2,1)}, bf1...) custom-call(bf16[256,1536]{1,0:T(8,128)(2,1)} %get-tuple-element.95., ...), custom_call_target="tpu_custom_call" | custom-call | flops 5000000000 | bytes 314572800 | tf_op jit(solution)/shard_map/conv_backward/pallas_call | solution.py:262
  404.0 8.7 %results.1 = (bf16[1,4,128,1536]{3,2,1,0:T(8,128)(2,1)}, f32[2,192]{1,0:T(2,128)}, f32[3,192,384]{2,1,0:T(8,128)}, f32[3,384]{1,0:T(4,128)}, f32[192,384]{1,0:T(...) custom-call(bf16[1,4,128,1536]{3,2,1,0:T(8,128)(2,1)} %get-tuple-ele, ...), custom_call_target="tpu_custom_call" | custom-call | bytes 26214400 | tf_op jit(solution)/shard_map/results/pallas_call | solution.py:262
  (28 shorter events, 0.7 us)
Async XLA Ops:
  7.2 313.6 %all-reduce.5.cloned.1.call-start = ((), (), s32[]{:S(2)}) async-start(), calls=%async_computation | async-start | bytes 1572864 | tf_op jit(solution)/shard_map/psum | solution.py:915
  265.6 53.3 %copy-start = (f32[1,1536]{1,0:T(1,128)S(1)}, f32[1,1536]{1,0:T(1,128)}, u32[]{:S(2)}) copy-start(f32[1,1536]{1,0:T(1,128)} %get-tuple-element.108) | copy-start | bytes 18436
  265.6 53.3 %copy-start.1 = (f32[1,1536]{1,0:T(1,128)S(1)}, f32[1,1536]{1,0:T(1,128)}, u32[]{:S(2)}) copy-start(f32[1,1536]{1,0:T(1,128)} %get-tuple-element.107) | copy-start | bytes 18436
  265.6 54.2 %copy-start.2 = (f32[8,128]{1,0:T(8,128)S(1)}, f32[8,128]{1,0:T(8,128)}, u32[]{:S(2)}) copy-start(f32[8,128]{1,0:T(8,128)} %get-tuple-element.109) | copy-start | bytes 12292
Sparse Core Ops, SparseCore 0:
  198.4 49.9 all-reduce.4

commit v5 on v4

--- a/solution.py
+++ b/solution.py
@@ -255,20 +255,76 @@
     return grad_raw, jnp.sum(back * raw * scale, 0, keepdims=True)
 
 
+LAZY = "lazy"
+LATE = "late"
+
+
+class Moves:
+    def __init__(self, incoming, leaving):
+        self.incoming, self.leaving, self.left = incoming, leaving, []
+        for _, copy in incoming:
+            copy.start()
+
+    def ready(self, *refs):
+        for ref in refs:
+            for known, copy in self.incoming:
+                if known is ref:
+                    copy.wait()
+
+    def leave(self, *refs):
+        for ref in refs:
+            for known, copy in self.leaving:
+                if known is ref:
+                    copy.start()
+                    self.left.append(copy)
+
+    def finish(self):
+        wait_all(self.left)
+
+
 def call(body, name, collective, outs, scratch, args, flops=0, moved=0):
     params = dict(vmem_limit_bytes=60 << 20)
     if collective is not None:
         params.update(collective_id=collective, has_side_effects=True)
+    lazy = [n for n, arg in enumerate(args) if isinstance(arg, tuple) and arg[1] is LAZY]
+    late = [n for n, out in enumerate(outs) if len(out) > 2 and out[2] is LATE]
+    arrays = [arg[0] if isinstance(arg, tuple) else arg for arg in args]
+    extra = [pltpu.VMEM(arrays[n].shape, arrays[n].dtype) for n in lazy]
+    extra += [pltpu.VMEM(outs[n][0], outs[n][1]) for n in late]
+    moves = len(lazy) + len(late)
+    if moves:
+        extra.append(pltpu.SemaphoreType.DMA((moves,)))
+
+    def whole(*refs):
+        refs = list(refs)
+        held = refs[len(refs) - len(extra) :]
+        refs = refs[: len(refs) - len(extra)]
+        incoming, leaving = [], []
+        for at, n in enumerate(lazy):
+            incoming.append((held[at], pltpu.make_async_copy(refs[n], held[at], held[-1].at[at])))
+            refs[n] = held[at]
+        for at, n in enumerate(late):
+            place_at = len(args) + n
+            kept = held[len(lazy) + at]
+            leaving.append((kept, pltpu.make_async_copy(kept, refs[place_at], held[-1].at[len(lazy) + at])))
+            refs[place_at] = kept
+        travel = Moves(incoming, leaving)
+        body(*refs, travel)
+        travel.finish()
+
+    def spec(mark):
+        return ANY if mark is LAZY or mark is LATE else mark
+
     results = pl.pallas_call(
-        body,
+        whole,
         name=name,
         out_shape=[jax.ShapeDtypeStruct(out[0], out[1]) for out in outs],
-        in_specs=[arg[1] if isinstance(arg, tuple) else VMEM for arg in args],
-        out_specs=[out[2] if len(out) > 2 else VMEM for out in outs],
-        scratch_shapes=list(scratch),
+        in_specs=[spec(arg[1]) if isinstance(arg, tuple) else VMEM for arg in args],
+        out_specs=[spec(out[2]) if len(out) > 2 else VMEM for out in outs],
+        scratch_shapes=list(scratch) + extra,
         compiler_params=pltpu.CompilerParams(**params),
         cost_estimate=pl.CostEstimate(flops=flops, bytes_accessed=moved, transcendentals=0),
-    )(*[arg[0] if isinstance(arg, tuple) else arg for arg in args])
+    )(*arrays)
     return list(results)
 
 
@@ -379,7 +435,7 @@
         in_ref, same_ref, gain_ref, win_ref, kernel_ref, wout_ref, attn_gain_ref, up_hbm, down_hbm,
         x_ref, g_ref, n1_ref, pc_ref, edge_ref, y_ref, h1_ref, n2_ref, f1_ref, a1_ref, m_ref, n3_ref,
         other, edges, normed_edges, ext, swap_send, swap_recv, edge_send, edge_recv, up_ref, down_ref, weight_sems, acc,
-        part, inbox, rs, rr, gs, gr, inbox2, rs2, rr2, gs2, gr2,
+        part, inbox, rs, rr, gs, gr, inbox2, rs2, rr2, gs2, gr2, travel,
     ):
         where = place()
         s, q, h = where
@@ -414,6 +470,7 @@
             far_edge = jnp.where(q == 0, before, edges[1, m])
             edge = jnp.where(first, far_edge, edges[0, m]).astype(FLOAT)
             normed_edges[m * 16 : (m + 1) * 16, :] = norm_apply(edge, gain_ref[0:1, :]).astype(HALF)
+        travel.ready(win_ref)
         for k in range(3):
             pc_ref[k] = product(n1_ref[...], win_ref[k])
         edge_b = product(normed_edges[...], win_ref[0])
@@ -432,7 +489,9 @@
                 + kernel_ref[0:1, :] * jnp.where(same_ref[span, 1:2] > 0, shifted_rows(ext, m, 2), 0.0)
             )
             y_ref[span, :] = (pc_ref[1, span, :] * mixed).astype(HALF)
+        travel.ready(wout_ref)
         part[...] = product(y_ref[...], wout_ref[...]).astype(HALF)
+        travel.leave(x_ref, g_ref, n1_ref, pc_ref, edge_ref, y_ref)
 
         def finish(flow, i, total):
             hidden = x_ref[own_rows(flow, i), :].astype(FLOAT) + total
@@ -440,6 +499,7 @@
             return norm_apply(hidden, gain_ref[1:2, :]).astype(HALF)
 
         head_total(part, n2_ref, inbox, rs, rr, gs, gr, where, heads, finish)
+        travel.leave(h1_ref, n2_ref)
         for j, (start, count) in enumerate(slabs):
             wait_all(weights[3 * j : 3 * j + 3])
             span = slice(start, start + count)
@@ -455,6 +515,7 @@
             else:
                 acc[...] += term
         part[...] = acc[...].astype(HALF)
+        travel.leave(f1_ref, a1_ref)
 
         def finish_middle(flow, i, total):
             middle = (h1_ref[kept_rows(i), :] + total).astype(HALF).astype(FLOAT)
@@ -468,16 +529,16 @@
         "conv_forward",
         0,
         [
-            ((tokens, width), HALF),
-            ((tokens, width), HALF),
-            ((tokens, width), HALF),
-            ((3, tokens, channels), FLOAT),
-            ((micro, 8, channels), FLOAT),
-            ((tokens, channels), HALF),
-            ((half_tokens, width), FLOAT),
-            ((tokens, width), HALF),
-            ((2, tokens, hidden_units), FLOAT),
-            ((tokens, hidden_units), HALF),
+            ((tokens, width), HALF, LATE),
+            ((tokens, width), HALF, LATE),
+            ((tokens, width), HALF, LATE),
+            ((3, tokens, channels), FLOAT, LATE),
+            ((micro, 8, channels), FLOAT, LATE),
+            ((tokens, channels), HALF, LATE),
+            ((half_tokens, width), FLOAT, LATE),
+            ((tokens, width), HALF, LATE),
+            ((2, tokens, hidden_units), FLOAT, LATE),
+            ((tokens, hidden_units), HALF, LATE),
             ((half_tokens, width), FLOAT),
             ((tokens, width), HALF),
         ],
@@ -496,7 +557,7 @@
         + part_scratch
         + total_scratch
         + total_scratch,
-        [incoming, same, conv_gains, w_in, conv_kernel, conv_out, attn_gains, (first_up, ANY), (conv_down, ANY)],
+        [incoming, same, conv_gains, (w_in, LAZY), conv_kernel, (conv_out, LAZY), attn_gains, (first_up, ANY), (conv_down, ANY)],
         flops=5 * 10**9,
         moved=200 << 20,
     )
@@ -535,9 +596,9 @@
     def half_rows(side):
         return slice(side * half_share, (side + 1) * half_share)
 
-    def combine(passing, arrived, where):
+    def combine(passing, arrived, where, own=None):
         for i, (_, _, sources, _) in enumerate(passed_blocks(where)):
-            total = passing(i)[...].astype(FLOAT)
+            total = (passing if own is None else own)(i)[...].astype(FLOAT)
             for source in sources:
                 total = total + arrived[source].astype(FLOAT)
             passing(i)[...] = total.astype(HALF)
@@ -598,6 +659,69 @@
             copies += sends
         return copies
 
+    small_rows = tokens // heads
+    widths = [query_width, query_width + pair_width, channels, 3 * channels]
+
+    def head_others(where):
+        s, q, h = where
+        return [(s, q, lax.rem(h + k, heads)) for k in range(1, heads)]
+
+    def mixer_sends(stages, incomes, send, recv, where):
+        return [
+            first_stage(
+                lambda dest, side, stage=stage: stage.at[dest, half_rows(side)],
+                lambda i, income=income: income.at[i],
+                send.at[k],
+                recv.at[k],
+                where,
+            )
+            for k, (stage, income) in enumerate(zip(stages, incomes))
+        ]
+
+    def mixer_steps(formers, latters, stages, given, former, halves, swaps, sends):
+        def step(t):
+            for k in range(len(formers)):
+
+                @pl.when(t == 2 * k)
+                def _(k=k):
+                    halves[k].wait()
+                    former[...] = transposed(formers[k], given.at[k])
+
+                @pl.when(t == 2 * k + 1)
+                def _(k=k):
+                    swaps[k].wait()
+                    result = product(former[...], latters[k][...]).astype(HALF)
+                    stages[k][...] = result.reshape(seqs, share, result.shape[1])
+                    start_all(sends[k])
+
+        return step
+
+    def mixer_second(stages, incomes, passes, turns, send, recv, where):
+        blocks = passed_blocks(where)
+        turning = []
+        for k, (stage, income, passed, turn) in enumerate(zip(stages, incomes, passes, turns)):
+
+            def own_block(i, stage=stage):
+                return stage.at[blocks[i][0], half_rows(blocks[i][1])]
+
+            def moved(i, stage=stage, passed=passed):
+                return own_block(i, stage) if passed is None else passed.at[i]
+
+            combine(moved, income, where, own_block)
+            sends = second_stage(moved, turn, send.at[k], recv.at[k], where)
+            start_all(sends)
+            turning.append(sends)
+        return turning
+
+    def latter_swaps(latters, send, recv, partner):
+        return [
+            remote(latter.at[0:tokens], latter.at[tokens : 2 * tokens], send.at[k], recv.at[k], partner)
+            for k, latter in enumerate(latters)
+        ]
+
+    def first_sums(count):
+        return [((first_blocks, half_share, size), HALF) for size in count]
+
     def transposed(array_ref, given_ref):
         start = pl.multiple_of(lax.axis_index("section") * half_model, 128)
         own = array_ref[:, pl.ds(start, half_model)]
@@ -622,7 +746,7 @@
             (1 - s, q, h),
         )
 
-    def gradient_tiles(former, latter, stage, partial_hbm, first_in, local_sems, send, recv, where):
+    def gradient_tiles(former, latter, stage, partial_hbm, first_in, local_sems, send, recv, where, kinds):
         def split(t):
             kind = lax.div(t, tiles)
             at = lax.rem(t, tiles)
@@ -650,7 +774,7 @@
             result = product(former[use], latter[kind, :, columns]).astype(HALF)
             stage[kind, :, :, columns] = result.reshape(seqs, share, tile_width)
 
-            @pl.when(t < 2 * tiles)
+            @pl.when(t < kinds * tiles)
             def _():
                 start_all(sent(t))
 
@@ -663,7 +787,7 @@
                     stored(t, dest).wait()
 
             loop(3 * tiles, stored_all)
-            loop(2 * tiles, lambda t: wait_all(sent(t)))
+            loop(kinds * tiles, lambda t: wait_all(sent(t)))
 
         return tile, finish
 
@@ -678,10 +802,11 @@
         pltpu.SemaphoreType.DMA((3, len(slabs))),
         pltpu.SemaphoreType.DMA((3, len(slabs))),
         pltpu.SemaphoreType.DMA((3 * tiles, seqs)),
-        pltpu.SemaphoreType.DMA((2 * tiles, first_blocks)),
-        pltpu.SemaphoreType.DMA((2 * tiles, first_blocks)),
+        pltpu.SemaphoreType.DMA((3 * tiles, first_blocks)),
+        pltpu.SemaphoreType.DMA((3 * tiles, first_blocks)),
     ]
-    partial_outs = [((3, seqs, share, padded_units), HALF, ANY), first_shape(2)]
+    def partial_outs(kinds):
+        return [((3, seqs, share, padded_units), HALF, ANY), first_shape(kinds)]
 
 
     def slot_peer(me, j, h):
@@ -746,7 +871,7 @@
     def attention_forward(
         n3_ref, wq_ref, wp_ref, cos_ref, sin_ref, qg_ref, kg_ref, segq_ref, seg_ref, wo_ref, m_ref, gain_ref,
         qr_ref, r_ref, q_ref, all_ref, o_ref, h2_ref, n4_ref,
-        send, recv, near_send, near_recv, part, inbox, rs, rr, gs, gr,
+        send, recv, near_send, near_recv, part, inbox, rs, rr, gs, gr, travel,
     ):
         where = place()
         s, q, h = where
@@ -760,11 +885,14 @@
             all_ref[me, :, span] = rotary(r_ref[:, span], kg_ref[...], cos, sin).astype(HALF)
         all_ref[me, :, half_pair:] = r_ref[:, half_pair:].astype(HALF)
         pass_on = gather_pairs(all_ref, me, where, send, recv, near_send, near_recv)
+        travel.ready(wq_ref)
         qr_ref[...] = product(n3_ref[...], wq_ref[...])
         for start, size in chunks_of(query_width):
             span = slice(start, start + size)
             q_ref[:, span] = rotary(qr_ref[:, span], qg_ref[...], cos, sin).astype(HALF)
+        travel.leave(r_ref, qr_ref, q_ref)
         pass_on()
+        travel.leave(all_ref)
         for m in range(micro):
             biases = [allowed_pairs(segq_ref, seg_ref, m, at, s, q) for at in range(m + 1)]
             results = []
@@ -777,6 +905,8 @@
                 )
                 results += [total[r * rows : (r + 1) * rows] for r in range(group)]
             o_ref[m * rows : (m + 1) * rows, :] = jnp.concatenate(results, -1).astype(HALF)
+        travel.leave(o_ref)
+        travel.ready(wo_ref, m_ref)
         part[...] = product(o_ref[...], wo_ref[...]).astype(HALF)
 
         def finish(flow, i, total):
@@ -791,18 +921,18 @@
         "attention_forward",
         2,
         [
-            ((tokens, query_width), FLOAT),
-            ((tokens, pair_width), FLOAT),
-            ((tokens, query_width), HALF),
-            ((slots, tokens, pair_width), HALF),
-            ((tokens, query_width), HALF),
+            ((tokens, query_width), FLOAT, LATE),
+            ((tokens, pair_width), FLOAT, LATE),
+            ((tokens, query_width), HALF, LATE),
+            ((slots, tokens, pair_width), HALF, LATE),
+            ((tokens, query_width), HALF, LATE),
             ((half_tokens, width), FLOAT),
             ((tokens, width), HALF),
         ],
         [dma(seqs - 1), dma(seqs - 1), dma(seqs), dma(seqs)] + part_scratch + total_scratch,
         [
-            n3, w_query, w_pair, cosine, sine, query_gain, key_gain, local_segments, segment_ids,
-            attn_out, middle, attn_gains,
+            n3, (w_query, LAZY), w_pair, cosine, sine, query_gain, key_gain, local_segments, segment_ids,
+            (attn_out, LAZY), (middle, LAZY), attn_gains,
         ],
         flops=4 * 10**9,
         moved=150 << 20,
@@ -819,7 +949,7 @@
         n4_ref, g_ref, h2_ref, gain_ref, up_hbm, down_hbm,
         py_ref, gh2_ref, low_ref, gg_ref, partial_hbm, first_in,
         acc_y, up_ref, down_ref, weight_sems, acc, given, former, latter, stage, hs, hr, ls, lr, local_sems, ts, tr,
-        part, inbox, rs, rr, gs, gr,
+        part, inbox, rs, rr, gs, gr, travel,
     ):
         where = place()
         s, q, h = where
@@ -861,6 +991,7 @@
                 acc_y[...] += term_y
         part[...] = acc[...].astype(HALF)
 
+        travel.ready(h2_ref)
         for flow, holder in ((0, 0), (1, heads - 1)):
 
             @pl.when(h == holder)
@@ -868,8 +999,9 @@
                 acc_y[flow * half_tokens : (flow + 1) * half_tokens, :] += h2_ref[...]
 
         py_ref[...] = acc_y[...].astype(HALF)
+        travel.leave(py_ref)
         tile, tiles_done = gradient_tiles(
-            former, latter, stage, partial_hbm, first_in, local_sems, ts, tr, where
+            former, latter, stage, partial_hbm, first_in, local_sems, ts, tr, where, 2
         )
 
         def filler(t):
@@ -901,25 +1033,25 @@
         "second_ffn",
         4,
         [
-            ((tokens, width), HALF),
+            ((tokens, width), HALF, LATE),
             ((half_tokens, width), FLOAT),
             ((tokens, width), HALF),
             ((1, width), FLOAT),
         ]
-        + partial_outs,
+        + partial_outs(2),
         [pltpu.VMEM((tokens, width), FLOAT)] + ffn_scratch + part_scratch + total_scratch,
-        [n4, g, h2, attn_gains, (second_up, ANY), (attn_down, ANY)],
+        [n4, g, (h2, LAZY), attn_gains, (second_up, ANY), (attn_down, ANY)],
         flops=12 * 10**9,
         moved=150 << 20,
     )
-    yout = lax.psum(part_y, "head")
     def attention_backward(
         glow_ref, wo_ref, q_ref, all_ref, segq_ref, seg_ref,
-        qr_ref, r_ref, cos_ref, sin_ref, qg_ref, kg_ref, wq_ref, wp_ref, m_ref, gh2_ref, gain_ref, partial2_hbm, first2_hbm,
-        bq_ref, br_ref, low_ref, gg_ref, gqk_ref, second_in, first_in,
-        grads, totals, gq_ref, gp_ref, near_slots, pair_slots, ns, nr, ps, pr,
+        qr_ref, r_ref, cos_ref, sin_ref, qg_ref, kg_ref, wq_ref, wp_ref, m_ref, gh2_ref, gain_ref, py_ref, n3_ref, o_ref, partial2_hbm, first2_hbm,
+        low_ref, gg_ref, gqk_ref, yown_ref, stage0, stage1, in0, in1, second_in, first_in,
+        bq_ref, br_ref, grads, totals, gq_ref, gp_ref, near_slots, pair_slots, ns, nr, ps, pr,
         passing, held, load_sems, vs, vr, fs, fr,
-        part, inbox, rs, rr, gs, gr,
+        ybox, ys, yr, given, former, latter0, latter1, hs, hr, ls, lr, ms, mr,
+        part, inbox, rs, rr, gs, gr, travel,
     ):
         where = place()
         s, q, h = where
@@ -927,9 +1059,22 @@
         peers = seq_peers(where, seqs)
         loads = pass_loads(partial2_hbm, (0, 1), first2_hbm, passing, held, load_sems, where)
         start_all(loads)
-        greet([partner] + peers, where, heads)
+        others = head_others(where)
+        latters = [latter0, latter1]
+        greet([partner] + peers + others, where, heads)
         wait_all(loads)
         travelling = pass_sends(2, passing, held, second_in, vs, vr, where)
+        travel.ready(py_ref, n3_ref, o_ref)
+        latter0[0:tokens, :] = o_ref[...]
+        ysends = [
+            remote(py_ref.at[rows_of(peer[2], small_rows)], ybox.at[n], ys.at[n], yr.at[n], peer)
+            for n, peer in enumerate(others)
+        ]
+        start_all(ysends)
+        halves = half_swaps([glow_ref, n3_ref], [given.at[0], given.at[1]], hs, hr, where)
+        start_all(halves)
+        swaps = latter_swaps(latters, ls, lr, partner)
+        swaps[0].start()
         gg_ref[...] = jnp.zeros_like(gg_ref)
         gqk_ref[...] = jnp.zeros_like(gqk_ref)
         grads[...] = back_product(glow_ref[...], wo_ref[...]).astype(HALF)
@@ -971,9 +1116,9 @@
             copy = remote(gp_ref.at[other * sections + 1 - s], near_slots.at[other], ns.at[other], nr.at[other], partner)
             copy.start()
             near.append(copy)
-        cos, sin = cos_ref[...], sin_ref[...]
         copies = []
         wait_all(near)
+        travel.ready(qr_ref, r_ref, cos_ref, sin_ref, wq_ref, wp_ref, m_ref, gh2_ref)
         for other in range(seqs):
             mine = gp_ref[other * sections + s].astype(FLOAT)
             near_slots[other] = (mine + near_slots[other].astype(FLOAT)).astype(HALF)
@@ -986,6 +1131,7 @@
         )
         start_all(later)
         travelling += later
+        cos, sin = cos_ref[...], sin_ref[...]
         for start, size in chunks_of(query_width):
             span = slice(start, start + size)
             grad_raw, grad_gain = rotary_back(qr_ref[:, span], qg_ref[...], cos, sin, gq_ref[:, span])
@@ -1003,30 +1149,46 @@
             br_ref[:, span] = grad_raw.astype(HALF)
             gqk_ref[1:2, :size] += grad_gain
         br_ref[:, half_pair:] = grad_pair[:, half_pair:].astype(HALF)
+        latter1[0:tokens, 0:query_width] = bq_ref[...]
+        latter1[0:tokens, query_width:] = br_ref[...]
+        swaps[1].start()
         part[...] = (partial + back_product(br_ref[...], wp_ref[...])).astype(HALF)
+        wait_all(ysends)
+        produced = py_ref[rows_of(h, small_rows), :].astype(FLOAT)
+        for n in range(heads - 1):
+            produced = produced + ybox[n].astype(FLOAT)
+        yown_ref[...] = produced.astype(HALF)
+        sends = mixer_sends([stage0, stage1], [in0, in1], ms, mr, where)
+        mixer_step = mixer_steps([glow_ref, n3_ref], latters, [stage0, stage1], given, former, halves, swaps, sends)
 
         def finish(flow, i, total):
             grad_entry, grad_gain = norm_back(m_ref[kept_rows(i), :], gain_ref[0:1, :], total)
             gg_ref[...] += grad_gain
             return (gh2_ref[kept_rows(i), :] + grad_entry).astype(HALF)
 
-        head_total(part, low_ref, inbox, rs, rr, gs, gr, where, heads, finish)
+        head_total(part, low_ref, inbox, rs, rr, gs, gr, where, heads, finish, mixer_step, 4)
+        for copies in sends:
+            wait_all(copies)
         wait_all(travelling)
 
-    (bq, br, gm_low, grad_gain_attn0, grad_qk, second2, first2_last) = call(
+    (gm_low, grad_gain_attn0, grad_qk, y_own, stage0, stage1, in0, in1, second2, first2_last) = call(
         attention_backward,
         "attention_backward",
         5,
         [
-            ((tokens, query_width), HALF),
-            ((tokens, pair_width), HALF),
             ((tokens, width), HALF),
             ((1, width), FLOAT),
             ((8, 128), FLOAT),
+            ((small_rows, width), HALF),
+            ((seqs, share, widths[0]), HALF),
+            ((seqs, share, widths[1]), HALF),
+            *first_sums(widths[:2]),
             second_shape(2),
             first_shape(1),
         ],
         [
+            pltpu.VMEM((tokens, query_width), HALF),
+            pltpu.VMEM((tokens, pair_width), HALF),
             pltpu.VMEM((tokens, query_width), HALF),
             pltpu.VMEM((micro, 2 * kv_local, block_tok, head_width), FLOAT),
             pltpu.VMEM((tokens, query_width), FLOAT),
@@ -1040,23 +1202,39 @@
         ]
         + passing_scratch(2)
         + [dma(first_blocks), dma(first_blocks)]
+        + [
+            pltpu.VMEM((heads - 1, small_rows, width), HALF),
+            dma(heads - 1),
+            dma(heads - 1),
+            pltpu.VMEM((2, tokens, half_model), HALF),
+            pltpu.VMEM((half_model, 2 * tokens), HALF),
+            pltpu.VMEM((2 * tokens, widths[0]), HALF),
+            pltpu.VMEM((2 * tokens, widths[1]), HALF),
+            dma(2),
+            dma(2),
+            dma(2),
+            dma(2),
+            dma_grid(2, first_blocks),
+            dma_grid(2, first_blocks),
+        ]
         + part_scratch
         + total_scratch,
         [
             gh2_low, attn_out, queries, all_pairs, local_segments, segment_ids,
-            query_raw, pair_raw, cosine, sine, query_gain, key_gain, w_query, w_pair, middle, gh2, attn_gains,
-            (partial2, ANY), (first2, ANY),
+            (query_raw, LAZY), (pair_raw, LAZY), (cosine, LAZY), (sine, LAZY), query_gain, key_gain,
+            (w_query, LAZY), (w_pair, LAZY), (middle, LAZY), (gh2, LAZY), attn_gains,
+            (part_y, LAZY), (n3, LAZY), (attended, LAZY), (partial2, ANY), (first2, ANY),
         ],
         flops=6 * 10**9,
         moved=130 << 20,
     )
 
     def first_ffn_back(
-        gm_ref, n2_ref, f1_ref, a1_ref, h1_ref, gain_ref, up_hbm, down_hbm, partial2_hbm, first2_hbm,
-        gh1_ref, low_ref, gg_ref, partial_hbm, first_in, second_in,
+        gm_ref, n2_ref, f1_ref, a1_ref, h1_ref, gain_ref, yown_ref, stage0, stage1, in0, in1, up_hbm, down_hbm, partial2_hbm, first2_hbm,
+        gh1_ref, low_ref, gg_ref, yout_ref, turn0, turn1, partial_hbm, first_in, second_in,
         up_ref, down_ref, weight_sems, acc, given, former, latter, stage, hs, hr, ls, lr, local_sems, ts, tr,
-        passing, held, load_sems, vs, vr,
-        part, inbox, rs, rr, gs, gr,
+        passing, held, load_sems, vs, vr, ys, yr, pass0, pass1, us, ur,
+        part, inbox, rs, rr, gs, gr, travel,
     ):
         where = place()
         s, q, h = where
@@ -1065,14 +1243,33 @@
         start_all(loads)
         start_all(weights)
         clear_padding(latter)
-        latter[0, 0:tokens, 0:hidden_units] = a1_ref[...]
-        greet([(1 - s, q, h)] + seq_peers(where, seqs), where, heads)
+        others = head_others(where)
+        own_y = rows_of(h, small_rows)
+        greet([(1 - s, q, h)] + seq_peers(where, seqs) + others, where, heads)
+        travel.ready(yown_ref, n2_ref, a1_ref)
+        yout_ref[own_y, :] = yown_ref[...]
+        ysends = [
+            remote(yout_ref.at[own_y], yout_ref.at[own_y], ys.at[n], yr.at[n], peer) for n, peer in enumerate(others)
+        ]
+        start_all(ysends)
         wait_all(loads)
         travelling = pass_sends(1, passing, held, second_in, vs, vr, where)
         halves = half_swaps([gm_ref, n2_ref], [given.at[0], given.at[1]], hs, hr, where)
         start_all(halves)
         gg_ref[...] = jnp.zeros_like(gg_ref)
+        latter[0, 0:tokens, 0:hidden_units] = a1_ref[...]
+        travel.ready(stage0, stage1, in0, in1)
+        turning = mixer_second([stage0, stage1], [in0, in1], [pass0, pass1], [turn0, turn1], us, ur, where)
+        tile, tiles_done = gradient_tiles(
+            former, latter, stage, partial_hbm, first_in, local_sems, ts, tr, where, 3
+        )
+        active_swaps = [
+            latter_swap(latter, 0, start, slab_width(start, count), ls.at[0, j], lr.at[0, j], where)
+            for j, (start, count) in enumerate(slabs)
+        ]
+        start_all(active_swaps)
         swaps = []
+        travel.ready(f1_ref, h1_ref)
         for j, (start, count) in enumerate(slabs):
             wait_all(weights[3 * j : 3 * j + 3])
             span = slice(start, start + count)
@@ -1084,7 +1281,7 @@
             grad_rise = (grad_active * (gate * chance)).astype(HALF)
             latter[1, 0:tokens, span] = grad_gate
             latter[2, 0:tokens, span] = grad_rise
-            for kind in range(3):
+            for kind in range(1, 3):
                 swap = latter_swap(
                     latter, kind, start, slab_width(start, count), ls.at[kind, j], lr.at[kind, j], where
                 )
@@ -1093,26 +1290,23 @@
             term = product(grad_gate, up_ref[0, span, :]) + product(grad_rise, up_ref[1, span, :])
             if j == 0:
                 acc[...] = term
+                halves[0].wait()
+                wait_all(active_swaps)
+                former[0] = transposed(gm_ref, given.at[0])
+                loop(tiles, tile)
             else:
                 acc[...] += term
         part[...] = acc[...].astype(HALF)
-        tile, tiles_done = gradient_tiles(
-            former, latter, stage, partial_hbm, first_in, local_sems, ts, tr, where
-        )
-
         def filler(t):
-            for k, array_ref in enumerate((gm_ref, n2_ref)):
-
-                @pl.when(t == k)
-                def _(k=k, array_ref=array_ref):
-                    halves[k].wait()
-                    if k:
-                        wait_all(swaps)
-                    former[k] = transposed(array_ref, given.at[k])
-
-            @pl.when(t >= 2)
+            @pl.when(t == 0)
             def _():
-                tile(t - 2)
+                halves[1].wait()
+                wait_all(swaps)
+                former[1] = transposed(n2_ref, given.at[1])
+
+            @pl.when(t >= 1)
+            def _():
+                tile(tiles + t - 1)
 
         def finish(flow, i, total):
             grad_hidden, grad_gain = norm_back(h1_ref[kept_rows(i), :], gain_ref[1:2, :], total)
@@ -1121,34 +1315,43 @@
             gh1_ref[kept_rows(i), :] = grad
             return grad.astype(HALF)
 
-        head_total(part, low_ref, inbox, rs, rr, gs, gr, where, heads, finish, filler, 3 * tiles + 2)
+        head_total(part, low_ref, inbox, rs, rr, gs, gr, where, heads, finish, filler, 2 * tiles + 1)
         tiles_done()
         wait_all(travelling)
-
-    (gh1, gh1_low, grad_gain_conv1, partial1, first1, second2_last) = call(
+        wait_all(ysends)
+        for copies in turning:
+            wait_all(copies)
+
+    (gh1, gh1_low, grad_gain_conv1, yout, turn0, turn1, partial1, first1, second2_last) = call(
         first_ffn_back,
         "first_ffn_back",
         6,
-        [((half_tokens, width), FLOAT), ((tokens, width), HALF), ((1, width), FLOAT)] + partial_outs + [second_shape(1)],
-        ffn_scratch + passing_scratch(1) + part_scratch + total_scratch,
-        [gm_low, n2, f1, a1, h1, conv_gains, (first_up, ANY), (conv_down, ANY), (partial2, ANY), (first2_last, ANY)],
+        [((half_tokens, width), FLOAT), ((tokens, width), HALF), ((1, width), FLOAT), ((tokens, width), HALF)]
+        + [((grid_rows, half_share, size), HALF) for size in widths[:2]]
+        + partial_outs(3)
+        + [second_shape(1)],
+        ffn_scratch + passing_scratch(1)
+        + [dma(heads - 1), dma(heads - 1)]
+        + [pltpu.VMEM((grid_rows, half_share, size), HALF) for size in widths[:2]]
+        + [dma_grid(2, grid_rows), dma_grid(2, grid_rows)]
+        + part_scratch + total_scratch,
+        [gm_low, (n2, LAZY), (f1, LAZY), (a1, LAZY), (h1, LAZY), conv_gains, (y_own, LAZY),
+         (stage0, LAZY), (stage1, LAZY), (in0, LAZY), (in1, LAZY), (first_up, ANY), (conv_down, ANY), (partial2, ANY), (first2_last, ANY)],
         flops=9 * 10**9,
         moved=150 << 20,
     )
     small_width = max(share, channels, 2 * head_width)
-    widths = [query_width, query_width + pair_width, channels, 3 * channels]
 
     def conv_backward(
         low_ref, gh1_ref, pc_ref, edge_ref, same_ref, kernel_ref, wout_ref, win_ref, x_ref, gain_ref, yout_ref,
-        ghlow_ref, n3_ref, n1_ref, o_ref, bq_ref, br_ref, mixed_ref, small_in,
+        n1_ref, mixed_ref, stage0, stage1, in0, in1, turn0, turn1, small_in,
         partial1, partial2, first1, first2, first2_last, second2, second2_last,
         edges_ref, sums_ref, gout2_ref, gmix_ref, gout1_ref, gin_ref, gdown2, gup2, gdown1, gup1,
         bp_ref, ext, spread, gz_ext, outgoing, arrived, full, gg_ref, edge_send, edge_recv, swap_send, swap_recv,
-        given, former, latter0, latter1, latter2, latter3, stage0, stage1, stage2, stage3,
-        in0, in1, in2, in3, turn0, turn1, turn2, turn3, hs, hr, ls, lr, ms, mr, us, ur,
-        own_buf, first_buf, second_buf, passing, item_sems, vs, vr, fs, fr, down_stage, up_stage, out_sems,
+        given, former, latter2, latter3, stage2, stage3, in2, in3, turn2, turn3, hs, hr, ls, lr, ms, mr, us, ur,
+        own_buf, first_buf, second_buf, passing, item_sems, vs, vr, down_stage, up_stage, out_sems,
         packed, boxes, summed, final, zs, zr, ss, sr,
-        part, inbox, rs, rr, gs, gr,
+        part, inbox, rs, rr, gs, gr, travel,
     ):
         where = place()
         s, q, h = where
@@ -1156,11 +1359,11 @@
         partner = (1 - s, q, h)
         preceding = (1 - s, jnp.where(first, lax.rem(q + seqs - 1, seqs), q), h)
         following = (1 - s, jnp.where(first, q, lax.rem(q + 1, seqs)), h)
-        others = [(s, q, lax.rem(h + k, heads)) for k in range(1, heads)]
+        others = head_others(where)
         me = q * sections + s
         slot_peers = [slot_peer(me, j, h) for j in range(1, slots)]
         peers = seq_peers(where, seqs)
-        latters, stages = [latter0, latter1, latter2, latter3], [stage0, stage1, stage2, stage3]
+        latters, stages = [latter2, latter3], [stage0, stage1, stage2, stage3]
         incomes, turns = [in0, in1, in2, in3], [turn0, turn1, turn2, turn3]
         loads = []
         sources = [
@@ -1169,7 +1372,7 @@
             (partial2.at[2], first2_last.at[0], second2_last.at[0]),
             (partial1.at[0], first1.at[0], None),
             (partial1.at[1], first1.at[1], None),
-            (partial1.at[2], None, None),
+            (partial1.at[2], first1.at[2], None),
         ]
         for n, (partial, arrived_hbm, passed_hbm) in enumerate(sources):
             copies = [pltpu.make_async_copy(partial.at[q], own_buf.at[n], item_sems.at[n, 0])]
@@ -1183,17 +1386,12 @@
         for copies in loads[3:] + loads[:3]:
             start_all(copies)
         greet([partner, preceding, following] + others + slot_peers, where, heads)
-        latters[0][0:tokens, :] = o_ref[...]
-        latters[1][0:tokens, 0:query_width] = bq_ref[...]
-        latters[1][0:tokens, query_width:] = br_ref[...]
-        latters[2][0:tokens, :] = mixed_ref[...]
-        former_refs = [ghlow_ref, n3_ref, low_ref, n1_ref]
-        halves = half_swaps(former_refs, [given.at[k] for k in range(4)], hs, hr, where)
+        travel.ready(n1_ref, mixed_ref)
+        latter2[0:tokens, :] = mixed_ref[...]
+        halves = half_swaps([low_ref, n1_ref], [given.at[0], given.at[1]], hs, hr, where)
         start_all(halves)
-        swaps = [
-            remote(latters[k].at[0:tokens], latters[k].at[tokens : 2 * tokens], ls.at[k], lr.at[k], partner) for k in range(4)
-        ]
-        start_all(swaps[:3])
+        swaps = latter_swaps(latters, ls, lr, partner)
+        swaps[0].start()
         gg_ref[...] = jnp.zeros_like(gg_ref)
         gated = pc_ref[0] * pc_ref[2]
         grad_y = back_product(low_ref[...], wout_ref[...])
@@ -1213,7 +1411,7 @@
         edge = remote(outgoing, arrived, edge_send.at[0], edge_recv.at[0], preceding)
         edge.start()
         bulk = []
-        for n in (3, 4):
+        for n in (3, 4, 5):
             wait_all(loads[n])
             combine(lambda i, n=n: passing.at[n - 3, i], first_buf.at[n], where)
             sends = second_stage(
@@ -1221,10 +1419,6 @@
             )
             start_all(sends)
             bulk.append(sends)
-        last_first = first_stage(
-            lambda dest, side: partial1.at[2, dest, half_rows(side)], lambda i: first_buf.at[5, i], fs, fr, where
-        )
-        start_all(last_first)
         taps = [None, None, None]
         for m in range(micro):
             span = slice(m * rows, (m + 1) * rows)
@@ -1257,8 +1451,9 @@
             span = slice(m * rows, (m + 1) * rows)
             bp_ref[span, 0:channels] = (spread[m] * pc_ref[2, span, :]).astype(HALF)
             bp_ref[span, 2 * channels :] = (spread[m] * pc_ref[0, span, :]).astype(HALF)
-        latters[3][0:tokens, :] = bp_ref[...]
-        swaps[3].start()
+        latter3[0:tokens, :] = bp_ref[...]
+        swaps[1].start()
+        travel.ready(win_ref, x_ref, gh1_ref, yout_ref, small_in)
         total = back_product(bp_ref[:, 0:channels], win_ref[0])
         total = total + back_product(bp_ref[:, channels : 2 * channels], win_ref[1])
         total = total + back_product(bp_ref[:, 2 * channels :], win_ref[2])
@@ -1270,33 +1465,9 @@
             gg_ref[...] += grad_gain
             return (gh1_ref[kept_rows(i), :] + grad_start).astype(HALF)
 
-        mixer_sends = [
-            first_stage(
-                lambda dest, side, k=k: stages[k].at[dest, half_rows(side)],
-                lambda i, k=k: incomes[k].at[i],
-                ms.at[k],
-                mr.at[k],
-                where,
-            )
-            for k in range(4)
-        ]
-
-        def mixer_step(t):
-            for k in range(4):
-
-                @pl.when(t == 2 * k)
-                def _(k=k):
-                    halves[k].wait()
-                    former[...] = transposed(former_refs[k], given.at[k])
-
-                @pl.when(t == 2 * k + 1)
-                def _(k=k):
-                    swaps[k].wait()
-                    result = product(former[...], latters[k][...]).astype(HALF)
-                    stages[k][...] = result.reshape(seqs, share, widths[k])
-                    start_all(mixer_sends[k])
-
-        head_total(part, full, inbox, rs, rr, gs, gr, where, heads, finish, mixer_step, 8)
+        sent = mixer_sends(stages[2:], incomes[2:], ms, mr, where)
+        mixer_step = mixer_steps([low_ref, n1_ref], latters, stages[2:], given, former, halves, swaps, sent)
+        head_total(part, full, inbox, rs, rr, gs, gr, where, heads, finish, mixer_step, 4)
         keep = pl.ds(pl.multiple_of(s * rows, rows), rows)
         edges_ref[0, :, keep, :] = jnp.where(first, full[...], yout_ref[...]).reshape(micro, rows, width)
         part[...] = jnp.where(first, yout_ref[...], full[...])
@@ -1316,17 +1487,6 @@
             copy = remote(packed, boxes.at[k], zs.at[k], zr.at[k], peer)
             copy.start()
             over.append(copy)
-        def passed_on(n):
-            sends = second_stage(
-                lambda i: passing.at[n - 3, i], second_buf.at[n], vs.at[n - 3], vr.at[n - 3], where
-            )
-            start_all(sends)
-            bulk.append(sends)
-
-        wait_all(last_first)
-        wait_all(loads[5])
-        combine(lambda i: passing.at[2, i], first_buf.at[5], where)
-        passed_on(5)
         wait_all(over)
         over_heads = boxes[0]
         for j in range(1, heads - 1):
@@ -1359,20 +1519,11 @@
                 fill_stage(1 + kind, up_stage.at[0, kind])
             leave(up_stage.at[0], gup2, 1)
 
-        mixer_turns = []
-        for k in range(4):
-            wait_all(mixer_sends[k])
-            blocks = passed_blocks(where)
-
-            def passing_block(i, k=k):
-                return stages[k].at[blocks[i][0], half_rows(blocks[i][1])]
-
-            combine(passing_block, incomes[k], where)
-            sends = second_stage(passing_block, turns[k], us.at[k], ur.at[k], where)
-            start_all(sends)
-            mixer_turns.append(sends)
-            if k == 1:
-                second_half_items()
+        for copies in sent:
+            wait_all(copies)
+        mixer_turns = mixer_second(stages[2:], incomes[2:], [None, None], turns[2:], us, ur, where)
+        travel.ready(stage0, stage1, in0, in1, turn0, turn1)
+        second_half_items()
         for n in (3, 4, 5):
             wait_all(bulk[n - 3])
             if n == 3:
@@ -1388,7 +1539,8 @@
             total = total + final[j]
         sums_ref[...] = total
         for k, target in enumerate((gout2_ref, gmix_ref, gout1_ref, None)):
-            wait_all(mixer_turns[k])
+            if k >= 2:
+                wait_all(mixer_turns[k - 2])
             for side, value in enumerate(two_halves(stages[k].at[q], incomes[k], turns[k], where)):
                 value = value.astype(HALF)
                 if target is None:
@@ -1444,22 +1596,22 @@
             dma(1),
             dma(micro),
             dma(micro),
-            pltpu.VMEM((4, tokens, half_model), HALF),
+            pltpu.VMEM((2, tokens, half_model), HALF),
             pltpu.VMEM((half_model, 2 * tokens), HALF),
         ]
-        + [pltpu.VMEM((2 * tokens, size), HALF) for size in widths]
-        + [pltpu.VMEM((seqs, share, size), HALF) for size in widths]
-        + [pltpu.VMEM((first_blocks, half_share, size), HALF) for size in widths]
-        + [pltpu.VMEM((grid_rows, half_share, size), HALF) for size in widths]
+        + [pltpu.VMEM((2 * tokens, size), HALF) for size in widths[2:]]
+        + [pltpu.VMEM((seqs, share, size), HALF) for size in widths[2:]]
+        + [pltpu.VMEM((first_blocks, half_share, size), HALF) for size in widths[2:]]
+        + [pltpu.VMEM((grid_rows, half_share, size), HALF) for size in widths[2:]]
         + [
-            dma(4),
-            dma(4),
-            dma(4),
-            dma(4),
-            dma_grid(4, first_blocks),
-            dma_grid(4, first_blocks),
-            dma_grid(4, grid_rows),
-            dma_grid(4, grid_rows),
+            dma(2),
+            dma(2),
+            dma(2),
+            dma(2),
+            dma_grid(2, first_blocks),
+            dma_grid(2, first_blocks),
+            dma_grid(2, grid_rows),
+            dma_grid(2, grid_rows),
             pltpu.VMEM((6, share, padded_units), HALF),
             pltpu.VMEM((6, first_blocks, half_share, padded_units), HALF),
             pltpu.VMEM((6, grid_rows, half_share, padded_units), HALF),
@@ -1467,8 +1619,6 @@
             dma_grid(6, 3 + grid_rows),
             dma_grid(3, grid_rows),
             dma_grid(3, grid_rows),
-            dma(first_blocks),
-            dma(first_blocks),
             pltpu.VMEM((2, share, hidden_units), HALF),
             pltpu.VMEM((2, 2, share, hidden_units), HALF),
             dma(4),
@@ -1484,8 +1634,9 @@
         + part_scratch
         + total_scratch,
         [
-            gh1_low, gh1, projected, edge_gated, same, conv_kernel, conv_out, w_in, x, conv_gains, yout,
-            gh2_low, n3, n1, attended, bq, br, mixed, small,
+            gh1_low, (gh1, LAZY), projected, edge_gated, same, conv_kernel, conv_out, (w_in, LAZY), (x, LAZY), conv_gains,
+            (yout, LAZY), (n1, LAZY), (mixed, LAZY), (stage0, LAZY), (stage1, LAZY), (in0, LAZY), (in1, LAZY), (turn0, LAZY), (turn1, LAZY),
+            (small, LAZY),
         ]
         + [(array, ANY) for array in (partial1, partial2, first1, first2, first2_last, second2, second2_last)],
         flops=5 * 10**9,
@@ -1495,7 +1646,7 @@
         edges_in, sums_in, gout2_in, gmix_in, gout1_in, gin_in, gdown2_in, gup2_in, gdown1_in, gup1_in,
         edges_out, cgain_out, gin_out, taps_out, gout1_out, gup1_out, gdown1_out,
         again_out, gq_out, gkv_out, gqk_out, gout2_out, gup2_out, gdown2_out,
-        down_in, up_in, down_stage, up_stage, edges_held, in_sems, out_sems, edge_sem,
+        down_in, up_in, down_stage, up_stage, edges_held, in_sems, out_sems, edge_sem, travel,
     ):
         edges_load = pltpu.make_async_copy(edges_in, edges_held, edge_sem.at[0])
         edges_load.start()

time: 426 us -> 387 us (0.908)
  Pallas kernels: 394 us -> 371 us
  between operations: 14.4 us -> 1.31 us
    pallas_call x7, Pallas kernels: 394 us -> 371 us  [call(): pl.pallas_call(whole, name=name, out_shape=[jax.ShapeDtypeStruct(out[0],...]
  transfers between devices with their start and end apart: 1 -> 0, of which waited for: 0 -> 0; matrix products, arithmetic and copies ran while one was open for 0% -> 0% of each run, Pallas kernels for 29% -> 0%
where the time goes in v5:
time: 387 us; the launch traced here: 381 us
  Pallas kernels  371 us (96%)
  local copies, waits for them, and re-layouts  5.44 us (1%)
    pallas_call x7, Pallas kernels, call(): pl.pallas_call(whole, name=name, out_shape=[jax.ShapeDtypeStruct(out[0],...  371 us

profile of v5, /device:TPU:0, one launch (start us, length us, event | category | flops | bytes accessed | tf_op | source)
XLA Modules:
  0.0 381.1 jit_solution(52021512365109141)
XLA Ops:
  0.7 0.7 copy.41
  1.6 0.1 reshape.141
  1.7 0.1 reshape.143
  1.8 0.8 constant_dynamic-slice_fusion.2
  2.5 0.1 reshape.138
  2.6 0.2 copy.37
  2.8 0.7 stack.8.refs_1_.refs_4_
  3.5 76.4 %conv_forward.1 = (bf16[256,1536]{1,0:T(8,128)(2,1)}, bf16[256,1536]{1,0:T(8,128)(2,1)}, bf16[256,1536]{1,0:T(8,128)(2,1)}, f32[3,256,384]{2,1,0:T(8,128)}, f32[...) custom-call(bf16[1,4,128,1536]{3,2,1,0:T(8,128)(2,1)} %refs_0_.1, ...), custom_call_target="tpu_custom_call" | custom-call | flops 5000000000 | bytes 209715200 | tf_op jit(solution)/shard_map/conv_forward/pallas_call | solution.py:318
  79.9 0.8 copy.38.refs_7_.refs_4_
  80.8 0.1 convert_element_type.39
  80.9 1.2 multiply_sine_fusion
  82.1 0.6 tile.24.refs_5_.refs_10_
  82.7 0.6 tile.27.refs_6_.refs_11_
  83.3 1.0 copy.45
  84.3 47.0 %attention_forward.1 = (f32[256,384]{1,0:T(8,128)}, f32[256,256]{1,0:T(8,128)}, bf16[256,384]{1,0:T(8,128)(2,1)}, bf16[8,256,256]{2,1,0:T(8,128)(2,1)}, bf16[256...) custom-call(bf16[256,1536]{1,0:T(8,128)(2,1)} %get-tuple-element.82.refs_0_.refs_18_, ...), custom_call_target="tpu_custom_call" | custom-call | flops 4000000000 | bytes 157286400 | tf_op jit(solution)/shard_map/attention_forward/pallas_call | solution.py:318
  131.3 52.2 %second_ffn.1 = (bf16[256,1536]{1,0:T(8,128)(2,1)}, f32[128,1536]{1,0:T(8,128)}, bf16[256,1536]{1,0:T(8,128)(2,1)}, f32[1,1536]{1,0:T(1,128)}, bf16[3,4,192,1792...) custom-call(bf16[256,1536]{1,0:T(8,128)(2,1)} %get-tuple-element.84.refs_0_, ...), custom_call_target="tpu_custom_call" | custom-call | flops 12000000000 | bytes 157286400 | tf_op jit(solution)/shard_map/second_ffn/pallas_call | solution.py:318
  183.5 60.2 %attention_backward.1 = (bf16[256,1536]{1,0:T(8,128)(2,1)}, f32[1,1536]{1,0:T(1,128)}, f32[8,128]{1,0:T(8,128)}, bf16[64,1536]{1,0:T(8,128)(2,1)}, bf16[4,192,38...) custom-call(bf16[256,1536]{1,0:T(8,128)(2,1)} %get-tuple-element.87., ...), custom_call_target="tpu_custom_call" | custom-call | flops 6000000000 | bytes 136314880 | tf_op jit(solution)/shard_map/attention_backward/pallas_call | solution.py:318
  243.7 67.9 %first_ffn_back.1 = (f32[128,1536]{1,0:T(8,128)}, bf16[256,1536]{1,0:T(8,128)(2,1)}, f32[1,1536]{1,0:T(1,128)}, bf16[256,1536]{1,0:T(8,128)(2,1)}, bf16[2,96,384...) custom-call(bf16[256,1536]{1,0:T(8,128)(2,1)} %get-tuple-element.97., ...), custom_call_target="tpu_custom_call" | custom-call | flops 8999999488 | bytes 157286400 | tf_op jit(solution)/shard_map/first_ffn_back/pallas_call | solution.py:318
  311.7 0.8 pad_maximum_fusion
  312.5 0.1 reshape.145
  312.7 0.1 reshape.146
  312.9 0.7 fusion.refs_19_
  313.6 58.2 %conv_backward.1 = (bf16[1,4,128,1536]{3,2,1,0:T(8,128)(2,1)}, f32[8,384]{1,0:T(8,128)}, bf16[192,384]{1,0:T(8,128)(2,1)}, bf16[192,640]{1,0:T(8,128)(2,1)}, bf1...) custom-call(bf16[256,1536]{1,0:T(8,128)(2,1)} %get-tuple-element.108, ...), custom_call_target="tpu_custom_call" | custom-call | flops 5000000000 | bytes 314572800 | tf_op jit(solution)/shard_map/conv_backward/pallas_call | solution.py:318
  371.8 8.7 %results.1 = (bf16[1,4,128,1536]{3,2,1,0:T(8,128)(2,1)}, f32[2,192]{1,0:T(2,128)}, f32[3,192,384]{2,1,0:T(8,128)}, f32[3,384]{1,0:T(4,128)}, f32[192,384]{1,0:T(...) custom-call(bf16[1,4,128,1536]{3,2,1,0:T(8,128)(2,1)} %get-tuple-ele, ...), custom_call_target="tpu_custom_call" | custom-call | bytes 26214400 | tf_op jit(solution)/shard_map/results/pallas_call | solution.py:318
  (31 shorter events, 0.6 us)
Async XLA Ops:
  3.5 77.2 %copy-start.3 = (s32[4,128]{1,0:T(4,128)S(1)}, s32[4,128]{1,0:T(4,128)}, u32[]{:S(2)}) copy-start(s32[4,128]{1,0:T(4,128)} %param.18) | copy-start | bytes 6148
  3.5 78.6 %copy-start.5 = (f32[2,64]{1,0:T(2,128)S(1)}, f32[2,64]{1,0:T(2,128)}, u32[]{:S(2)}) copy-start(f32[2,64]{1,0:T(2,128)} %param.28) | copy-start | bytes 1540
  3.5 79.8 %copy-start = (bf16[1536,2,128]{2,1,0:T(2,128)(2,1)S(1)}, bf16[1536,2,128]{2,1,0:T(2,128)(2,1)}, u32[]{:S(2)}) copy-start(bf16[1536,2,128]{2,1,0:T(2,128)(2,1)} %param.27) | copy-start | bytes 2359300
  243.7 68.0 %copy-start.1 = (f32[1,1536]{1,0:T(1,128)S(1)}, f32[1,1536]{1,0:T(1,128)}, u32[]{:S(2)}) copy-start(f32[1,1536]{1,0:T(1,128)} %get-tuple-element.120) | copy-start | bytes 18436
  243.7 68.0 %copy-start.2 = (f32[1,1536]{1,0:T(1,128)S(1)}, f32[1,1536]{1,0:T(1,128)}, u32[]{:S(2)}) copy-start(f32[1,1536]{1,0:T(1,128)} %get-tuple-element.119) | copy-start | bytes 18436
  243.7 68.8 %copy-start.4 = (f32[8,128]{1,0:T(8,128)S(1)}, f32[8,128]{1,0:T(8,128)}, u32[]{:S(2)}) copy-start(f32[8,128]{1,0:T(8,128)} %get-tuple-element.121) | copy-start | bytes 12292

commit v6 on v5

--- a/solution.py
+++ b/solution.py
@@ -373,25 +373,11 @@
     half_model = width // sections
     share = width // (sections * seqs)
 
-    segments = segment_ids.reshape(length)
-
-    def own_tokens(per_token):
-        start = seq * local_rows + section * rows
-        return lax.dynamic_slice_in_dim(per_token.reshape(micro, block_tok), start, rows, 1).reshape(tokens)
-
-    def moved_back(by):
-        return jnp.concatenate([jnp.full((by,), -1, jnp.int32), segments[:-by]])
-
-    local_segments = own_tokens(segments)
-    same = jnp.stack([(local_segments == own_tokens(moved_back(by))).astype(FLOAT) for by in (1, 2)], 1)
-    local_segments = local_segments[:, None]
     pair_index = lax.broadcasted_iota(jnp.int32, (1, 2 * head_width), 1) % (head_width // 2)
     angle_rates = THETA ** (-2.0 * pair_index.astype(FLOAT) / head_width)
     local_positions = lax.dynamic_slice_in_dim(positions, section * rows, rows, 1).reshape(tokens)
     angles = local_positions.astype(FLOAT)[:, None] * angle_rates
     cosine, sine = jnp.cos(angles), jnp.sin(angles)
-    query_gain = jnp.tile(qk_gains[0:1], (1, 2))
-    key_gain = jnp.tile(qk_gains[1:2], (1, 2))
     w_in = conv_in.transpose(1, 0, 2)
     w_pair = w_keyval.reshape(width, pair_width)
     first_up = conv_gate_up.transpose(1, 2, 0)
@@ -400,6 +386,20 @@
     tile_width = 256
     tiles = -(-hidden_units // tile_width)
     padded_units = tiles * tile_width
+
+    def own_column(seg_ref, m, back):
+        start = lax.axis_index("seq") * local_rows + lax.axis_index("section") * rows - back
+        wanted = start + lax.broadcasted_iota(jnp.int32, (rows, block_tok), 0)
+        lane = lax.broadcasted_iota(jnp.int32, (rows, block_tok), 1)
+        found = jnp.where(lane == wanted, seg_ref[m : m + 1, :].astype(FLOAT), 0.0)
+        if back and m:
+            found = found + jnp.where(lane == wanted + block_tok, seg_ref[m - 1 : m, :].astype(FLOAT), 0.0)
+        elif back:
+            found = found + jnp.where((wanted < 0) & (lane == 0), -1.0, 0.0)
+        return jnp.sum(found, -1, keepdims=True)
+
+    def twice(row):
+        return jnp.concatenate([row, row], -1)
 
     def shifted_rows(ext, micro_at, back):
         return ext[micro_at, 8 - back : 8 - back + rows, :]
@@ -432,8 +432,8 @@
         return copies
 
     def conv_forward(
-        in_ref, same_ref, gain_ref, win_ref, kernel_ref, wout_ref, attn_gain_ref, up_hbm, down_hbm,
-        x_ref, g_ref, n1_ref, pc_ref, edge_ref, y_ref, h1_ref, n2_ref, f1_ref, a1_ref, m_ref, n3_ref,
+        in_ref, gain_ref, win_ref, kernel_ref, wout_ref, attn_gain_ref, up_hbm, down_hbm, seg_ref,
+        x_ref, g_ref, n1_ref, pc_ref, edge_ref, y_ref, h1_ref, n2_ref, f1_ref, a1_ref, m_ref, n3_ref, same_ref, segq_ref,
         other, edges, normed_edges, ext, swap_send, swap_recv, edge_send, edge_recv, up_ref, down_ref, weight_sems, acc,
         part, inbox, rs, rr, gs, gr, inbox2, rs2, rr2, gs2, gr2, travel,
     ):
@@ -444,7 +444,7 @@
         preceding = (s, lax.rem(q + seqs - 1, seqs), h)
         weights = weight_loads(up_hbm, down_hbm, up_ref, down_ref, weight_sems)
         start_all(weights)
-        greet([partner, following, preceding], where, heads)
+        greet([partner, following, preceding] + seq_peers(where, seqs), where, heads)
         give = pl.multiple_of((1 - s) * rows, rows)
         swap = remote(in_ref.at[0, :, pl.ds(give, rows)], other, swap_send.at[0], swap_recv.at[0], partner)
         swap.start()
@@ -455,6 +455,12 @@
         )
         far.start()
         keep = pl.multiple_of(s * rows, rows)
+        for m in range(micro):
+            span = slice(m * rows, (m + 1) * rows)
+            column = own_column(seg_ref, m, 0)
+            segq_ref[span, :] = column
+            for back in (1, 2):
+                same_ref[span, back - 1 : back] = jnp.where(column == own_column(seg_ref, m, back), 1.0, 0.0)
         swap.wait()
         mine = in_ref[0, :, pl.ds(keep, rows), :].reshape(tokens, width)
         theirs = other[...].reshape(tokens, width)
@@ -491,7 +497,7 @@
             y_ref[span, :] = (pc_ref[1, span, :] * mixed).astype(HALF)
         travel.ready(wout_ref)
         part[...] = product(y_ref[...], wout_ref[...]).astype(HALF)
-        travel.leave(x_ref, g_ref, n1_ref, pc_ref, edge_ref, y_ref)
+        travel.leave(x_ref, g_ref, n1_ref, pc_ref, edge_ref, y_ref, same_ref, segq_ref)
 
         def finish(flow, i, total):
             hidden = x_ref[own_rows(flow, i), :].astype(FLOAT) + total
@@ -523,44 +529,7 @@
             return norm_apply(middle, attn_gain_ref[0:1, :]).astype(HALF)
 
         head_total(part, n3_ref, inbox2, rs2, rr2, gs2, gr2, where, heads, finish_middle)
-
-    (x, g, n1, projected, edge_gated, mixed, h1, n2, f1, a1, middle, n3) = call(
-        conv_forward,
-        "conv_forward",
-        0,
-        [
-            ((tokens, width), HALF, LATE),
-            ((tokens, width), HALF, LATE),
-            ((tokens, width), HALF, LATE),
-            ((3, tokens, channels), FLOAT, LATE),
-            ((micro, 8, channels), FLOAT, LATE),
-            ((tokens, channels), HALF, LATE),
-            ((half_tokens, width), FLOAT, LATE),
-            ((tokens, width), HALF, LATE),
-            ((2, tokens, hidden_units), FLOAT, LATE),
-            ((tokens, hidden_units), HALF, LATE),
-            ((half_tokens, width), FLOAT),
-            ((tokens, width), HALF),
-        ],
-        [
-            pltpu.VMEM((micro, rows, width), HALF),
-            pltpu.VMEM((2, micro, 16, width), HALF),
-            pltpu.VMEM((micro * 16, width), HALF),
-            pltpu.VMEM((micro, 8 + rows, channels), FLOAT),
-            dma(1),
-            dma(1),
-            dma(2),
-            dma(2),
-        ]
-        + weight_scratch
-        + [pltpu.VMEM((tokens, width), FLOAT)]
-        + part_scratch
-        + total_scratch
-        + total_scratch,
-        [incoming, same, conv_gains, (w_in, LAZY), conv_kernel, (conv_out, LAZY), attn_gains, (first_up, ANY), (conv_down, ANY)],
-        flops=5 * 10**9,
-        moved=200 << 20,
-    )
+        travel.leave(m_ref, n3_ref)
 
 
     grid_rows = seqs // 2
@@ -827,7 +796,7 @@
 
     def allowed_pairs(segq_ref, seg_ref, m, at, s, q):
         own_segments = segq_ref[m * rows : (m + 1) * rows, :]
-        allowed = own_segments == seg_ref[at : at + 1, :]
+        allowed = own_segments == seg_ref[at : at + 1, :].astype(FLOAT)
         if at == m:
             base = q * local_rows + s * rows
             order = base + lax.broadcasted_iota(jnp.int32, (rows, block_tok), 0)
@@ -869,27 +838,27 @@
         return pass_on
 
     def attention_forward(
-        n3_ref, wq_ref, wp_ref, cos_ref, sin_ref, qg_ref, kg_ref, segq_ref, seg_ref, wo_ref, m_ref, gain_ref,
+        n3_ref, wq_ref, wp_ref, cos_ref, sin_ref, qk_ref, segq_ref, seg_ref, wo_ref, m_ref, gain_ref,
         qr_ref, r_ref, q_ref, all_ref, o_ref, h2_ref, n4_ref,
         send, recv, near_send, near_recv, part, inbox, rs, rr, gs, gr, travel,
     ):
         where = place()
         s, q, h = where
         me = q * sections + s
-        greet([(1 - s, q, h)] + seq_peers(where, seqs), where, heads)
+        travel.ready(wp_ref, cos_ref, sin_ref)
         cos, sin = cos_ref[...], sin_ref[...]
         r_ref[...] = product(n3_ref[...], wp_ref[...])
         half_pair = pair_width // 2
         for start, size in chunks_of(half_pair):
             span = slice(start, start + size)
-            all_ref[me, :, span] = rotary(r_ref[:, span], kg_ref[...], cos, sin).astype(HALF)
+            all_ref[me, :, span] = rotary(r_ref[:, span], twice(qk_ref[1:2, :]), cos, sin).astype(HALF)
         all_ref[me, :, half_pair:] = r_ref[:, half_pair:].astype(HALF)
         pass_on = gather_pairs(all_ref, me, where, send, recv, near_send, near_recv)
         travel.ready(wq_ref)
         qr_ref[...] = product(n3_ref[...], wq_ref[...])
         for start, size in chunks_of(query_width):
             span = slice(start, start + size)
-            q_ref[:, span] = rotary(qr_ref[:, span], qg_ref[...], cos, sin).astype(HALF)
+            q_ref[:, span] = rotary(qr_ref[:, span], twice(qk_ref[0:1, :]), cos, sin).astype(HALF)
         travel.leave(r_ref, qr_ref, q_ref)
         pass_on()
         travel.leave(all_ref)
@@ -906,7 +875,7 @@
                 results += [total[r * rows : (r + 1) * rows] for r in range(group)]
             o_ref[m * rows : (m + 1) * rows, :] = jnp.concatenate(results, -1).astype(HALF)
         travel.leave(o_ref)
-        travel.ready(wo_ref, m_ref)
+        travel.ready(wo_ref)
         part[...] = product(o_ref[...], wo_ref[...]).astype(HALF)
 
         def finish(flow, i, total):
@@ -916,11 +885,65 @@
 
         head_total(part, n4_ref, inbox, rs, rr, gs, gr, where, heads, finish)
 
-    (query_raw, pair_raw, queries, all_pairs, attended, h2, n4) = call(
-        attention_forward,
-        "attention_forward",
-        2,
+    def forward(
+        in_ref, gain_ref, win_ref, kernel_ref, wout_ref, attn_gain_ref, up_hbm, down_hbm, seg_ref,
+        wq_ref, wp_ref, cos_ref, sin_ref, qk_ref, wo_ref,
+        x_ref, g_ref, n1_ref, pc_ref, edge_ref, y_ref, h1_ref, n2_ref, f1_ref, a1_ref, m_ref, n3_ref, same_ref, segq_ref,
+        qr_ref, r_ref, q_ref, all_ref, o_ref, h2_ref, n4_ref, *rest,
+    ):
+        travel, rest = rest[-1], rest[:-1]
+        split = len(conv_scratch)
+        conv_forward(
+            in_ref, gain_ref, win_ref, kernel_ref, wout_ref, attn_gain_ref, up_hbm, down_hbm, seg_ref,
+            x_ref, g_ref, n1_ref, pc_ref, edge_ref, y_ref, h1_ref, n2_ref, f1_ref, a1_ref, m_ref, n3_ref,
+            same_ref, segq_ref, *rest[:split], travel,
+        )
+        part = rest[part_at]
+        attention_forward(
+            n3_ref, wq_ref, wp_ref, cos_ref, sin_ref, qk_ref, segq_ref, seg_ref, wo_ref, m_ref, attn_gain_ref,
+            qr_ref, r_ref, q_ref, all_ref, o_ref, h2_ref, n4_ref, *rest[split : split + 4], part, *rest[split + 4 :], travel,
+        )
+
+    conv_scratch = (
+            [
+                pltpu.VMEM((micro, rows, width), HALF),
+                pltpu.VMEM((2, micro, 16, width), HALF),
+                pltpu.VMEM((micro * 16, width), HALF),
+                pltpu.VMEM((micro, 8 + rows, channels), FLOAT),
+                dma(1),
+                dma(1),
+                dma(2),
+                dma(2),
+            ]
+            + weight_scratch
+            + [pltpu.VMEM((tokens, width), FLOAT)]
+            + part_scratch
+            + total_scratch
+            + total_scratch
+    )
+    part_at = len(conv_scratch) - 2 * len(total_scratch) - 1
+    (
+        x, g, n1, projected, edge_gated, mixed, h1, n2, f1, a1, middle, n3, same, local_segments,
+        query_raw, pair_raw, queries, all_pairs, attended, h2, n4,
+    ) = call(
+        forward,
+        "forward",
+        0,
         [
+            ((tokens, width), HALF, LATE),
+            ((tokens, width), HALF, LATE),
+            ((tokens, width), HALF, LATE),
+            ((3, tokens, channels), FLOAT, LATE),
+            ((micro, 8, channels), FLOAT, LATE),
+            ((tokens, channels), HALF, LATE),
+            ((half_tokens, width), FLOAT, LATE),
+            ((tokens, width), HALF, LATE),
+            ((2, tokens, hidden_units), FLOAT, LATE),
+            ((tokens, hidden_units), HALF, LATE),
+            ((half_tokens, width), FLOAT, LATE),
+            ((tokens, width), HALF, LATE),
+            ((tokens, 2), FLOAT, LATE),
+            ((tokens, 1), FLOAT, LATE),
             ((tokens, query_width), FLOAT, LATE),
             ((tokens, pair_width), FLOAT, LATE),
             ((tokens, query_width), HALF, LATE),
@@ -929,13 +952,14 @@
             ((half_tokens, width), FLOAT),
             ((tokens, width), HALF),
         ],
-        [dma(seqs - 1), dma(seqs - 1), dma(seqs), dma(seqs)] + part_scratch + total_scratch,
+        conv_scratch + [dma(seqs - 1), dma(seqs - 1), dma(seqs), dma(seqs)] + total_scratch,
         [
-            n3, (w_query, LAZY), w_pair, cosine, sine, query_gain, key_gain, local_segments, segment_ids,
-            (attn_out, LAZY), (middle, LAZY), attn_gains,
+            incoming, conv_gains, (w_in, LAZY), conv_kernel, (conv_out, LAZY), attn_gains,
+            (first_up, ANY), (conv_down, ANY), segment_ids,
+            (w_query, LAZY), (w_pair, LAZY), (cosine, LAZY), (sine, LAZY), qk_gains, (attn_out, LAZY),
         ],
-        flops=4 * 10**9,
-        moved=150 << 20,
+        flops=9 * 10**9,
+        moved=350 << 20,
     )
 
     def slab_width(start, count):
@@ -1046,7 +1070,7 @@
     )
     def attention_backward(
         glow_ref, wo_ref, q_ref, all_ref, segq_ref, seg_ref,
-        qr_ref, r_ref, cos_ref, sin_ref, qg_ref, kg_ref, wq_ref, wp_ref, m_ref, gh2_ref, gain_ref, py_ref, n3_ref, o_ref, partial2_hbm, first2_hbm,
+        qr_ref, r_ref, cos_ref, sin_ref, qk_ref, wq_ref, wp_ref, m_ref, gh2_ref, gain_ref, py_ref, n3_ref, o_ref, partial2_hbm, first2_hbm,
         low_ref, gg_ref, gqk_ref, yown_ref, stage0, stage1, in0, in1, second_in, first_in,
         bq_ref, br_ref, grads, totals, gq_ref, gp_ref, near_slots, pair_slots, ns, nr, ps, pr,
         passing, held, load_sems, vs, vr, fs, fr,
@@ -1058,12 +1082,15 @@
         partner = (1 - s, q, h)
         peers = seq_peers(where, seqs)
         loads = pass_loads(partial2_hbm, (0, 1), first2_hbm, passing, held, load_sems, where)
+        loads += load_passing(partial2_hbm.at[2], passing.at[2], load_sems.at[2], where)
         start_all(loads)
         others = head_others(where)
         latters = [latter0, latter1]
         greet([partner] + peers + others, where, heads)
-        wait_all(loads)
-        travelling = pass_sends(2, passing, held, second_in, vs, vr, where)
+        later = first_stage(
+            lambda dest, side: partial2_hbm.at[2, dest, half_rows(side)], lambda i: first_in.at[0, i], fs, fr, where
+        )
+        start_all(later)
         travel.ready(py_ref, n3_ref, o_ref)
         latter0[0:tokens, :] = o_ref[...]
         ysends = [
@@ -1126,18 +1153,15 @@
             copy = remote(near_slots.at[peer[1]], pair_slots.at[k], ps.at[k], pr.at[k], peer)
             copy.start()
             copies.append(copy)
-        later = first_stage(
-            lambda dest, side: partial2_hbm.at[2, dest, half_rows(side)], lambda i: first_in.at[0, i], fs, fr, where
-        )
-        start_all(later)
-        travelling += later
         cos, sin = cos_ref[...], sin_ref[...]
         for start, size in chunks_of(query_width):
             span = slice(start, start + size)
-            grad_raw, grad_gain = rotary_back(qr_ref[:, span], qg_ref[...], cos, sin, gq_ref[:, span])
+            grad_raw, grad_gain = rotary_back(qr_ref[:, span], twice(qk_ref[0:1, :]), cos, sin, gq_ref[:, span])
             bq_ref[:, span] = grad_raw.astype(HALF)
             gqk_ref[0:1, :size] += grad_gain
         partial = back_product(bq_ref[...], wq_ref[...])
+        wait_all(loads)
+        travelling = pass_sends(2, passing, held, second_in, vs, vr, where)
         wait_all(copies)
         grad_pair = near_slots[q].astype(FLOAT)
         for j in range(seqs - 1):
@@ -1145,10 +1169,16 @@
         half_pair = pair_width // 2
         for start, size in chunks_of(half_pair):
             span = slice(start, start + size)
-            grad_raw, grad_gain = rotary_back(r_ref[:, span], kg_ref[...], cos, sin, grad_pair[:, span])
+            grad_raw, grad_gain = rotary_back(r_ref[:, span], twice(qk_ref[1:2, :]), cos, sin, grad_pair[:, span])
             br_ref[:, span] = grad_raw.astype(HALF)
             gqk_ref[1:2, :size] += grad_gain
         br_ref[:, half_pair:] = grad_pair[:, half_pair:].astype(HALF)
+        wait_all(later)
+        combine(lambda i: passing.at[2, i], first_in.at[0], where)
+        turning = second_stage(lambda i: passing.at[2, i], second_in.at[2], vs.at[2], vr.at[2], where)
+        start_all(turning)
+        travelling += turning
+        travel.leave(first_in)
         latter1[0:tokens, 0:query_width] = bq_ref[...]
         latter1[0:tokens, query_width:] = br_ref[...]
         swaps[1].start()
@@ -1183,8 +1213,8 @@
             ((seqs, share, widths[0]), HALF),
             ((seqs, share, widths[1]), HALF),
             *first_sums(widths[:2]),
-            second_shape(2),
-            first_shape(1),
+            second_shape(3),
+            ((1, first_blocks, half_share, padded_units), HALF, LATE),
         ],
         [
             pltpu.VMEM((tokens, query_width), HALF),
@@ -1200,7 +1230,7 @@
             dma(seqs - 1),
             dma(seqs - 1),
         ]
-        + passing_scratch(2)
+        + passing_scratch(3)
         + [dma(first_blocks), dma(first_blocks)]
         + [
             pltpu.VMEM((heads - 1, small_rows, width), HALF),
@@ -1221,7 +1251,7 @@
         + total_scratch,
         [
             gh2_low, attn_out, queries, all_pairs, local_segments, segment_ids,
-            (query_raw, LAZY), (pair_raw, LAZY), (cosine, LAZY), (sine, LAZY), query_gain, key_gain,
+            (query_raw, LAZY), (pair_raw, LAZY), (cosine, LAZY), (sine, LAZY), qk_gains,
             (w_query, LAZY), (w_pair, LAZY), (middle, LAZY), (gh2, LAZY), attn_gains,
             (part_y, LAZY), (n3, LAZY), (attended, LAZY), (partial2, ANY), (first2, ANY),
         ],
@@ -1230,17 +1260,15 @@
     )
 
     def first_ffn_back(
-        gm_ref, n2_ref, f1_ref, a1_ref, h1_ref, gain_ref, yown_ref, stage0, stage1, in0, in1, up_hbm, down_hbm, partial2_hbm, first2_hbm,
-        gh1_ref, low_ref, gg_ref, yout_ref, turn0, turn1, partial_hbm, first_in, second_in,
+        gm_ref, n2_ref, f1_ref, a1_ref, h1_ref, gain_ref, yown_ref, stage0, stage1, in0, in1, up_hbm, down_hbm,
+        gh1_ref, low_ref, gg_ref, yout_ref, turn0, turn1, partial_hbm, first_in,
         up_ref, down_ref, weight_sems, acc, given, former, latter, stage, hs, hr, ls, lr, local_sems, ts, tr,
-        passing, held, load_sems, vs, vr, ys, yr, pass0, pass1, us, ur,
+        ys, yr, pass0, pass1, us, ur,
         part, inbox, rs, rr, gs, gr, travel,
     ):
         where = place()
         s, q, h = where
         weights = weight_loads(up_hbm, down_hbm, up_ref, down_ref, weight_sems)
-        loads = pass_loads(partial2_hbm, (2,), first2_hbm, passing, held, load_sems, where)
-        start_all(loads)
         start_all(weights)
         clear_padding(latter)
         others = head_others(where)
@@ -1252,8 +1280,6 @@
             remote(yout_ref.at[own_y], yout_ref.at[own_y], ys.at[n], yr.at[n], peer) for n, peer in enumerate(others)
         ]
         start_all(ysends)
-        wait_all(loads)
-        travelling = pass_sends(1, passing, held, second_in, vs, vr, where)
         halves = half_swaps([gm_ref, n2_ref], [given.at[0], given.at[1]], hs, hr, where)
         start_all(halves)
         gg_ref[...] = jnp.zeros_like(gg_ref)
@@ -1317,26 +1343,23 @@
 
         head_total(part, low_ref, inbox, rs, rr, gs, gr, where, heads, finish, filler, 2 * tiles + 1)
         tiles_done()
-        wait_all(travelling)
         wait_all(ysends)
         for copies in turning:
             wait_all(copies)
 
-    (gh1, gh1_low, grad_gain_conv1, yout, turn0, turn1, partial1, first1, second2_last) = call(
+    (gh1, gh1_low, grad_gain_conv1, yout, turn0, turn1, partial1, first1) = call(
         first_ffn_back,
         "first_ffn_back",
         6,
         [((half_tokens, width), FLOAT), ((tokens, width), HALF), ((1, width), FLOAT), ((tokens, width), HALF)]
         + [((grid_rows, half_share, size), HALF) for size in widths[:2]]
-        + partial_outs(3)
-        + [second_shape(1)],
-        ffn_scratch + passing_scratch(1)
-        + [dma(heads - 1), dma(heads - 1)]
+        + partial_outs(3),
+        ffn_scratch + [dma(heads - 1), dma(heads - 1)]
         + [pltpu.VMEM((grid_rows, half_share, size), HALF) for size in widths[:2]]
         + [dma_grid(2, grid_rows), dma_grid(2, grid_rows)]
         + part_scratch + total_scratch,
         [gm_low, (n2, LAZY), (f1, LAZY), (a1, LAZY), (h1, LAZY), conv_gains, (y_own, LAZY),
-         (stage0, LAZY), (stage1, LAZY), (in0, LAZY), (in1, LAZY), (first_up, ANY), (conv_down, ANY), (partial2, ANY), (first2_last, ANY)],
+         (stage0, LAZY), (stage1, LAZY), (in0, LAZY), (in1, LAZY), (first_up, ANY), (conv_down, ANY)],
         flops=9 * 10**9,
         moved=150 << 20,
     )
@@ -1345,7 +1368,7 @@
     def conv_backward(
         low_ref, gh1_ref, pc_ref, edge_ref, same_ref, kernel_ref, wout_ref, win_ref, x_ref, gain_ref, yout_ref,
         n1_ref, mixed_ref, stage0, stage1, in0, in1, turn0, turn1, small_in,
-        partial1, partial2, first1, first2, first2_last, second2, second2_last,
+        partial1, partial2, first1, first2, first2_last, second2,
         edges_ref, sums_ref, gout2_ref, gmix_ref, gout1_ref, gin_ref, gdown2, gup2, gdown1, gup1,
         bp_ref, ext, spread, gz_ext, outgoing, arrived, full, gg_ref, edge_send, edge_recv, swap_send, swap_recv,
         given, former, latter2, latter3, stage2, stage3, in2, in3, turn2, turn3, hs, hr, ls, lr, ms, mr, us, ur,
@@ -1369,7 +1392,7 @@
         sources = [
             (partial2.at[0], first2.at[0], second2.at[0]),
             (partial2.at[1], first2.at[1], second2.at[1]),
-            (partial2.at[2], first2_last.at[0], second2_last.at[0]),
+            (partial2.at[2], first2_last.at[0], second2.at[2]),
             (partial1.at[0], first1.at[0], None),
             (partial1.at[1], first1.at[1], None),
             (partial1.at[2], first1.at[2], None),
@@ -1638,7 +1661,7 @@
             (yout, LAZY), (n1, LAZY), (mixed, LAZY), (stage0, LAZY), (stage1, LAZY), (in0, LAZY), (in1, LAZY), (turn0, LAZY), (turn1, LAZY),
             (small, LAZY),
         ]
-        + [(array, ANY) for array in (partial1, partial2, first1, first2, first2_last, second2, second2_last)],
+        + [(array, ANY) for array in (partial1, partial2, first1, first2, first2_last, second2)],
         flops=5 * 10**9,
         moved=300 << 20,
     )

time: 387 us -> 375 us (0.969)
  Pallas kernels: 371 us -> 361 us
    pallas_call x7 -> x6, Pallas kernels: 371 us -> 361 us  [call(): pl.pallas_call(whole, name=name, out_shape=[jax.ShapeDtypeStruct(out[0],...]
where the time goes in v6:
time: 375 us; the launch traced here: 369 us
  Pallas kernels  361 us (96%)
    pallas_call x6, Pallas kernels, call(): pl.pallas_call(whole, name=name, out_shape=[jax.ShapeDtypeStruct(out[0],...  361 us

profile of v6, /device:TPU:0, one launch (start us, length us, event | category | flops | bytes accessed | tf_op | source)
XLA Modules:
  0.0 368.7 jit_solution(12738633612201278493)
XLA Ops:
  0.6 0.8 dynamic-slice_convert_fusion
  1.4 0.1 convert_element_type.23
  1.5 1.2 multiply_sine_fusion
  2.7 2.1 copy.34
  4.9 118.1 %forward.1 = (bf16[256,1536]{1,0:T(8,128)(2,1)}, bf16[256,1536]{1,0:T(8,128)(2,1)}, bf16[256,1536]{1,0:T(8,128)(2,1)}, f32[3,256,384]{2,1,0:T(8,128)}, f32[4,8,3...) custom-call(bf16[1,4,128,1536]{3,2,1,0:T(8,128)(2,1)} %refs_0_.1, ...), custom_call_target="tpu_custom_call" | custom-call | flops 8999999488 | bytes 367001600 | tf_op jit(solution)/shard_map/forward/pallas_call | solution.py:318
  122.9 52.1 %second_ffn.1 = (bf16[256,1536]{1,0:T(8,128)(2,1)}, f32[128,1536]{1,0:T(8,128)}, bf16[256,1536]{1,0:T(8,128)(2,1)}, f32[1,1536]{1,0:T(1,128)}, bf16[3,4,192,1792...) custom-call(bf16[256,1536]{1,0:T(8,128)(2,1)} %get-tuple-element.83.refs_0_, ...), custom_call_target="tpu_custom_call" | custom-call | flops 12000000000 | bytes 157286400 | tf_op jit(solution)/shard_map/second_ffn/pallas_call | solution.py:318
  175.0 60.1 %attention_backward.1 = (bf16[256,1536]{1,0:T(8,128)(2,1)}, f32[1,1536]{1,0:T(1,128)}, f32[8,128]{1,0:T(8,128)}, bf16[64,1536]{1,0:T(8,128)(2,1)}, bf16[4,192,38...) custom-call(bf16[256,1536]{1,0:T(8,128)(2,1)} %get-tuple-element.86., ...), custom_call_target="tpu_custom_call" | custom-call | flops 6000000000 | bytes 136314880 | tf_op jit(solution)/shard_map/attention_backward/pallas_call | solution.py:318
  235.1 0.0 copy-start
  235.1 0.0 copy-start.1
  235.1 0.0 copy-start.2
  235.2 64.5 %first_ffn_back.1 = (f32[128,1536]{1,0:T(8,128)}, bf16[256,1536]{1,0:T(8,128)(2,1)}, f32[1,1536]{1,0:T(1,128)}, bf16[256,1536]{1,0:T(8,128)(2,1)}, bf16[2,96,384...) custom-call(bf16[256,1536]{1,0:T(8,128)(2,1)} %get-tuple-element.99., ...), custom_call_target="tpu_custom_call" | custom-call | flops 8999999488 | bytes 157286400 | tf_op jit(solution)/shard_map/first_ffn_back/pallas_call | solution.py:318
  299.7 0.0 copy-done
  299.7 0.0 copy-done.1
  299.7 0.8 pad_maximum_fusion
  300.5 0.1 reshape.69
  300.6 0.0 copy-done.2
  300.6 0.1 slice_add_fusion
  300.7 0.1 reshape.70
  300.8 0.1 pad.12.clone
  300.9 0.7 fusion.refs_19_
  301.6 57.9 %conv_backward.1 = (bf16[1,4,128,1536]{3,2,1,0:T(8,128)(2,1)}, f32[8,384]{1,0:T(8,128)}, bf16[192,384]{1,0:T(8,128)(2,1)}, bf16[192,640]{1,0:T(8,128)(2,1)}, bf1...) custom-call(bf16[256,1536]{1,0:T(8,128)(2,1)} %get-tuple-element.109, ...), custom_call_target="tpu_custom_call" | custom-call | flops 5000000000 | bytes 314572800 | tf_op jit(solution)/shard_map/conv_backward/pallas_call | solution.py:318
  359.5 8.7 %results.1 = (bf16[1,4,128,1536]{3,2,1,0:T(8,128)(2,1)}, f32[2,192]{1,0:T(2,128)}, f32[3,192,384]{2,1,0:T(8,128)}, f32[3,384]{1,0:T(4,128)}, f32[192,384]{1,0:T(...) custom-call(bf16[1,4,128,1536]{3,2,1,0:T(8,128)(2,1)} %get-tuple-ele, ...), custom_call_target="tpu_custom_call" | custom-call | bytes 26214400 | tf_op jit(solution)/shard_map/results/pallas_call | solution.py:318
  (6 shorter events, 0.1 us)
Async XLA Ops:
  235.1 64.6 %copy-start = (f32[1,1536]{1,0:T(1,128)S(1)}, f32[1,1536]{1,0:T(1,128)}, u32[]{:S(2)}) copy-start(f32[1,1536]{1,0:T(1,128)} %get-tuple-element.122) | copy-start | bytes 18436
  235.1 64.6 %copy-start.1 = (f32[1,1536]{1,0:T(1,128)S(1)}, f32[1,1536]{1,0:T(1,128)}, u32[]{:S(2)}) copy-start(f32[1,1536]{1,0:T(1,128)} %get-tuple-element.121) | copy-start | bytes 18436
  235.1 65.4 %copy-start.2 = (f32[8,128]{1,0:T(8,128)S(1)}, f32[8,128]{1,0:T(8,128)}, u32[]{:S(2)}) copy-start(f32[8,128]{1,0:T(8,128)} %get-tuple-element.123) | copy-start | bytes 12292

commit v7 on v6

--- a/solution.py
+++ b/solution.py
@@ -69,25 +69,31 @@
     pl.semaphore_wait(pltpu.get_barrier_semaphore(), count)
 
 
-def greet(others, where=None, size=0):
+def greet(others, where, size):
     for peer in others:
         signal(peer)
-    if where is None:
-        wait_greetings(len(others))
-        return
     section, seq, head = where
     end = (head == 0) | (head == size - 1)
 
     @pl.when(end)
     def _():
         signal((section, seq, jnp.where(head == 0, 1, size - 2)))
-        wait_greetings(len(others) + 1)
 
     @pl.when(jnp.logical_not(end))
     def _():
         signal((section, seq, jnp.minimum(head + 1, size - 1)))
         signal((section, seq, jnp.maximum(head - 1, 0)))
-        wait_greetings(len(others) + 2)
+
+    def met():
+        @pl.when(end)
+        def _():
+            wait_greetings(len(others) + 1)
+
+        @pl.when(jnp.logical_not(end))
+        def _():
+            wait_greetings(len(others) + 2)
+
+    return met
 
 
 def seq_peers(where, seqs):
@@ -262,7 +268,9 @@
 class Moves:
     def __init__(self, incoming, leaving):
         self.incoming, self.leaving, self.left = incoming, leaving, []
-        for _, copy in incoming:
+
+    def begin(self):
+        for _, copy in self.incoming:
             copy.start()
 
     def ready(self, *refs):
@@ -282,7 +290,7 @@
         wait_all(self.left)
 
 
-def call(body, name, collective, outs, scratch, args, flops=0, moved=0):
+def call(body, name, collective, outs, scratch, args, flops=0, moved=0, begin=True):
     params = dict(vmem_limit_bytes=60 << 20)
     if collective is not None:
         params.update(collective_id=collective, has_side_effects=True)
@@ -309,6 +317,8 @@
             leaving.append((kept, pltpu.make_async_copy(kept, refs[place_at], held[-1].at[len(lazy) + at])))
             refs[place_at] = kept
         travel = Moves(incoming, leaving)
+        if begin:
+            travel.begin()
         body(*refs, travel)
         travel.finish()
 
@@ -444,7 +454,14 @@
         preceding = (s, lax.rem(q + seqs - 1, seqs), h)
         weights = weight_loads(up_hbm, down_hbm, up_ref, down_ref, weight_sems)
         start_all(weights)
-        greet([partner, following, preceding] + seq_peers(where, seqs), where, heads)
+        met = greet([partner, following, preceding] + seq_peers(where, seqs), where, heads)
+        for m in range(micro):
+            span = slice(m * rows, (m + 1) * rows)
+            column = own_column(seg_ref, m, 0)
+            segq_ref[span, :] = column
+            for back in (1, 2):
+                same_ref[span, back - 1 : back] = jnp.where(column == own_column(seg_ref, m, back), 1.0, 0.0)
+        met()
         give = pl.multiple_of((1 - s) * rows, rows)
         swap = remote(in_ref.at[0, :, pl.ds(give, rows)], other, swap_send.at[0], swap_recv.at[0], partner)
         swap.start()
@@ -455,12 +472,6 @@
         )
         far.start()
         keep = pl.multiple_of(s * rows, rows)
-        for m in range(micro):
-            span = slice(m * rows, (m + 1) * rows)
-            column = own_column(seg_ref, m, 0)
-            segq_ref[span, :] = column
-            for back in (1, 2):
-                same_ref[span, back - 1 : back] = jnp.where(column == own_column(seg_ref, m, back), 1.0, 0.0)
         swap.wait()
         mine = in_ref[0, :, pl.ds(keep, rows), :].reshape(tokens, width)
         theirs = other[...].reshape(tokens, width)
@@ -677,9 +688,7 @@
                 return own_block(i, stage) if passed is None else passed.at[i]
 
             combine(moved, income, where, own_block)
-            sends = second_stage(moved, turn, send.at[k], recv.at[k], where)
-            start_all(sends)
-            turning.append(sends)
+            turning.append(second_stage(moved, turn, send.at[k], recv.at[k], where))
         return turning
 
     def latter_swaps(latters, send, recv, partner):
@@ -721,10 +730,10 @@
             at = lax.rem(t, tiles)
             return kind, pl.ds(pl.multiple_of(at * tile_width, tile_width), tile_width)
 
-        def stored(t, dest):
+        def stored(t):
             kind, columns = split(t)
             return pltpu.make_async_copy(
-                stage.at[kind, dest, :, columns], partial_hbm.at[kind, dest, :, columns], local_sems.at[t, dest]
+                stage.at[kind, :, :, columns], partial_hbm.at[kind, :, :, columns], local_sems.at[t]
             )
 
         def sent(t):
@@ -747,15 +756,10 @@
             def _():
                 start_all(sent(t))
 
-            for dest in range(seqs):
-                stored(t, dest).start()
+            stored(t).start()
 
         def finish():
-            def stored_all(t):
-                for dest in range(seqs):
-                    stored(t, dest).wait()
-
-            loop(3 * tiles, stored_all)
+            loop(3 * tiles, lambda t: stored(t).wait())
             loop(kinds * tiles, lambda t: wait_all(sent(t)))
 
         return tile, finish
@@ -770,7 +774,7 @@
         dma(2),
         pltpu.SemaphoreType.DMA((3, len(slabs))),
         pltpu.SemaphoreType.DMA((3, len(slabs))),
-        pltpu.SemaphoreType.DMA((3 * tiles, seqs)),
+        pltpu.SemaphoreType.DMA((3 * tiles,)),
         pltpu.SemaphoreType.DMA((3 * tiles, first_blocks)),
         pltpu.SemaphoreType.DMA((3 * tiles, first_blocks)),
     ]
@@ -805,15 +809,11 @@
         return jnp.concatenate([bias] * group, 0)
 
     def probabilities(rows_in, keys, biases):
-        scores = [
-            jnp.where(bias < 0, -1e30, back_product(rows_in, key) * score_scale)
-            for key, bias in zip(keys, biases)
-        ]
+        scores = [back_product(rows_in, key) + bias for key, bias in zip(keys, biases)]
         summit = functools.reduce(jnp.maximum, [jnp.max(part, -1, keepdims=True) for part in scores])
         raised = [jnp.exp(part - summit) for part in scores]
         total = functools.reduce(jnp.add, [jnp.sum(part, -1, keepdims=True) for part in raised])
-        inverse = 1.0 / total
-        return [part * inverse for part in raised]
+        return raised, 1.0 / total
 
     def gather_pairs(all_ref, me, where, send, recv, near_send, near_recv):
         s, q, h = where
@@ -867,10 +867,13 @@
             results = []
             for c in range(kv_local):
                 keys = [keys_of(all_ref, at, c, 0) for at in range(m + 1)]
-                weights = probabilities(query_rows(q_ref, m, c), keys, biases)
+                raised, inverse = probabilities(query_rows(q_ref, m, c) * HALF(score_scale), keys, biases)
                 total = functools.reduce(
                     jnp.add,
-                    [product(weights[at].astype(HALF), keys_of(all_ref, at, c, 1)) for at in range(m + 1)],
+                    [
+                        product((raised[at] * inverse).astype(HALF), keys_of(all_ref, at, c, 1))
+                        for at in range(m + 1)
+                    ],
                 )
                 results += [total[r * rows : (r + 1) * rows] for r in range(group)]
             o_ref[m * rows : (m + 1) * rows, :] = jnp.concatenate(results, -1).astype(HALF)
@@ -980,9 +983,8 @@
         weights = weight_loads(up_hbm, down_hbm, up_ref, down_ref, weight_sems)
         start_all(weights)
         clear_padding(latter)
-        greet([(1 - s, q, h)] + seq_peers(where, seqs), where, heads)
+        met = greet([(1 - s, q, h)] + seq_peers(where, seqs), where, heads)
         halves = half_swaps([g_ref, n4_ref], [given.at[0], given.at[1]], hs, hr, where)
-        start_all(halves)
         gg_ref[...] = jnp.zeros_like(gg_ref)
         swaps = []
         for j, (start, count) in enumerate(slabs):
@@ -999,6 +1001,9 @@
             latter[0, 0:tokens, span] = active
             latter[1, 0:tokens, span] = grad_gate
             latter[2, 0:tokens, span] = grad_rise
+            if j == 0:
+                met()
+                start_all(halves)
             for kind in range(3):
                 swap = latter_swap(
                     latter, kind, start, slab_width(start, count), ls.at[kind, j], lr.at[kind, j], where
@@ -1086,7 +1091,9 @@
         start_all(loads)
         others = head_others(where)
         latters = [latter0, latter1]
-        greet([partner] + peers + others, where, heads)
+        met = greet([partner] + peers + others, where, heads)
+        grads[...] = back_product(glow_ref[...], wo_ref[...]).astype(HALF)
+        met()
         later = first_stage(
             lambda dest, side: partial2_hbm.at[2, dest, half_rows(side)], lambda i: first_in.at[0, i], fs, fr, where
         )
@@ -1104,16 +1111,16 @@
         swaps[0].start()
         gg_ref[...] = jnp.zeros_like(gg_ref)
         gqk_ref[...] = jnp.zeros_like(gqk_ref)
-        grads[...] = back_product(glow_ref[...], wo_ref[...]).astype(HALF)
         for m in range(micro):
             biases = [allowed_pairs(segq_ref, seg_ref, m, at, s, q) for at in range(m + 1)]
             results = []
             for c in range(kv_local):
                 keys = [keys_of(all_ref, at, c, 0) for at in range(m + 1)]
                 values = [keys_of(all_ref, at, c, 1) for at in range(m + 1)]
-                rows_in = query_rows(q_ref, m, c)
+                rows_in = query_rows(q_ref, m, c) * HALF(score_scale)
                 grad_rows = query_rows(grads, m, c)
-                chances = probabilities(rows_in, keys, biases)
+                raised, inverse = probabilities(rows_in, keys, biases)
+                chances = [part * inverse for part in raised]
                 grad_chances = [back_product(grad_rows, value) for value in values]
                 inner = functools.reduce(
                     jnp.add,
@@ -1124,7 +1131,7 @@
                     grad_scores = (chances[at] * (grad_chances[at] - inner)).astype(HALF)
                     term = product(grad_scores, keys[at])
                     total = term if total is None else total + term
-                    grad_key = outer_sum(grad_scores, rows_in) * score_scale
+                    grad_key = outer_sum(grad_scores, rows_in)
                     grad_value = outer_sum(chances[at].astype(HALF), grad_rows)
                     if at == m:
                         totals[at, c] = grad_key
@@ -1273,9 +1280,15 @@
         clear_padding(latter)
         others = head_others(where)
         own_y = rows_of(h, small_rows)
-        greet([(1 - s, q, h)] + seq_peers(where, seqs) + others, where, heads)
+        met = greet([(1 - s, q, h)] + seq_peers(where, seqs) + others, where, heads)
         travel.ready(yown_ref, n2_ref, a1_ref)
         yout_ref[own_y, :] = yown_ref[...]
+        latter[0, 0:tokens, 0:hidden_units] = a1_ref[...]
+        travel.ready(stage0, stage1, in0, in1)
+        turning = mixer_second([stage0, stage1], [in0, in1], [pass0, pass1], [turn0, turn1], us, ur, where)
+        met()
+        for copies in turning:
+            start_all(copies)
         ysends = [
             remote(yout_ref.at[own_y], yout_ref.at[own_y], ys.at[n], yr.at[n], peer) for n, peer in enumerate(others)
         ]
@@ -1283,9 +1296,6 @@
         halves = half_swaps([gm_ref, n2_ref], [given.at[0], given.at[1]], hs, hr, where)
         start_all(halves)
         gg_ref[...] = jnp.zeros_like(gg_ref)
-        latter[0, 0:tokens, 0:hidden_units] = a1_ref[...]
-        travel.ready(stage0, stage1, in0, in1)
-        turning = mixer_second([stage0, stage1], [in0, in1], [pass0, pass1], [turn0, turn1], us, ur, where)
         tile, tiles_done = gradient_tiles(
             former, latter, stage, partial_hbm, first_in, local_sems, ts, tr, where, 3
         )
@@ -1294,6 +1304,10 @@
             for j, (start, count) in enumerate(slabs)
         ]
         start_all(active_swaps)
+        halves[0].wait()
+        former[0] = transposed(gm_ref, given.at[0])
+        wait_all(active_swaps)
+        loop(tiles, tile)
         swaps = []
         travel.ready(f1_ref, h1_ref)
         for j, (start, count) in enumerate(slabs):
@@ -1316,10 +1330,6 @@
             term = product(grad_gate, up_ref[0, span, :]) + product(grad_rise, up_ref[1, span, :])
             if j == 0:
                 acc[...] = term
-                halves[0].wait()
-                wait_all(active_swaps)
-                former[0] = transposed(gm_ref, given.at[0])
-                loop(tiles, tile)
             else:
                 acc[...] += term
         part[...] = acc[...].astype(HALF)
@@ -1367,7 +1377,7 @@
 
     def conv_backward(
         low_ref, gh1_ref, pc_ref, edge_ref, same_ref, kernel_ref, wout_ref, win_ref, x_ref, gain_ref, yout_ref,
-        n1_ref, mixed_ref, stage0, stage1, in0, in1, turn0, turn1, small_in,
+        n1_ref, mixed_ref, stage0, stage1, in0, in1, turn0, turn1, gain1_ref, gain2_ref, gain3_ref, gqk_ref,
         partial1, partial2, first1, first2, first2_last, second2,
         edges_ref, sums_ref, gout2_ref, gmix_ref, gout1_ref, gin_ref, gdown2, gup2, gdown1, gup1,
         bp_ref, ext, spread, gz_ext, outgoing, arrived, full, gg_ref, edge_send, edge_recv, swap_send, swap_recv,
@@ -1406,15 +1416,23 @@
             else:
                 copies += load_passing(partial, passing.at[n - 3], item_sems.at[n, pl.ds(3, grid_rows)], where)
             loads.append(copies)
-        for copies in loads[3:] + loads[:3]:
+        for copies in loads[3:]:
             start_all(copies)
-        greet([partner, preceding, following] + others + slot_peers, where, heads)
-        travel.ready(n1_ref, mixed_ref)
-        latter2[0:tokens, :] = mixed_ref[...]
-        halves = half_swaps([low_ref, n1_ref], [given.at[0], given.at[1]], hs, hr, where)
-        start_all(halves)
-        swaps = latter_swaps(latters, ls, lr, partner)
-        swaps[0].start()
+        travel.begin()
+        for copies in loads[:3]:
+            start_all(copies)
+        met = greet([partner, preceding, following] + others + slot_peers, where, heads)
+        bulk = []
+
+        def pass_item(n):
+            wait_all(loads[n])
+            combine(lambda i: passing.at[n - 3, i], first_buf.at[n], where)
+            sends = second_stage(
+                lambda i: passing.at[n - 3, i], second_buf.at[n], vs.at[n - 3], vr.at[n - 3], where
+            )
+            start_all(sends)
+            bulk.append(sends)
+
         gg_ref[...] = jnp.zeros_like(gg_ref)
         gated = pc_ref[0] * pc_ref[2]
         grad_y = back_product(low_ref[...], wout_ref[...])
@@ -1431,17 +1449,17 @@
             outgoing[m] = zero
             outgoing[m, 0:1, :] = two[0:1]
             outgoing[m, 1:2, :] = one[0:1] + two[1:2]
+        met()
         edge = remote(outgoing, arrived, edge_send.at[0], edge_recv.at[0], preceding)
         edge.start()
-        bulk = []
         for n in (3, 4, 5):
-            wait_all(loads[n])
-            combine(lambda i, n=n: passing.at[n - 3, i], first_buf.at[n], where)
-            sends = second_stage(
-                lambda i, n=n: passing.at[n - 3, i], second_buf.at[n], vs.at[n - 3], vr.at[n - 3], where
-            )
-            start_all(sends)
-            bulk.append(sends)
+            pass_item(n)
+        travel.ready(n1_ref, mixed_ref)
+        latter2[0:tokens, :] = mixed_ref[...]
+        halves = half_swaps([low_ref, n1_ref], [given.at[0], given.at[1]], hs, hr, where)
+        start_all(halves)
+        swaps = latter_swaps(latters, ls, lr, partner)
+        swaps[0].start()
         taps = [None, None, None]
         for m in range(micro):
             span = slice(m * rows, (m + 1) * rows)
@@ -1476,7 +1494,7 @@
             bp_ref[span, 2 * channels :] = (spread[m] * pc_ref[0, span, :]).astype(HALF)
         latter3[0:tokens, :] = bp_ref[...]
         swaps[1].start()
-        travel.ready(win_ref, x_ref, gh1_ref, yout_ref, small_in)
+        travel.ready(win_ref, x_ref, gh1_ref, yout_ref)
         total = back_product(bp_ref[:, 0:channels], win_ref[0])
         total = total + back_product(bp_ref[:, channels : 2 * channels], win_ref[1])
         total = total + back_product(bp_ref[:, 2 * channels :], win_ref[2])
@@ -1501,10 +1519,14 @@
             )
             copy.start()
             edge_swaps.append(copy)
-        packed[...] = small_in[...]
+        packed[...] = jnp.zeros_like(packed)
+        folded = [gqk_ref[n : n + 1, 0:head_width] + gqk_ref[n : n + 1, head_width : 2 * head_width] for n in range(2)]
+        folded = jnp.concatenate(folded, -1)
         packed[:, 5:8, 0:channels] = jnp.broadcast_to(jnp.concatenate(taps, 0)[None], (slots, 3, channels))
         for d in range(slots):
-            packed[d, 0:1, 0:share] = gg_ref[:, d * share : (d + 1) * share]
+            for n, rows_in in enumerate((gg_ref, gain1_ref, gain2_ref, gain3_ref)):
+                packed[d, n : n + 1, 0:share] = rows_in[:, d * share : (d + 1) * share]
+            packed[d, 4:5, 0 : 2 * head_width] = folded
         over = []
         for k, peer in enumerate(others):
             copy = remote(packed, boxes.at[k], zs.at[k], zr.at[k], peer)
@@ -1545,6 +1567,8 @@
         for copies in sent:
             wait_all(copies)
         mixer_turns = mixer_second(stages[2:], incomes[2:], [None, None], turns[2:], us, ur, where)
+        for copies in mixer_turns:
+            start_all(copies)
         travel.ready(stage0, stage1, in0, in1, turn0, turn1)
         second_half_items()
         for n in (3, 4, 5):
@@ -1572,23 +1596,6 @@
                 else:
                     target[half_rows(side), :] = value
         wait_all(outs)
-
-    folded = grad_qk[0:2, :head_width] + grad_qk[0:2, head_width : 2 * head_width]
-    gain_rows = jnp.concatenate(
-        [jnp.zeros_like(grad_gain_conv1), grad_gain_conv1, grad_gain_attn0, grad_gain_attn1], 0
-    )
-
-    def to_width(array):
-        return jnp.pad(array, [(0, 0)] * (array.ndim - 1) + [(0, small_width - array.shape[-1])])
-
-    small = jnp.concatenate(
-        [
-            to_width(gain_rows.reshape(4, slots, share).transpose(1, 0, 2)),
-            jnp.broadcast_to(to_width(folded.reshape(1, 1, 2 * head_width)), (slots, 1, small_width)),
-            jnp.zeros((slots, 3, small_width), FLOAT),
-        ],
-        1,
-    )
 
     (section_edges, sums, gout2, gmix, gout1, gin, gdown2, gup2, gdown1, gup1) = call(
         conv_backward,
@@ -1659,11 +1666,12 @@
         [
             gh1_low, (gh1, LAZY), projected, edge_gated, same, conv_kernel, conv_out, (w_in, LAZY), (x, LAZY), conv_gains,
             (yout, LAZY), (n1, LAZY), (mixed, LAZY), (stage0, LAZY), (stage1, LAZY), (in0, LAZY), (in1, LAZY), (turn0, LAZY), (turn1, LAZY),
-            (small, LAZY),
+            grad_gain_conv1, grad_gain_attn0, grad_gain_attn1, grad_qk,
         ]
         + [(array, ANY) for array in (partial1, partial2, first1, first2, first2_last, second2)],
         flops=5 * 10**9,
         moved=300 << 20,
+        begin=False,
     )
     def results(
         edges_in, sums_in, gout2_in, gmix_in, gout1_in, gin_in, gdown2_in, gup2_in, gdown1_in, gup1_in,

time: 375 us -> 368 us (0.981)
  Pallas kernels: 361 us -> 356 us
    pallas_call x6, Pallas kernels: 361 us -> 356 us  [call(): pl.pallas_call(whole, name=name, out_shape=[jax.ShapeDtypeStruct(out[0],...]
where the time goes in v7:
time: 368 us; the launch traced here: 362 us
  Pallas kernels  356 us (97%)
    pallas_call x6, Pallas kernels, call(): pl.pallas_call(whole, name=name, out_shape=[jax.ShapeDtypeStruct(out[0],...  356 us

profile of v7, /device:TPU:0, one launch (start us, length us, event | category | flops | bytes accessed | tf_op | source)
XLA Modules:
  0.0 361.8 jit_solution(11912454472755618831)
XLA Ops:
  0.7 0.8 dynamic-slice_convert_fusion
  1.4 0.1 convert_element_type.19
  1.5 1.2 multiply_sine_fusion
  2.7 2.1 copy.32
  4.9 117.9 %forward.1 = (bf16[256,1536]{1,0:T(8,128)(2,1)}, bf16[256,1536]{1,0:T(8,128)(2,1)}, bf16[256,1536]{1,0:T(8,128)(2,1)}, f32[3,256,384]{2,1,0:T(8,128)}, f32[4,8,3...) custom-call(bf16[1,4,128,1536]{3,2,1,0:T(8,128)(2,1)} %refs_0_.1, ...), custom_call_target="tpu_custom_call" | custom-call | flops 8999999488 | bytes 367001600 | tf_op jit(solution)/shard_map/forward/pallas_call | solution.py:328
  122.8 51.7 %second_ffn.1 = (bf16[256,1536]{1,0:T(8,128)(2,1)}, f32[128,1536]{1,0:T(8,128)}, bf16[256,1536]{1,0:T(8,128)(2,1)}, f32[1,1536]{1,0:T(1,128)}, bf16[3,4,192,1792...) custom-call(bf16[256,1536]{1,0:T(8,128)(2,1)} %get-tuple-element.83.refs_0_, ...), custom_call_target="tpu_custom_call" | custom-call | flops 12000000000 | bytes 157286400 | tf_op jit(solution)/shard_map/second_ffn/pallas_call | solution.py:328
  174.5 59.8 %attention_backward.1 = (bf16[256,1536]{1,0:T(8,128)(2,1)}, f32[1,1536]{1,0:T(1,128)}, f32[8,128]{1,0:T(8,128)}, bf16[64,1536]{1,0:T(8,128)(2,1)}, bf16[4,192,38...) custom-call(bf16[256,1536]{1,0:T(8,128)(2,1)} %get-tuple-element.86., ...), custom_call_target="tpu_custom_call" | custom-call | flops 6000000000 | bytes 136314880 | tf_op jit(solution)/shard_map/attention_backward/pallas_call | solution.py:328
  234.4 64.3 %first_ffn_back.1 = (f32[128,1536]{1,0:T(8,128)}, bf16[256,1536]{1,0:T(8,128)(2,1)}, f32[1,1536]{1,0:T(1,128)}, bf16[256,1536]{1,0:T(8,128)(2,1)}, bf16[2,96,384...) custom-call(bf16[256,1536]{1,0:T(8,128)(2,1)} %get-tuple-element.99., ...), custom_call_target="tpu_custom_call" | custom-call | flops 8999999488 | bytes 157286400 | tf_op jit(solution)/shard_map/first_ffn_back/pallas_call | solution.py:328
  298.6 53.9 %conv_backward.1 = (bf16[1,4,128,1536]{3,2,1,0:T(8,128)(2,1)}, f32[8,384]{1,0:T(8,128)}, bf16[192,384]{1,0:T(8,128)(2,1)}, bf16[192,640]{1,0:T(8,128)(2,1)}, bf1...) custom-call(bf16[256,1536]{1,0:T(8,128)(2,1)} %get-tuple-element.109, ...), custom_call_target="tpu_custom_call" | custom-call | flops 5000000000 | bytes 314572800 | tf_op jit(solution)/shard_map/conv_backward/pallas_call | solution.py:328
  352.6 8.7 %results.1 = (bf16[1,4,128,1536]{3,2,1,0:T(8,128)(2,1)}, f32[2,192]{1,0:T(2,128)}, f32[3,192,384]{2,1,0:T(8,128)}, f32[3,384]{1,0:T(4,128)}, f32[192,384]{1,0:T(...) custom-call(bf16[1,4,128,1536]{3,2,1,0:T(8,128)(2,1)} %get-tuple-ele, ...), custom_call_target="tpu_custom_call" | custom-call | bytes 26214400 | tf_op jit(solution)/shard_map/results/pallas_call | solution.py:328
  (1 shorter events, 0.0 us)

commit v8 on v7

--- a/solution.py
+++ b/solution.py
@@ -267,11 +267,13 @@
 
 class Moves:
     def __init__(self, incoming, leaving):
-        self.incoming, self.leaving, self.left = incoming, leaving, []
-
-    def begin(self):
-        for _, copy in self.incoming:
-            copy.start()
+        self.incoming, self.leaving, self.left, self.begun = incoming, leaving, [], []
+
+    def begin(self, *refs):
+        for known, copy in self.incoming:
+            if not any(known is ref for ref in self.begun) and (not refs or any(known is ref for ref in refs)):
+                copy.start()
+                self.begun.append(known)
 
     def ready(self, *refs):
         for ref in refs:
@@ -461,6 +463,7 @@
             segq_ref[span, :] = column
             for back in (1, 2):
                 same_ref[span, back - 1 : back] = jnp.where(column == own_column(seg_ref, m, back), 1.0, 0.0)
+        travel.ready(in_ref)
         met()
         give = pl.multiple_of((1 - s) * rows, rows)
         swap = remote(in_ref.at[0, :, pl.ds(give, rows)], other, swap_send.at[0], swap_recv.at[0], partner)
@@ -957,7 +960,7 @@
         ],
         conv_scratch + [dma(seqs - 1), dma(seqs - 1), dma(seqs), dma(seqs)] + total_scratch,
         [
-            incoming, conv_gains, (w_in, LAZY), conv_kernel, (conv_out, LAZY), attn_gains,
+            (incoming, LAZY), conv_gains, (w_in, LAZY), conv_kernel, (conv_out, LAZY), attn_gains,
             (first_up, ANY), (conv_down, ANY), segment_ids,
             (w_query, LAZY), (w_pair, LAZY), (cosine, LAZY), (sine, LAZY), qk_gains, (attn_out, LAZY),
         ],
@@ -987,6 +990,7 @@
         halves = half_swaps([g_ref, n4_ref], [given.at[0], given.at[1]], hs, hr, where)
         gg_ref[...] = jnp.zeros_like(gg_ref)
         swaps = []
+        travel.ready(n4_ref, g_ref)
         for j, (start, count) in enumerate(slabs):
             wait_all(weights[3 * j : 3 * j + 3])
             span = slice(start, start + count)
@@ -1069,7 +1073,7 @@
         ]
         + partial_outs(2),
         [pltpu.VMEM((tokens, width), FLOAT)] + ffn_scratch + part_scratch + total_scratch,
-        [n4, g, (h2, LAZY), attn_gains, (second_up, ANY), (attn_down, ANY)],
+        [(n4, LAZY), (g, LAZY), (h2, LAZY), attn_gains, (second_up, ANY), (attn_down, ANY)],
         flops=12 * 10**9,
         moved=150 << 20,
     )
@@ -1092,6 +1096,7 @@
         others = head_others(where)
         latters = [latter0, latter1]
         met = greet([partner] + peers + others, where, heads)
+        travel.ready(glow_ref, wo_ref, q_ref, all_ref)
         grads[...] = back_product(glow_ref[...], wo_ref[...]).astype(HALF)
         met()
         later = first_stage(
@@ -1257,7 +1262,7 @@
         + part_scratch
         + total_scratch,
         [
-            gh2_low, attn_out, queries, all_pairs, local_segments, segment_ids,
+            (gh2_low, LAZY), (attn_out, LAZY), (queries, LAZY), (all_pairs, LAZY), local_segments, segment_ids,
             (query_raw, LAZY), (pair_raw, LAZY), (cosine, LAZY), (sine, LAZY), qk_gains,
             (w_query, LAZY), (w_pair, LAZY), (middle, LAZY), (gh2, LAZY), attn_gains,
             (part_y, LAZY), (n3, LAZY), (attended, LAZY), (partial2, ANY), (first2, ANY),
@@ -1281,7 +1286,7 @@
         others = head_others(where)
         own_y = rows_of(h, small_rows)
         met = greet([(1 - s, q, h)] + seq_peers(where, seqs) + others, where, heads)
-        travel.ready(yown_ref, n2_ref, a1_ref)
+        travel.ready(gm_ref, yown_ref, n2_ref, a1_ref)
         yout_ref[own_y, :] = yown_ref[...]
         latter[0, 0:tokens, 0:hidden_units] = a1_ref[...]
         travel.ready(stage0, stage1, in0, in1)
@@ -1368,7 +1373,7 @@
         + [pltpu.VMEM((grid_rows, half_share, size), HALF) for size in widths[:2]]
         + [dma_grid(2, grid_rows), dma_grid(2, grid_rows)]
         + part_scratch + total_scratch,
-        [gm_low, (n2, LAZY), (f1, LAZY), (a1, LAZY), (h1, LAZY), conv_gains, (y_own, LAZY),
+        [(gm_low, LAZY), (n2, LAZY), (f1, LAZY), (a1, LAZY), (h1, LAZY), conv_gains, (y_own, LAZY),
          (stage0, LAZY), (stage1, LAZY), (in0, LAZY), (in1, LAZY), (first_up, ANY), (conv_down, ANY)],
         flops=9 * 10**9,
         moved=150 << 20,
@@ -1416,6 +1421,7 @@
             else:
                 copies += load_passing(partial, passing.at[n - 3], item_sems.at[n, pl.ds(3, grid_rows)], where)
             loads.append(copies)
+        travel.begin(low_ref, wout_ref, pc_ref)
         for copies in loads[3:]:
             start_all(copies)
         travel.begin()
@@ -1434,6 +1440,7 @@
             bulk.append(sends)
 
         gg_ref[...] = jnp.zeros_like(gg_ref)
+        travel.ready(low_ref, wout_ref, pc_ref)
         gated = pc_ref[0] * pc_ref[2]
         grad_y = back_product(low_ref[...], wout_ref[...])
         gz = grad_y * pc_ref[1]
@@ -1664,7 +1671,7 @@
         + part_scratch
         + total_scratch,
         [
-            gh1_low, (gh1, LAZY), projected, edge_gated, same, conv_kernel, conv_out, (w_in, LAZY), (x, LAZY), conv_gains,
+            (gh1_low, LAZY), (gh1, LAZY), (projected, LAZY), edge_gated, same, conv_kernel, (conv_out, LAZY), (w_in, LAZY), (x, LAZY), conv_gains,
             (yout, LAZY), (n1, LAZY), (mixed, LAZY), (stage0, LAZY), (stage1, LAZY), (in0, LAZY), (in1, LAZY), (turn0, LAZY), (turn1, LAZY),
             grad_gain_conv1, grad_gain_attn0, grad_gain_attn1, grad_qk,
         ]
@@ -1688,6 +1695,19 @@
             )
         ]
         start_all(loads)
+        cgain_out[...] = sums_in[0:2, 0:share]
+        again_out[...] = sums_in[2:4, 0:share]
+        taps_out[...] = sums_in[5:8, 0:channels]
+        travel.ready(gmix_in, gout1_in, gout2_in, gin_in)
+        for kind in range(2):
+            gqk_out[kind : kind + 1, :] = sums_in[4:5, kind * head_width : (kind + 1) * head_width]
+            start = query_width + kind * (pair_width // 2)
+            gkv_out[:, kind, :] = gmix_in[:, start : start + pair_width // 2].astype(FLOAT)
+        gq_out[...] = gmix_in[:, 0:query_width].astype(FLOAT)
+        gout1_out[...] = gout1_in[...].astype(FLOAT)
+        gout2_out[...] = gout2_in[...].astype(FLOAT)
+        gin_out[...] = gin_in[...].astype(FLOAT)
+        travel.leave(gq_out, gkv_out, gout1_out, gout2_out, gin_out)
         stores = []
         for k, (down_out, up_out) in enumerate(((gdown1_out, gup1_out), (gdown2_out, gup2_out))):
             loads[2 * k].wait()
@@ -1699,17 +1719,6 @@
                 up_stage[k, :, kind, :] = up_in[k, kind].astype(FLOAT)
             stores.append(pltpu.make_async_copy(up_stage.at[k], up_out, out_sems.at[2 * k + 1]))
             stores[-1].start()
-        cgain_out[...] = sums_in[0:2, 0:share]
-        again_out[...] = sums_in[2:4, 0:share]
-        taps_out[...] = sums_in[5:8, 0:channels]
-        for kind in range(2):
-            gqk_out[kind : kind + 1, :] = sums_in[4:5, kind * head_width : (kind + 1) * head_width]
-            start = query_width + kind * (pair_width // 2)
-            gkv_out[:, kind, :] = gmix_in[:, start : start + pair_width // 2].astype(FLOAT)
-        gq_out[...] = gmix_in[:, 0:query_width].astype(FLOAT)
-        gout1_out[...] = gout1_in[...].astype(FLOAT)
-        gout2_out[...] = gout2_in[...].astype(FLOAT)
-        gin_out[...] = gin_in[...].astype(FLOAT)
         edges_load.wait()
         stores.append(pltpu.make_async_copy(edges_held, edges_out, edge_sem.at[1]))
         stores[-1].start()
@@ -1724,16 +1733,16 @@
         [
             ((1, micro, local_rows, width), HALF, ANY),
             ((2, share), FLOAT),
-            ((3, share, channels), FLOAT),
+            ((3, share, channels), FLOAT, LATE),
             ((3, channels), FLOAT),
-            ((share, channels), FLOAT),
+            ((share, channels), FLOAT, LATE),
             ((share, 2, hidden_units), FLOAT, ANY),
             ((share, hidden_units), FLOAT, ANY),
             ((2, share), FLOAT),
-            ((share, query_width), FLOAT),
-            ((share, 2, pair_width // 2), FLOAT),
+            ((share, query_width), FLOAT, LATE),
+            ((share, 2, pair_width // 2), FLOAT, LATE),
             ((2, head_width), FLOAT),
-            ((share, query_width), FLOAT),
+            ((share, query_width), FLOAT, LATE),
             ((share, 2, hidden_units), FLOAT, ANY),
             ((share, hidden_units), FLOAT, ANY),
         ],
@@ -1747,7 +1756,7 @@
             dma(4),
             dma(2),
         ],
-        [(section_edges, ANY), sums, gout2, gmix, gout1, gin]
+        [(section_edges, ANY), sums, (gout2, LAZY), (gmix, LAZY), (gout1, LAZY), (gin, LAZY)]
         + [(array, ANY) for array in (gdown2, gup2, gdown1, gup1)],
         moved=25 << 20,
     )

time: 368 us -> 372 us (1.011)
  Pallas kernels: 356 us -> 360 us
    pallas_call x6, Pallas kernels: 356 us -> 360 us  [call(): pl.pallas_call(whole, name=name, out_shape=[jax.ShapeDtypeStruct(out[0],...]
where the time goes in v8:
time: 372 us; the launch traced here: 366 us
  Pallas kernels  360 us (97%)
    pallas_call x6, Pallas kernels, call(): pl.pallas_call(whole, name=name, out_shape=[jax.ShapeDtypeStruct(out[0],...  360 us

profile of v8, /device:TPU:0, one launch (start us, length us, event | category | flops | bytes accessed | tf_op | source)
XLA Modules:
  0.0 365.6 jit_solution(13263663257145266345)
XLA Ops:
  0.7 0.8 dynamic-slice_convert_fusion
  1.4 0.1 convert_element_type.19
  1.5 1.2 multiply_sine_fusion
  2.7 2.1 copy.32
  4.9 119.1 %forward.1 = (bf16[256,1536]{1,0:T(8,128)(2,1)}, bf16[256,1536]{1,0:T(8,128)(2,1)}, bf16[256,1536]{1,0:T(8,128)(2,1)}, f32[3,256,384]{2,1,0:T(8,128)}, f32[4,8,3...) custom-call(bf16[1,4,128,1536]{3,2,1,0:T(8,128)(2,1)} %refs_0_.1, ...), custom_call_target="tpu_custom_call" | custom-call | flops 8999999488 | bytes 367001600 | tf_op jit(solution)/shard_map/forward/pallas_call | solution.py:330
  123.9 54.3 %second_ffn.1 = (bf16[256,1536]{1,0:T(8,128)(2,1)}, f32[128,1536]{1,0:T(8,128)}, bf16[256,1536]{1,0:T(8,128)(2,1)}, f32[1,1536]{1,0:T(1,128)}, bf16[3,4,192,1792...) custom-call(bf16[256,1536]{1,0:T(8,128)(2,1)} %get-tuple-element.83.refs_0_, ...), custom_call_target="tpu_custom_call" | custom-call | flops 12000000000 | bytes 157286400 | tf_op jit(solution)/shard_map/second_ffn/pallas_call | solution.py:330
  178.2 60.4 %attention_backward.1 = (bf16[256,1536]{1,0:T(8,128)(2,1)}, f32[1,1536]{1,0:T(1,128)}, f32[8,128]{1,0:T(8,128)}, bf16[64,1536]{1,0:T(8,128)(2,1)}, bf16[4,192,38...) custom-call(bf16[256,1536]{1,0:T(8,128)(2,1)} %get-tuple-element.86., ...), custom_call_target="tpu_custom_call" | custom-call | flops 6000000000 | bytes 136314880 | tf_op jit(solution)/shard_map/attention_backward/pallas_call | solution.py:330
  238.7 63.4 %first_ffn_back.1 = (f32[128,1536]{1,0:T(8,128)}, bf16[256,1536]{1,0:T(8,128)(2,1)}, f32[1,1536]{1,0:T(1,128)}, bf16[256,1536]{1,0:T(8,128)(2,1)}, bf16[2,96,384...) custom-call(bf16[256,1536]{1,0:T(8,128)(2,1)} %get-tuple-element.99., ...), custom_call_target="tpu_custom_call" | custom-call | flops 8999999488 | bytes 157286400 | tf_op jit(solution)/shard_map/first_ffn_back/pallas_call | solution.py:330
  302.0 55.0 %conv_backward.1 = (bf16[1,4,128,1536]{3,2,1,0:T(8,128)(2,1)}, f32[8,384]{1,0:T(8,128)}, bf16[192,384]{1,0:T(8,128)(2,1)}, bf16[192,640]{1,0:T(8,128)(2,1)}, bf1...) custom-call(bf16[256,1536]{1,0:T(8,128)(2,1)} %get-tuple-element.109, ...), custom_call_target="tpu_custom_call" | custom-call | flops 5000000000 | bytes 314572800 | tf_op jit(solution)/shard_map/conv_backward/pallas_call | solution.py:330
  357.0 8.0 %results.1 = (bf16[1,4,128,1536]{3,2,1,0:T(8,128)(2,1)}, f32[2,192]{1,0:T(2,128)}, f32[3,192,384]{2,1,0:T(8,128)}, f32[3,384]{1,0:T(4,128)}, f32[192,384]{1,0:T(...) custom-call(bf16[1,4,128,1536]{3,2,1,0:T(8,128)(2,1)} %get-tuple-ele, ...), custom_call_target="tpu_custom_call" | custom-call | bytes 26214400 | tf_op jit(solution)/shard_map/results/pallas_call | solution.py:330
  (1 shorter events, 0.0 us)
